TPU v7x, 32 devices: a whole 2x2x4 slice. The times are simulated.
32 devices in a mesh: row: 8 (over y, x, core), col: 4 (over z).
Axes of the slice: x: 2, y: 2, z: 4, core: 2. Of those that a mesh axis runs over, the one named last changes fastest.
Arguments:
- integrals: float32 [262144, 1024], P(('row', 'col')), may hold values from -0.1875 to 0.1875
- amplitudes: float32 [64, 32768], P(None, ('row', 'col')), may hold values from -6 to 6
Outputs:
- ladder: float32 [16384, 32768], P('row', 'col')
All inputs are finite; a program needn't handle non-finite values.
Results may differ from a plain program's by a relative error of at most 0.00007.
Values sent between devices are 32-bit elements; how exact they have to be, the bound alone decides.
No kernel may reach another device: no remote copies, remote signals or barrier semaphores. Data moves between devices by JAX's collectives and lax.ppermute only.
A program may use at most 448 MiB of HBM per device.

v0:
```python
import jax
import jax.numpy as jnp
from jax import lax
from jax.sharding import PartitionSpec as P

NV = 512
NO = 64
NI = 32
NC = 2


def arrange(flat_amps):
    return flat_amps.reshape(NC, NI, NV, NO).transpose(0, 2, 1, 3).reshape(NC * NV, NI * NO)


def body(integrals, amplitudes):
    flat_amps = lax.all_gather(amplitudes, ("row", "col"), axis=1, tiled=True)
    panel_amps = arrange(flat_amps)
    col_count = lax.axis_size("col")
    local_avals = integrals.shape[0] // NV
    b_width = NV // col_count
    blocks = integrals.reshape(local_avals, col_count, b_width, NC * NV)
    piece = lax.all_to_all(blocks, "col", split_axis=1, concat_axis=0, tiled=True)
    leading = piece.shape[:3]
    result = jnp.dot(
        piece.reshape(-1, NC * NV),
        panel_amps,
        precision=lax.Precision.HIGHEST,
        preferred_element_type=jnp.float32,
    )
    moved = result.reshape(leading + (NI * NO,))
    group_avals = moved.shape[0]
    ladder = moved.reshape(group_avals, b_width, NI, NO).transpose(0, 2, 1, 3)
    return ladder.reshape(group_avals * NI, b_width * NO)


def solution(mesh):
    return jax.shard_map(
        body,
        mesh=mesh,
        in_specs=(P(("row", "col"), None), P(None, ("row", "col"))),
        out_specs=P("row", "col"),
        check_vma=False,
    )
```

profile of v0, /device:TPU:25, one launch (start us, length us, event | category | flops | bytes accessed | tf_op | source)
XLA Modules:
  0.0 1263.3 jit_solution(9209612362592736215)
XLA Ops:
  6.5 23.5 %copy.7 = f32[16,4,128,1024]{3,2,0,1:T(8,128)} copy(f32[16,4,128,1024]{3,2,1,0:T(8,128)} %bitcast.30) | data formatting | bytes 67108864 | tf_op jit(solution)/shard_map/reshape | solution.py:22
  30.1 9.7 all-to-all-start
  39.8 0.0 all-gather.2.cloned.1.call-start
  39.8 0.7 all-gather.2.cloned.1.call-update
  40.5 762.1 %all-gather.2.cloned.1.call-done = f32[64,32768]{1,0:T(8,128)} async-done(((f32[64,1024]{1,0:T(8,128)}), f32[64,32768]{1,0:T(8,128)}) %all-gather.2.cloned.1.call-update) | async-done | bytes 8388624 | tf_op jit(solution)/shard_map/all_gather | solution.py:17
  802.6 13.1 %reshape.18 = f32[2,32,512,64]{3,2,1,0:T(8,128)} reshape(f32[64,32768]{1,0:T(8,128)} %all-gather.2.cloned.1.call-done) | data formatting | bytes 16777216 | tf_op jit(solution)/shard_map/reshape | solution.py:13
  815.7 15.8 %copy.8 = f32[2,512,32,64]{1,0,3,2:T(2,128)} copy(f32[2,512,32,64]{3,1,2,0:T(8,128)} %bitcast.28) | data formatting | bytes 16777216 | tf_op jit(solution)/shard_map/transpose | solution.py:13
  831.5 8.7 copy.11
  840.2 0.0 all-to-all-done
  840.2 221.4 %convolution_bitcast_fusion = f32[64,32,128,64]{2,3,1,0:T(8,128)} fusion(f32[64,128,1024,1]{2,1,3,0:T(8,128)} %bitcast.5, f32[32,64,1024,1]{2,1,0,3:T(8,128)} %bitcast.31), kind=kOutput, calls=%fused_computation | convolution fusion | flops 206158430208 | bytes 109051904 | tf_op jit(solution)/shard_map/dot_general | solution.py:25
  1061.6 87.0 %copy.9 = f32[64,32,128,64]{3,2,1,0:T(8,128)} copy(f32[64,32,128,64]{2,3,1,0:T(8,128)} %convolution_bitcast_fusion) | data formatting | bytes 134217728 | tf_op jit(solution)/shard_map/transpose | solution.py:33
  1148.6 107.9 %reshape.20 = f32[2048,8192]{1,0:T(8,128)} reshape(f32[64,32,128,64]{3,2,1,0:T(8,128)} %copy.9) | data formatting | bytes 134217728 | tf_op jit(solution)/shard_map/reshape | solution.py:34
Async XLA Ops:
  30.1 810.1 %all-to-all-start = ((f32[16,4,128,1024]{3,2,0,1:T(8,128)}), f32[16,4,128,1024]{3,2,0,1:T(8,128)}, u32[]{:S(2)}, u32[]{:S(2)}) async-start(f32[16,4,128,1024]{3,2,0,1:T(8,128)} %copy.7), calls=%async_computation | async-start | bytes 67108864 | tf_op jit(solution)/shard_map/all_to_all | solution.py:23
  39.8 762.8 %all-gather.2.cloned.1.call-start = ((), (), s32[]{:S(2)}) async-start(), calls=%async_computation.1 | async-start | bytes 8650752 | tf_op jit(solution)/shard_map/all_gather | solution.py:17
Sparse Core Ops, SparseCore 0:
  43.6 758.9 all-gather.1
where the time goes:
time: 1270 us; the launch traced here: 1260 us
  waiting for transfers between devices  763 us (60%)
  local copies, waits for them, and re-layouts  256 us (20%)
  matrix products  221 us (17%)
  between operations  13.4 us (1%)
    all_gather x1, waiting for transfers between devices, body(): flat_amps = lax.all_gather(amplitudes, ('row', 'col'), axis=1, tiled=True)  762 us
    dot_general x1, matrix products, body(): jnp.dot(piece.reshape(-1, NC * NV), panel_amps, precision=lax.Precision.H...  221 us
    reshape x1, local copies, waits for them, and re-layouts, body(): return ladder.reshape(group_avals * NI, b_width * NO)  108 us
    transpose x1, local copies, waits for them, and re-layouts, body(): ladder = moved.reshape(group_avals, b_width, NI, NO).transpose(0, 2, 1, 3)  87 us
  transfers between devices with their start and end apart: 2, of which 1 were waited for; matrix products, arithmetic and copies ran while one was open for 3% of the time, Pallas kernels for 0%

commit v1 on v0

v1 whole, which is shorter than its diff:
```python
import functools

import jax
import jax.numpy as jnp
from jax import lax
from jax.experimental import pallas as pl
from jax.experimental.pallas import tpu as pltpu
from jax.sharding import PartitionSpec as P


NV = 512
NO = 64
NI = 32
NC = 2
LANES = 128
SUBLANES = 8


def split(values):
    high = values.astype(jnp.bfloat16)
    low = (values - high.astype(jnp.float32)).astype(jnp.bfloat16)
    return high, low


def ladder_kernel(group, at_ref, v_ref, th_ref, tl_ref, *refs):
    o_ref, part_ref = refs[-2:]
    b_width, depth = v_ref.shape[2:]
    half = b_width // 2
    rows = group * half
    vh, vl = split(v_ref[...].reshape(group * b_width, depth))
    width = SUBLANES * NO
    low_half = lax.broadcasted_iota(jnp.int32, (rows, LANES), 1) < NO

    @pl.loop(0, NI // SUBLANES)
    def _(n):
        columns = pl.ds(pl.multiple_of(n * width, width), width)
        th, tl = th_ref[:, columns], tl_ref[:, columns]
        dot = functools.partial(jnp.dot, preferred_element_type=jnp.float32)
        acc = dot(vh, tl) + dot(vl, th) + dot(vh, th)
        for pair in range(SUBLANES // 2):
            part_ref[pair] = acc[:, pair * LANES : (pair + 1) * LANES]
            even = part_ref[pair, pl.ds(0, rows, stride=2), :]
            odd = part_ref[pair, pl.ds(1, rows, stride=2), :]
            first = jnp.where(low_half, even, pltpu.roll(odd, NO, axis=1))
            second = jnp.where(low_half, pltpu.roll(even, NO, axis=1), odd)
            for a in range(group):
                base = (a * (NI // SUBLANES) + n) * half * SUBLANES + 2 * pair
                o_ref[pl.ds(base, half, stride=SUBLANES), :] = first[a * half : (a + 1) * half]
                o_ref[pl.ds(base + 1, half, stride=SUBLANES), :] = second[a * half : (a + 1) * half]


def multiply(at, integrals, th, tl, ladder, out_shape):
    avals, _, b_width, depth = integrals.shape
    group = 2 if avals % 2 == 0 else 1
    block_rows = group * NI * b_width * NO // LANES
    aliased = ladder is not None
    spec = pl.BlockSpec((depth, NI * NO), lambda g, at: (0, 0), pipeline_mode=pl.Buffered(1))
    products = avals * b_width * depth * NI * NO
    return pl.pallas_call(
        functools.partial(ladder_kernel, group),
        out_shape=out_shape,
        grid_spec=pltpu.PrefetchScalarGridSpec(
            num_scalar_prefetch=1,
            grid=(avals // group,),
            in_specs=[
                pl.BlockSpec((group, 1, b_width, depth), lambda g, at: (g, at[1], 0, 0)),
                spec,
                spec,
            ]
            + [pl.BlockSpec(memory_space=pl.ANY)] * aliased,
            out_specs=pl.BlockSpec((block_rows, LANES), lambda g, at: (at[0] // group + g, 0)),
            scratch_shapes=[pltpu.VMEM((SUBLANES // 2, group * b_width, LANES), jnp.float32)],
        ),
        input_output_aliases={4: 0} if aliased else {},
        compiler_params=pltpu.CompilerParams(vmem_limit_bytes=40 << 20),
        cost_estimate=pl.CostEstimate(
            flops=6 * products,
            bytes_accessed=4 * (integrals.size + avals * b_width * NI * NO + depth * NI * NO),
            transcendentals=0,
        ),
    )(at, integrals, th, tl, *([ladder] if aliased else []))


def gather_over(axis, pieces, masks):
    size = lax.axis_size(axis)
    here = lax.axis_index(axis)
    held = {0: pieces}
    for mask in masks:
        sent = sorted(held)
        block = jnp.concatenate([held[k] for k in sent]) if len(sent) > 1 else held[sent[0]]
        got = lax.ppermute(block, axis, [(k, k ^ mask) for k in range(size)])
        each = pieces.shape[0]
        for n, k in enumerate(sent):
            held[k ^ mask] = got[n * each : (n + 1) * each]
    stacked = jnp.stack([held[k] for k in range(size)])
    bit = 1
    while bit < size:
        view = stacked.reshape((size // (2 * bit), 2, bit) + pieces.shape)
        stacked = jnp.where((here & bit) != 0, view[:, ::-1], view).reshape((size,) + pieces.shape)
        bit *= 2
    return stacked.reshape((size * pieces.shape[0],) + pieces.shape[1:])


def gather_amplitudes(amplitudes):
    cols, rows = lax.axis_size("col"), lax.axis_size("row")
    bits = [1 << k for k in range((cols - 1).bit_length())]
    masks = ([cols - 1] + bits[:-1]) if cols > 1 else []
    pieces = gather_over("col", amplitudes[None], masks)
    pieces = gather_over("row", pieces, [1 << k for k in range((rows - 1).bit_length())])
    each = amplitudes.shape[1] // NO
    panel = pieces.reshape(-1, NC, NI, each, NO).transpose(1, 0, 3, 2, 4)
    return panel.reshape(NC * NV, NI * NO)


def chunks_of(avals):
    if avals < 16:
        return [1] * avals
    unit = avals // 8
    return [unit, 2 * unit, 2 * unit, 2 * unit, unit]


def body(integrals, amplitudes):
    cols = lax.axis_size("col")
    here = lax.axis_index("col")
    avals = integrals.shape[0] // NV
    b_width = NV // cols
    depth = integrals.shape[1]
    blocks = integrals.reshape(avals, cols, b_width, depth)

    shifts = [s for pair in zip(range(1, cols), range(cols - 1, 0, -1)) for s in pair]
    shifts = list(dict.fromkeys(shifts))
    arrived = []
    start = 0
    source = blocks
    for count in chunks_of(avals):
        pieces = [
            lax.dynamic_slice(source, (start, (here + shift) % cols, 0, 0), (count, 1, b_width, depth))
            for shift in shifts
        ]
        source, *pieces = lax.optimization_barrier((source, *pieces))
        for shift, piece in zip(shifts, pieces):
            got = lax.ppermute(piece, "col", [(k, (k + shift) % cols) for k in range(cols)])
            arrived.append(((here - shift) % cols * avals + start, got))
        start += count

    panel = gather_amplitudes(amplitudes)
    rounded = lax.reduce_precision(panel, 8, 7)
    th, tl = rounded.astype(jnp.bfloat16), (panel - rounded).astype(jnp.bfloat16)

    rows = cols * avals * NI
    tiles = rows * b_width * NO // LANES
    out_shape = jax.ShapeDtypeStruct((tiles, LANES), jnp.float32)
    ladder = multiply(jnp.stack([here * avals, here]), blocks, th, tl, None, out_shape)
    for at, got in arrived:
        ladder = multiply(jnp.stack([at, jnp.zeros_like(at)]), got, th, tl, ladder, out_shape)
    ladder = ladder.reshape(rows // SUBLANES, b_width * NO // LANES, SUBLANES, LANES)
    return ladder.transpose(0, 2, 1, 3).reshape(rows, b_width * NO)


def solution(mesh):
    return jax.shard_map(
        body,
        mesh=mesh,
        in_specs=(P(("row", "col"), None), P(None, ("row", "col"))),
        out_specs=P("row", "col"),
        check_vma=False,
    )
```

time: 1270 us -> 833 us (0.66)
  waiting for transfers between devices: 763 us -> 334 us
  matrix products: 221 us -> 0 us
  Pallas kernels: 0 us -> 200 us
  starting transfers between devices: 9.73 us -> 199 us
  local copies, waits for them, and re-layouts: 256 us -> 75.8 us
  other arithmetic: 0 us -> 19.3 us
  between operations: 13.4 us -> 0.19 us
    all_gather x1 -> x0, waiting for transfers between devices: 762 us -> none  [body(): flat_amps = lax.all_gather(amplitudes, ('row', 'col'), axis=1, tiled=True)]
    ppermute x0 -> x20, waiting for transfers between devices: none -> 334 us  [the longest x15 208 us: body(): lax.ppermute(piece, 'col', [(k, (k + shift) % cols) for k in range(cols)])]
    dot_general x1 -> x0, matrix products: 221 us -> none  [body(): jnp.dot(piece.reshape(-1, NC * NV), panel_amps, precision=lax.Precision.H...]
    pallas_call x0 -> x16, Pallas kernels: none -> 200 us  [multiply(): pl.pallas_call(functools.partial(ladder_kernel, group), out_shape=out_sha...]
    ppermute x0 -> x20, starting transfers between devices: none -> 199 us  [the longest x15 191 us: body(): lax.ppermute(piece, 'col', [(k, (k + shift) % cols) for k in range(cols)])]
    reshape x3 -> x1, local copies, waits for them, and re-layouts: 145 us -> 14.8 us  [gather_amplitudes(): return panel.reshape(NC * NV, NI * NO)]
    transpose x2 -> x1, local copies, waits for them, and re-layouts: 103 us -> 15.8 us  [gather_amplitudes(): panel = pieces.reshape(-1, NC, NI, each, NO).transpose(1, 0, 3, 2, 4)]
    dynamic_slice x0 -> x5, local copies, waits for them, and re-layouts: none -> 24.8 us  [body(): lax.dynamic_slice(source, (start, (here + shift) % cols, 0, 0), (count, 1...]
  transfers between devices with their start and end apart: 2 -> 20, of which waited for: 1 -> 9; matrix products, arithmetic and copies ran while one was open for 3% -> 11% of each run, Pallas kernels for 0% -> 23%
where the time goes in v1:
time: 833 us; the launch traced here: 829 us
  waiting for transfers between devices  334 us (40%)
  Pallas kernels  200 us (24%)
  starting transfers between devices  199 us (24%)
  local copies, waits for them, and re-layouts  75.8 us (9%)
  other arithmetic  19.3 us (2%)
    ppermute x15, waiting for transfers between devices, body(): lax.ppermute(piece, 'col', [(k, (k + shift) % cols) for k in range(cols)])  208 us
    pallas_call x16, Pallas kernels, multiply(): pl.pallas_call(functools.partial(ladder_kernel, group), out_shape=out_sha...  200 us
    ppermute x15, starting transfers between devices, body(): lax.ppermute(piece, 'col', [(k, (k + shift) % cols) for k in range(cols)])  191 us
    ppermute x5, waiting for transfers between devices, gather_over(): got = lax.ppermute(block, axis, [(k, k ^ mask) for k in range(size)])  126 us
    dynamic_slice x5, local copies, waits for them, and re-layouts, body(): lax.dynamic_slice(source, (start, (here + shift) % cols, 0, 0), (count, 1...  24.8 us
  transfers between devices with their start and end apart: 20, of which 9 were waited for; matrix products, arithmetic and copies ran while one was open for 11% of the time, Pallas kernels for 23%

profile of v1, /device:TPU:25, one launch (start us, length us, event | category | flops | bytes accessed | tf_op | source)
XLA Modules:
  0.0 829.3 jit_solution(7267679506853182692)
XLA Ops:
  0.0 9.3 %collective-permute-done.1 = f32[1,64,1024]{2,1,0:T(8,128)S(1)} collective-permute-done((f32[1,64,1024]{2,1,0:T(8,128)}, f32[1,64,1024]{2,1,0:T(8,128)S(1)}, u32[]{:S(2)}, u32[]{:S(2)}) %collective-permute-start.1) | collective-permute-done | bytes 262176 | tf_op jit(solution)/shard_map/ppermute | solution.py:91
  10.3 4.0 collective-permute-start.2
  14.3 10.8 %collective-permute-done.2 = f32[2,64,1024]{2,1,0:T(8,128)S(1)} collective-permute-done((f32[2,64,1024]{2,1,0:T(8,128)S(1)}, f32[2,64,1024]{2,1,0:T(8,128)S(1)}, u32[]{:S(2)}, u32[]{:S(2)}) %collective-permute-start.2) | collective-permute-done | bytes 524320 | tf_op jit(solution)/shard_map/ppermute | solution.py:91
  26.4 2.2 collective-permute-start.3
  28.5 2.3 collective-permute-done.3
  32.2 45.6 %collective-permute-done.4 = f32[8,64,1024]{2,1,0:T(8,128)S(1)} collective-permute-done((f32[8,64,1024]{2,1,0:T(8,128)S(1)}, f32[8,64,1024]{2,1,0:T(8,128)S(1)}, u32[]{:S(2)}, u32[]{:S(2)}) %collective-permute-start.4) | collective-permute-done | bytes 2097184 | tf_op jit(solution)/shard_map/ppermute | solution.py:91
  79.2 2.4 pad_maximum_fusion
  82.8 3.7 constant_dynamic-slice_fusion.12
  89.5 5.7 constant_dynamic-slice_fusion.9
  95.2 2.0 collective-permute-start.16
  97.2 5.8 constant_dynamic-slice_fusion.6
  103.1 5.8 constant_dynamic-slice_fusion.3
  108.8 3.8 constant_dynamic-slice_fusion
  114.3 58.5 %collective-permute-done.5 = f32[16,64,1024]{2,1,0:T(8,128)} collective-permute-done((f32[16,64,1024]{2,1,0:T(8,128)}, f32[16,64,1024]{2,1,0:T(8,128)}, u32[]{:S(2)}, u32[]{:S(2)}) %collective-permute-start.5) | collective-permute-done | bytes 4194336 | tf_op jit(solution)/shard_map/ppermute | solution.py:91
  179.5 1.9 reverse_select_fusion.2
  181.4 1.9 reverse_select_fusion.1
  183.3 4.3 reverse_select_fusion
  187.6 13.3 %reshape_reshape_reshape.3 = f32[32,2,32,16,64]{4,3,2,1,0:T(8,128)} reshape(f32[1,2,4,4,64,1024]{5,4,3,2,1,0:T(8,128)} %reverse_select_fusion) | data formatting | bytes 16777216 | tf_op jit(solution)/shard_map/reshape;reshape;reshape | solution.py:111
  200.9 15.8 %copy.18 = f32[2,32,16,32,64]{4,3,2,1,0:T(8,128)} copy(f32[2,32,16,32,64]{4,2,3,0,1:T(8,128)} %bitcast.75) | data formatting | bytes 16777216 | tf_op jit(solution)/shard_map/transpose | solution.py:111
  216.8 14.8 %reshape.21 = f32[1024,2048]{1,0:T(8,128)} reshape(f32[2,32,16,32,64]{4,3,2,1,0:T(8,128)} %copy.18) | data formatting | bytes 16777216 | tf_op jit(solution)/shard_map/reshape | solution.py:112
  231.6 5.2 fusion
  236.8 41.5 %shard_map.28.refs_0_ = f32[131072,128]{1,0:T(8,128)} custom-call(s32[2]{0:T(128)S(1)} %pad_add_fusion.15.at_ref, f32[16,4,128,1024]{3,2,1,0:T(8,128)} %bitcast.74, bf16[1024,2048]{1,0:T(8,128)(2,1)S(1)} %get-tuple-element.59.th_ref, bf16[1024,2048]{1,0:T(8,128)(2,1)S(1)} %get-tuple-element.58.tl_ref), custom_call_target="tpu_custom_call" | custom-call | flops 25769803776 | bytes 58720256 | tf_op jit(solution)/shard_map/pallas_call | solution.py:59
  278.4 6.6 shard_map.29.refs_0_
  285.1 2.4 collective-permute-start.13
  287.4 6.6 shard_map.30.refs_0_
  294.1 7.9 shard_map.31.refs_0_
  303.3 12.7 %shard_map.32.refs_0_ = f32[131072,128]{1,0:T(8,128)} custom-call(s32[2]{0:T(128)S(1)} %pad_add_fusion.3.at_ref, f32[4,1,128,1024]{3,2,1,0:T(8,128)} %collective-permute-done.16.v_ref, bf16[1024,2048]{1,0:T(8,128)(2,1)S(1)} %get-tuple-element.59.th_ref, bf16[1024,2048]{1,0:T(8,128)(2,1)S(1)} %get-tuple-element.58.tl_ref, ...), custom_call_target="tpu_custom_call", output_to_operand_aliasing={{}: (4, {})} | custom-call | flops 6442450944 | bytes 14680064 | tf_op jit(solution)/shard_map/pallas_call | solution.py:59
  316.0 1.9 collective-permute-start.10
  317.9 12.7 %shard_map.33.refs_0_ = f32[131072,128]{1,0:T(8,128)} custom-call(s32[2]{0:T(128)S(1)} %pad_add_fusion.4.at_ref, f32[4,1,128,1024]{3,2,1,0:T(8,128)} %collective-permute-done.15.v_ref, bf16[1024,2048]{1,0:T(8,128)(2,1)S(1)} %get-tuple-element.59.th_ref, bf16[1024,2048]{1,0:T(8,128)(2,1)S(1)} %get-tuple-element.58.tl_ref, ...), custom_call_target="tpu_custom_call", output_to_operand_aliasing={{}: (4, {})} | custom-call | flops 6442450944 | bytes 14680064 | tf_op jit(solution)/shard_map/pallas_call | solution.py:59
  330.6 44.0 %collective-permute-done.14.v_ref = f32[4,1,128,1024]{3,2,1,0:T(8,128)} collective-permute-done((f32[4,1,128,1024]{3,2,1,0:T(8,128)}, f32[4,1,128,1024]{3,2,1,0:T(8,128)}, u32[]{:S(2)}, u32[]{:S(2)}) %collective-permute-start.14) | collective-permute-done | bytes 2097184 | tf_op jit(solution)/shard_map/ppermute | solution.py:142
  374.6 42.8 %collective-permute-start.9 = (f32[4,1,128,1024]{3,2,1,0:T(8,128)}, f32[4,1,128,1024]{3,2,1,0:T(8,128)}, u32[]{:S(2)}, u32[]{:S(2)}) collective-permute-start(f32[4,1,128,1024]{3,2,1,0:T(8,128)} %get-tuple-element.32), channel_id=1, source_target_pairs={{0,3},{1,0},{2,1},{3,2},{4,7},{5,4},{6,5},{7,6},{8,11},{9,8},{10,9... | collective-permute-start | bytes 6291464 | tf_op jit(solution)/shard_map/ppermute | solution.py:142
  417.3 12.7 %shard_map.34.refs_0_ = f32[131072,128]{1,0:T(8,128)} custom-call(s32[2]{0:T(128)S(1)} %pad_add_fusion.5.at_ref, f32[4,1,128,1024]{3,2,1,0:T(8,128)} %collective-permute-done.14.v_ref, bf16[1024,2048]{1,0:T(8,128)(2,1)S(1)} %get-tuple-element.59.th_ref, bf16[1024,2048]{1,0:T(8,128)(2,1)S(1)} %get-tuple-element.58.tl_ref, ...), custom_call_target="tpu_custom_call", output_to_operand_aliasing={{}: (4, {})} | custom-call | flops 6442450944 | bytes 14680064 | tf_op jit(solution)/shard_map/pallas_call | solution.py:59
  430.0 78.1 %collective-permute-start.8 = (f32[4,1,128,1024]{3,2,1,0:T(8,128)}, f32[4,1,128,1024]{3,2,1,0:T(8,128)}, u32[]{:S(2)}, u32[]{:S(2)}) collective-permute-start(f32[4,1,128,1024]{3,2,1,0:T(8,128)} %get-tuple-element.31), channel_id=1, source_target_pairs={{0,2},{1,3},{2,0},{3,1},{4,6},{5,7},{6,4},{7,5},{8,10},{9,11},{10,... | collective-permute-start | bytes 6291464 | tf_op jit(solution)/shard_map/ppermute | solution.py:142
  508.1 12.7 %shard_map.35.refs_0_ = f32[131072,128]{1,0:T(8,128)} custom-call(s32[2]{0:T(128)S(1)} %pad_add_fusion.6.at_ref, f32[4,1,128,1024]{3,2,1,0:T(8,128)} %collective-permute-done.13.v_ref, bf16[1024,2048]{1,0:T(8,128)(2,1)S(1)} %get-tuple-element.59.th_ref, bf16[1024,2048]{1,0:T(8,128)(2,1)S(1)} %get-tuple-element.58.tl_ref, ...), custom_call_target="tpu_custom_call", output_to_operand_aliasing={{}: (4, {})} | custom-call | flops 6442450944 | bytes 14680064 | tf_op jit(solution)/shard_map/pallas_call | solution.py:59
  520.8 3.6 collective-permute-start.7
  524.4 12.7 %shard_map.36.refs_0_ = f32[131072,128]{1,0:T(8,128)} custom-call(s32[2]{0:T(128)S(1)} %pad_add_fusion.7.at_ref, f32[4,1,128,1024]{3,2,1,0:T(8,128)} %collective-permute-done.12.v_ref, bf16[1024,2048]{1,0:T(8,128)(2,1)S(1)} %get-tuple-element.59.th_ref, bf16[1024,2048]{1,0:T(8,128)(2,1)S(1)} %get-tuple-element.58.tl_ref, ...), custom_call_target="tpu_custom_call", output_to_operand_aliasing={{}: (4, {})} | custom-call | flops 6442450944 | bytes 14680064 | tf_op jit(solution)/shard_map/pallas_call | solution.py:59
  537.1 104.6 %collective-permute-done.11.v_ref = f32[4,1,128,1024]{3,2,1,0:T(8,128)} collective-permute-done((f32[4,1,128,1024]{3,2,1,0:T(8,128)}, f32[4,1,128,1024]{3,2,1,0:T(8,128)}, u32[]{:S(2)}, u32[]{:S(2)}) %collective-permute-start.11) | collective-permute-done | bytes 2097184 | tf_op jit(solution)/shard_map/ppermute | solution.py:142
  641.7 20.7 %collective-permute-start.6 = (f32[2,1,128,1024]{3,2,1,0:T(8,128)}, f32[2,1,128,1024]{3,2,1,0:T(8,128)}, u32[]{:S(2)}, u32[]{:S(2)}) collective-permute-start(f32[2,1,128,1024]{3,2,1,0:T(8,128)} %get-tuple-element.29), channel_id=1, source_target_pairs={{0,3},{1,0},{2,1},{3,2},{4,7},{5,4},{6,5},{7,6},{8,11},{9,8},{10,9... | collective-permute-start | bytes 3145736 | tf_op jit(solution)/shard_map/ppermute | solution.py:142
  662.4 12.7 %shard_map.37.refs_0_ = f32[131072,128]{1,0:T(8,128)} custom-call(s32[2]{0:T(128)S(1)} %pad_add_fusion.8.at_ref, f32[4,1,128,1024]{3,2,1,0:T(8,128)} %collective-permute-done.11.v_ref, bf16[1024,2048]{1,0:T(8,128)(2,1)S(1)} %get-tuple-element.59.th_ref, bf16[1024,2048]{1,0:T(8,128)(2,1)S(1)} %get-tuple-element.58.tl_ref, ...), custom_call_target="tpu_custom_call", output_to_operand_aliasing={{}: (4, {})} | custom-call | flops 6442450944 | bytes 14680064 | tf_op jit(solution)/shard_map/pallas_call | solution.py:59
  675.1 33.3 %collective-permute-start = (f32[2,1,128,1024]{3,2,1,0:T(8,128)}, f32[2,1,128,1024]{3,2,1,0:T(8,128)}, u32[]{:S(2)}, u32[]{:S(2)}) collective-permute-start(f32[2,1,128,1024]{3,2,1,0:T(8,128)} %get-tuple-element.28), channel_id=1, source_target_pairs={{0,2},{1,3},{2,0},{3,1},{4,6},{5,7},{6,4},{7,5},{8,10},{9,11},{10,... | collective-permute-start | bytes 3145736 | tf_op jit(solution)/shard_map/ppermute | solution.py:142
  708.4 12.7 %shard_map.38.refs_0_ = f32[131072,128]{1,0:T(8,128)} custom-call(s32[2]{0:T(128)S(1)} %pad_add_fusion.9.at_ref, f32[4,1,128,1024]{3,2,1,0:T(8,128)} %collective-permute-done.10.v_ref, bf16[1024,2048]{1,0:T(8,128)(2,1)S(1)} %get-tuple-element.59.th_ref, bf16[1024,2048]{1,0:T(8,128)(2,1)S(1)} %get-tuple-element.58.tl_ref, ...), custom_call_target="tpu_custom_call", output_to_operand_aliasing={{}: (4, {})} | custom-call | flops 6442450944 | bytes 14680064 | tf_op jit(solution)/shard_map/pallas_call | solution.py:59
  721.0 12.7 %shard_map.39.refs_0_ = f32[131072,128]{1,0:T(8,128)} custom-call(s32[2]{0:T(128)S(1)} %pad_add_fusion.10.at_ref, f32[4,1,128,1024]{3,2,1,0:T(8,128)} %collective-permute-done.9.v_ref, bf16[1024,2048]{1,0:T(8,128)(2,1)S(1)} %get-tuple-element.59.th_ref, bf16[1024,2048]{1,0:T(8,128)(2,1)S(1)} %get-tuple-element.58.tl_ref, ...), custom_call_target="tpu_custom_call", output_to_operand_aliasing={{}: (4, {})} | custom-call | flops 6442450944 | bytes 14680064 | tf_op jit(solution)/shard_map/pallas_call | solution.py:59
  733.7 42.8 %collective-permute-done.8.v_ref = f32[4,1,128,1024]{3,2,1,0:T(8,128)} collective-permute-done((f32[4,1,128,1024]{3,2,1,0:T(8,128)}, f32[4,1,128,1024]{3,2,1,0:T(8,128)}, u32[]{:S(2)}, u32[]{:S(2)}) %collective-permute-start.8) | collective-permute-done | bytes 2097184 | tf_op jit(solution)/shard_map/ppermute | solution.py:142
  776.5 12.7 %shard_map.40.refs_0_ = f32[131072,128]{1,0:T(8,128)} custom-call(s32[2]{0:T(128)S(1)} %pad_add_fusion.11.at_ref, f32[4,1,128,1024]{3,2,1,0:T(8,128)} %collective-permute-done.8.v_ref, bf16[1024,2048]{1,0:T(8,128)(2,1)S(1)} %get-tuple-element.59.th_ref, bf16[1024,2048]{1,0:T(8,128)(2,1)S(1)} %get-tuple-element.58.tl_ref, ...), custom_call_target="tpu_custom_call", output_to_operand_aliasing={{}: (4, {})} | custom-call | flops 6442450944 | bytes 14680064 | tf_op jit(solution)/shard_map/pallas_call | solution.py:59
  789.2 7.9 shard_map.41.refs_0_
  797.1 7.9 shard_map.42.refs_0_
  804.9 16.5 %collective-permute-done.v_ref = f32[2,1,128,1024]{3,2,1,0:T(8,128)} collective-permute-done((f32[2,1,128,1024]{3,2,1,0:T(8,128)}, f32[2,1,128,1024]{3,2,1,0:T(8,128)}, u32[]{:S(2)}, u32[]{:S(2)}) %collective-permute-start) | collective-permute-done | bytes 1048608 | tf_op jit(solution)/shard_map/ppermute | solution.py:142
  821.4 7.9 shard_map.43
  (59 shorter events, 19.1 us)
Async XLA Ops:
  0.0 9.3 %collective-permute-start.1 = (f32[1,64,1024]{2,1,0:T(8,128)}, f32[1,64,1024]{2,1,0:T(8,128)S(1)}, u32[]{:S(2)}, u32[]{:S(2)}) collective-permute-start(f32[1,64,1024]{2,1,0:T(8,128)} %bitcast.84), channel_id=1, source_target_pairs={{0,3},{1,2},{2,1},{3,0},{4,7},{5,6},{6,5},{7,4},{8,11},{9,10},{10,... | collective-permute-start | bytes 786440 | tf_op jit(solution)/shard_map/ppermute | solution.py:91
  10.3 14.7 %collective-permute-start.2 = (f32[2,64,1024]{2,1,0:T(8,128)S(1)}, f32[2,64,1024]{2,1,0:T(8,128)S(1)}, u32[]{:S(2)}, u32[]{:S(2)}) collective-permute-start(f32[2,64,1024]{2,1,0:T(8,128)S(1)} %pad_maximum_fusion.3), channel_id=1, source_target_pairs={{0,1},{1,0},{2,3},{3,2},{4,5},{5,4},{6,7},{7,6},{8,9},{9,8},{10,11... | collective-permute-start | bytes 1572872 | tf_op jit(solution)/shard_map/ppermute | solution.py:91
  26.4 4.5 collective-permute-start.3
  30.8 55.7 %copy-start = (f32[4,64,1024]{2,1,0:T(8,128)}, f32[4,64,1024]{2,1,0:T(8,128)S(1)}, u32[]{:S(2)}) copy-start(f32[4,64,1024]{2,1,0:T(8,128)S(1)} %collective-permute-done.3) | copy-start | bytes 3145732
  31.0 46.9 %collective-permute-start.4 = (f32[8,64,1024]{2,1,0:T(8,128)S(1)}, f32[8,64,1024]{2,1,0:T(8,128)S(1)}, u32[]{:S(2)}, u32[]{:S(2)}) collective-permute-start(f32[8,64,1024]{2,1,0:T(8,128)S(1)} %pad_maximum_fusion.1), channel_id=1, source_target_pairs={{0,8},{4,12},{8,0},{12,4},{16,24},{20,28},{24,16},{28,20},{1,9},{5... | collective-permute-start | bytes 6291464 | tf_op jit(solution)/shard_map/ppermute | solution.py:91
  77.8 1.4 copy-start.2
  81.6 91.2 %collective-permute-start.5 = (f32[16,64,1024]{2,1,0:T(8,128)}, f32[16,64,1024]{2,1,0:T(8,128)}, u32[]{:S(2)}, u32[]{:S(2)}) collective-permute-start(f32[16,64,1024]{2,1,0:T(8,128)} %pad_maximum_fusion), channel_id=1, source_target_pairs={{0,16},{4,20},{8,24},{12,28},{16,0},{20,4},{24,8},{28,12},{1,17},{... | collective-permute-start | bytes 12582920 | tf_op jit(solution)/shard_map/ppermute | solution.py:91
  86.5 191.8 %collective-permute-start.19 = (f32[2,1,128,1024]{3,2,1,0:T(8,128)}, f32[2,1,128,1024]{3,2,1,0:T(8,128)S(1)}, u32[]{:S(2)}, u32[]{:S(2)}) collective-permute-start(f32[2,1,128,1024]{3,2,1,0:T(8,128)} %get-tuple-element.42), channel_id=1, source_target_pairs={{0,1},{1,2},{2,3},{3,0},{4,5},{5,6},{6,7},{7,4},{8,9},{9,10},{10,1... | collective-permute-start | bytes 3145736 | tf_op jit(solution)/shard_map/ppermute | solution.py:142
  87.8 197.3 %collective-permute-start.18 = (f32[2,1,128,1024]{3,2,1,0:T(8,128)}, f32[2,1,128,1024]{3,2,1,0:T(8,128)S(1)}, u32[]{:S(2)}, u32[]{:S(2)}) collective-permute-start(f32[2,1,128,1024]{3,2,1,0:T(8,128)} %get-tuple-element.41), channel_id=1, source_target_pairs={{0,3},{1,0},{2,1},{3,2},{4,7},{5,4},{6,5},{7,6},{8,11},{9,8},{10,9... | collective-permute-start | bytes 3145736 | tf_op jit(solution)/shard_map/ppermute | solution.py:142
  88.0 206.1 %collective-permute-start.17 = (f32[2,1,128,1024]{3,2,1,0:T(8,128)}, f32[2,1,128,1024]{3,2,1,0:T(8,128)}, u32[]{:S(2)}, u32[]{:S(2)}) collective-permute-start(f32[2,1,128,1024]{3,2,1,0:T(8,128)} %get-tuple-element.40), channel_id=1, source_target_pairs={{0,2},{1,3},{2,0},{3,1},{4,6},{5,7},{6,4},{7,5},{8,10},{9,11},{10,... | collective-permute-start | bytes 3145736 | tf_op jit(solution)/shard_map/ppermute | solution.py:142
  95.2 206.7 %collective-permute-start.16 = (f32[4,1,128,1024]{3,2,1,0:T(8,128)}, f32[4,1,128,1024]{3,2,1,0:T(8,128)}, u32[]{:S(2)}, u32[]{:S(2)}) collective-permute-start(f32[4,1,128,1024]{3,2,1,0:T(8,128)} %get-tuple-element.39), channel_id=1, source_target_pairs={{0,1},{1,2},{2,3},{3,0},{4,5},{5,6},{6,7},{7,4},{8,9},{9,10},{10,1... | collective-permute-start | bytes 6291464 | tf_op jit(solution)/shard_map/ppermute | solution.py:142
  103.1 10.9 %copy-start.1 = (f32[4,64,1024]{2,1,0:T(8,128)S(1)}, f32[4,64,1024]{2,1,0:T(8,128)}, u32[]{:S(2)}) copy-start(f32[4,64,1024]{2,1,0:T(8,128)} %copy-done) | copy-start | bytes 3145732
  108.8 5.2 copy-start.3
  172.8 143.2 %collective-permute-start.15 = (f32[4,1,128,1024]{3,2,1,0:T(8,128)}, f32[4,1,128,1024]{3,2,1,0:T(8,128)}, u32[]{:S(2)}, u32[]{:S(2)}) collective-permute-start(f32[4,1,128,1024]{3,2,1,0:T(8,128)} %get-tuple-element.38), channel_id=1, source_target_pairs={{0,3},{1,0},{2,1},{3,2},{4,7},{5,4},{6,5},{7,6},{8,11},{9,8},{10,9... | collective-permute-start | bytes 6291464 | tf_op jit(solution)/shard_map/ppermute | solution.py:142
  278.3 96.2 %collective-permute-start.14 = (f32[4,1,128,1024]{3,2,1,0:T(8,128)}, f32[4,1,128,1024]{3,2,1,0:T(8,128)}, u32[]{:S(2)}, u32[]{:S(2)}) collective-permute-start(f32[4,1,128,1024]{3,2,1,0:T(8,128)} %get-tuple-element.37), channel_id=1, source_target_pairs={{0,2},{1,3},{2,0},{3,1},{4,6},{5,7},{6,4},{7,5},{8,10},{9,11},{10,... | collective-permute-start | bytes 6291464 | tf_op jit(solution)/shard_map/ppermute | solution.py:142
  285.1 145.0 %collective-permute-start.13 = (f32[4,1,128,1024]{3,2,1,0:T(8,128)}, f32[4,1,128,1024]{3,2,1,0:T(8,128)}, u32[]{:S(2)}, u32[]{:S(2)}) collective-permute-start(f32[4,1,128,1024]{3,2,1,0:T(8,128)} %get-tuple-element.36), channel_id=1, source_target_pairs={{0,1},{1,2},{2,3},{3,0},{4,5},{5,6},{6,7},{7,4},{8,9},{9,10},{10,1... | collective-permute-start | bytes 6291464 | tf_op jit(solution)/shard_map/ppermute | solution.py:142
  294.0 226.7 %collective-permute-start.12 = (f32[4,1,128,1024]{3,2,1,0:T(8,128)}, f32[4,1,128,1024]{3,2,1,0:T(8,128)}, u32[]{:S(2)}, u32[]{:S(2)}) collective-permute-start(f32[4,1,128,1024]{3,2,1,0:T(8,128)} %get-tuple-element.35), channel_id=1, source_target_pairs={{0,3},{1,0},{2,1},{3,2},{4,7},{5,4},{6,5},{7,6},{8,11},{9,8},{10,9... | collective-permute-start | bytes 6291464 | tf_op jit(solution)/shard_map/ppermute | solution.py:142
  301.9 339.7 %collective-permute-start.11 = (f32[4,1,128,1024]{3,2,1,0:T(8,128)}, f32[4,1,128,1024]{3,2,1,0:T(8,128)}, u32[]{:S(2)}, u32[]{:S(2)}) collective-permute-start(f32[4,1,128,1024]{3,2,1,0:T(8,128)} %get-tuple-element.34), channel_id=1, source_target_pairs={{0,2},{1,3},{2,0},{3,1},{4,6},{5,7},{6,4},{7,5},{8,10},{9,11},{10,... | collective-permute-start | bytes 6291464 | tf_op jit(solution)/shard_map/ppermute | solution.py:142
  316.0 359.0 %collective-permute-start.10 = (f32[4,1,128,1024]{3,2,1,0:T(8,128)}, f32[4,1,128,1024]{3,2,1,0:T(8,128)}, u32[]{:S(2)}, u32[]{:S(2)}) collective-permute-start(f32[4,1,128,1024]{3,2,1,0:T(8,128)} %get-tuple-element.33), channel_id=1, source_target_pairs={{0,1},{1,2},{2,3},{3,0},{4,5},{5,6},{6,7},{7,4},{8,9},{9,10},{10,1... | collective-permute-start | bytes 6291464 | tf_op jit(solution)/shard_map/ppermute | solution.py:142
  374.6 346.5 %collective-permute-start.9 = (f32[4,1,128,1024]{3,2,1,0:T(8,128)}, f32[4,1,128,1024]{3,2,1,0:T(8,128)}, u32[]{:S(2)}, u32[]{:S(2)}) collective-permute-start(f32[4,1,128,1024]{3,2,1,0:T(8,128)} %get-tuple-element.32), channel_id=1, source_target_pairs={{0,3},{1,0},{2,1},{3,2},{4,7},{5,4},{6,5},{7,6},{8,11},{9,8},{10,9... | collective-permute-start | bytes 6291464 | tf_op jit(solution)/shard_map/ppermute | solution.py:142
  430.0 346.5 %collective-permute-start.8 = (f32[4,1,128,1024]{3,2,1,0:T(8,128)}, f32[4,1,128,1024]{3,2,1,0:T(8,128)}, u32[]{:S(2)}, u32[]{:S(2)}) collective-permute-start(f32[4,1,128,1024]{3,2,1,0:T(8,128)} %get-tuple-element.31), channel_id=1, source_target_pairs={{0,2},{1,3},{2,0},{3,1},{4,6},{5,7},{6,4},{7,5},{8,10},{9,11},{10,... | collective-permute-start | bytes 6291464 | tf_op jit(solution)/shard_map/ppermute | solution.py:142
  520.8 268.4 %collective-permute-start.7 = (f32[2,1,128,1024]{3,2,1,0:T(8,128)}, f32[2,1,128,1024]{3,2,1,0:T(8,128)}, u32[]{:S(2)}, u32[]{:S(2)}) collective-permute-start(f32[2,1,128,1024]{3,2,1,0:T(8,128)} %get-tuple-element.30), channel_id=1, source_target_pairs={{0,1},{1,2},{2,3},{3,0},{4,5},{5,6},{6,7},{7,4},{8,9},{9,10},{10,1... | collective-permute-start | bytes 3145736 | tf_op jit(solution)/shard_map/ppermute | solution.py:142
  641.7 155.4 %collective-permute-start.6 = (f32[2,1,128,1024]{3,2,1,0:T(8,128)}, f32[2,1,128,1024]{3,2,1,0:T(8,128)}, u32[]{:S(2)}, u32[]{:S(2)}) collective-permute-start(f32[2,1,128,1024]{3,2,1,0:T(8,128)} %get-tuple-element.29), channel_id=1, source_target_pairs={{0,3},{1,0},{2,1},{3,2},{4,7},{5,4},{6,5},{7,6},{8,11},{9,8},{10,9... | collective-permute-start | bytes 3145736 | tf_op jit(solution)/shard_map/ppermute | solution.py:142
  675.1 146.4 %collective-permute-start = (f32[2,1,128,1024]{3,2,1,0:T(8,128)}, f32[2,1,128,1024]{3,2,1,0:T(8,128)}, u32[]{:S(2)}, u32[]{:S(2)}) collective-permute-start(f32[2,1,128,1024]{3,2,1,0:T(8,128)} %get-tuple-element.28), channel_id=1, source_target_pairs={{0,2},{1,3},{2,0},{3,1},{4,6},{5,7},{6,4},{7,5},{8,10},{9,11},{10,... | collective-permute-start | bytes 3145736 | tf_op jit(solution)/shard_map/ppermute | solution.py:142

commit v2 on v1

--- a/solution.py
+++ b/solution.py
@@ -14,6 +14,7 @@
 NC = 2
 LANES = 128
 SUBLANES = 8
+WIDTH = 256
 
 
 def split(values):
@@ -23,56 +24,64 @@
 
 
 def ladder_kernel(group, at_ref, v_ref, th_ref, tl_ref, *refs):
-    o_ref, part_ref = refs[-2:]
+    o_ref, vh_ref, vl_ref, part_ref = refs[-4:]
     b_width, depth = v_ref.shape[2:]
     half = b_width // 2
     rows = group * half
-    vh, vl = split(v_ref[...].reshape(group * b_width, depth))
-    width = SUBLANES * NO
+
+    @pl.when(pl.program_id(1) == 0)
+    def _():
+        vh_ref[...], vl_ref[...] = split(v_ref[...].reshape(group * b_width, depth))
+
+    pairs = WIDTH // LANES
     low_half = lax.broadcasted_iota(jnp.int32, (rows, LANES), 1) < NO
 
-    @pl.loop(0, NI // SUBLANES)
+    @pl.loop(0, SUBLANES * NO // WIDTH)
     def _(n):
-        columns = pl.ds(pl.multiple_of(n * width, width), width)
+        columns = pl.ds(pl.multiple_of(n * WIDTH, WIDTH), WIDTH)
         th, tl = th_ref[:, columns], tl_ref[:, columns]
+        vh, vl = vh_ref[...], vl_ref[...]
         dot = functools.partial(jnp.dot, preferred_element_type=jnp.float32)
         acc = dot(vh, tl) + dot(vl, th) + dot(vh, th)
-        for pair in range(SUBLANES // 2):
+        for pair in range(pairs):
             part_ref[pair] = acc[:, pair * LANES : (pair + 1) * LANES]
             even = part_ref[pair, pl.ds(0, rows, stride=2), :]
             odd = part_ref[pair, pl.ds(1, rows, stride=2), :]
             first = jnp.where(low_half, even, pltpu.roll(odd, NO, axis=1))
             second = jnp.where(low_half, pltpu.roll(even, NO, axis=1), odd)
+            i = 2 * (n * pairs + pair)
             for a in range(group):
-                base = (a * (NI // SUBLANES) + n) * half * SUBLANES + 2 * pair
-                o_ref[pl.ds(base, half, stride=SUBLANES), :] = first[a * half : (a + 1) * half]
-                o_ref[pl.ds(base + 1, half, stride=SUBLANES), :] = second[a * half : (a + 1) * half]
+                o_ref[a, pl.ds(i, half, stride=SUBLANES), :] = first[a * half : (a + 1) * half]
+                o_ref[a, pl.ds(i + 1, half, stride=SUBLANES), :] = second[a * half : (a + 1) * half]
 
 
 def multiply(at, integrals, th, tl, ladder, out_shape):
     avals, _, b_width, depth = integrals.shape
     group = 2 if avals % 2 == 0 else 1
-    block_rows = group * NI * b_width * NO // LANES
     aliased = ladder is not None
-    spec = pl.BlockSpec((depth, NI * NO), lambda g, at: (0, 0), pipeline_mode=pl.Buffered(1))
+    columns = SUBLANES * NO
+    spec = pl.BlockSpec((depth, columns), lambda g, n, at: (0, n))
     products = avals * b_width * depth * NI * NO
     return pl.pallas_call(
         functools.partial(ladder_kernel, group),
         out_shape=out_shape,
         grid_spec=pltpu.PrefetchScalarGridSpec(
             num_scalar_prefetch=1,
-            grid=(avals // group,),
+            grid=(avals // group, NI // SUBLANES),
             in_specs=[
-                pl.BlockSpec((group, 1, b_width, depth), lambda g, at: (g, at[1], 0, 0)),
+                pl.BlockSpec((group, 1, b_width, depth), lambda g, n, at: (g, at[1], 0, 0)),
                 spec,
                 spec,
             ]
             + [pl.BlockSpec(memory_space=pl.ANY)] * aliased,
-            out_specs=pl.BlockSpec((block_rows, LANES), lambda g, at: (at[0] // group + g, 0)),
-            scratch_shapes=[pltpu.VMEM((SUBLANES // 2, group * b_width, LANES), jnp.float32)],
+            out_specs=pl.BlockSpec(
+                (group, columns * b_width // LANES, LANES), lambda g, n, at: (at[0] // group + g, n, 0)
+            ),
+            scratch_shapes=[pltpu.VMEM((group * b_width, depth), jnp.bfloat16)] * 2
+            + [pltpu.VMEM((WIDTH // LANES, group * b_width, LANES), jnp.float32)],
         ),
         input_output_aliases={4: 0} if aliased else {},
-        compiler_params=pltpu.CompilerParams(vmem_limit_bytes=40 << 20),
+        compiler_params=pltpu.CompilerParams(vmem_limit_bytes=32 << 20),
         cost_estimate=pl.CostEstimate(
             flops=6 * products,
             bytes_accessed=4 * (integrals.size + avals * b_width * NI * NO + depth * NI * NO),
@@ -115,8 +124,8 @@
 def chunks_of(avals):
     if avals < 16:
         return [1] * avals
-    unit = avals // 8
-    return [unit, 2 * unit, 2 * unit, 2 * unit, unit]
+    unit = avals // 16
+    return [unit * count for count in (2, 2, 4, 4, 2, 1, 1)]
 
 
 def body(integrals, amplitudes):
@@ -148,8 +157,7 @@
     th, tl = rounded.astype(jnp.bfloat16), (panel - rounded).astype(jnp.bfloat16)
 
     rows = cols * avals * NI
-    tiles = rows * b_width * NO // LANES
-    out_shape = jax.ShapeDtypeStruct((tiles, LANES), jnp.float32)
+    out_shape = jax.ShapeDtypeStruct((cols * avals, NI * b_width * NO // LANES, LANES), jnp.float32)
     ladder = multiply(jnp.stack([here * avals, here]), blocks, th, tl, None, out_shape)
     for at, got in arrived:
         ladder = multiply(jnp.stack([at, jnp.zeros_like(at)]), got, th, tl, ladder, out_shape)

time: 833 us -> 864 us (1.037)
  starting transfers between devices: 199 us -> 108 us
  Pallas kernels: 200 us -> 264 us
  waiting for transfers between devices: 334 us -> 392 us
    ppermute x15 -> x21, starting transfers between devices: 191 us -> 99.6 us  [body(): lax.ppermute(piece, 'col', [(k, (k + shift) % cols) for k in range(cols)])]
    pallas_call x16 -> x22, Pallas kernels: 200 us -> 264 us  [multiply(): pl.pallas_call(functools.partial(ladder_kernel, group), out_shape=out_sha...]
    ppermute x15 -> x21, waiting for transfers between devices: 208 us -> 271 us  [body(): lax.ppermute(piece, 'col', [(k, (k + shift) % cols) for k in range(cols)])]
    dynamic_slice x5 -> x7, local copies, waits for them, and re-layouts: 24.8 us -> 27.7 us  [body(): lax.dynamic_slice(source, (start, (here + shift) % cols, 0, 0), (count, 1...]
  transfers between devices with their start and end apart: 20 -> 26, of which waited for: 9 -> 11; matrix products, arithmetic and copies ran while one was open for 11% -> 11% of each run, Pallas kernels for 23% -> 30%
where the time goes in v2:
time: 864 us; the launch traced here: 860 us
  waiting for transfers between devices  392 us (45%)
  Pallas kernels  264 us (31%)
  starting transfers between devices  108 us (12%)
  local copies, waits for them, and re-layouts  74.7 us (9%)
  other arithmetic  20.9 us (2%)
    ppermute x21, waiting for transfers between devices, body(): lax.ppermute(piece, 'col', [(k, (k + shift) % cols) for k in range(cols)])  271 us
    pallas_call x22, Pallas kernels, multiply(): pl.pallas_call(functools.partial(ladder_kernel, group), out_shape=out_sha...  264 us
    ppermute x5, waiting for transfers between devices, gather_over(): got = lax.ppermute(block, axis, [(k, k ^ mask) for k in range(size)])  121 us
    ppermute x21, starting transfers between devices, body(): lax.ppermute(piece, 'col', [(k, (k + shift) % cols) for k in range(cols)])  99.6 us
    dynamic_slice x7, local copies, waits for them, and re-layouts, body(): lax.dynamic_slice(source, (start, (here + shift) % cols, 0, 0), (count, 1...  27.7 us
  transfers between devices with their start and end apart: 26, of which 11 were waited for; matrix products, arithmetic and copies ran while one was open for 11% of the time, Pallas kernels for 30%

profile of v2, /device:TPU:25, one launch (start us, length us, event | category | flops | bytes accessed | tf_op | source)
XLA Modules:
  0.0 859.5 jit_solution(15247467005776802686)
XLA Ops:
  0.0 9.3 %collective-permute-done.1 = f32[1,64,1024]{2,1,0:T(8,128)S(1)} collective-permute-done((f32[1,64,1024]{2,1,0:T(8,128)}, f32[1,64,1024]{2,1,0:T(8,128)S(1)}, u32[]{:S(2)}, u32[]{:S(2)}) %collective-permute-start.1) | collective-permute-done | bytes 262176 | tf_op jit(solution)/shard_map/ppermute | solution.py:100
  10.3 4.0 collective-permute-start.2
  14.3 10.8 %collective-permute-done.2 = f32[2,64,1024]{2,1,0:T(8,128)S(1)} collective-permute-done((f32[2,64,1024]{2,1,0:T(8,128)S(1)}, f32[2,64,1024]{2,1,0:T(8,128)S(1)}, u32[]{:S(2)}, u32[]{:S(2)}) %collective-permute-start.2) | collective-permute-done | bytes 524320 | tf_op jit(solution)/shard_map/ppermute | solution.py:100
  33.7 3.6 constant_dynamic-slice_fusion.18
  40.4 3.7 constant_dynamic-slice_fusion.15
  46.1 5.9 constant_dynamic-slice_fusion.12
  51.9 27.7 %collective-permute-done.4 = f32[8,64,1024]{2,1,0:T(8,128)} collective-permute-done((f32[8,64,1024]{2,1,0:T(8,128)}, f32[8,64,1024]{2,1,0:T(8,128)}, u32[]{:S(2)}, u32[]{:S(2)}) %collective-permute-start.4) | collective-permute-done | bytes 2097184 | tf_op jit(solution)/shard_map/ppermute | solution.py:100
  82.9 5.7 constant_dynamic-slice_fusion.9
  88.7 3.6 constant_dynamic-slice_fusion.6
  101.9 70.7 %collective-permute-done.5 = f32[16,64,1024]{2,1,0:T(8,128)S(1)} collective-permute-done((f32[16,64,1024]{2,1,0:T(8,128)S(1)}, f32[16,64,1024]{2,1,0:T(8,128)S(1)}, u32[]{:S(2)}, u32[]{:S(2)}) %collective-permute-start.5) | collective-permute-done | bytes 4194336 | tf_op jit(solution)/shard_map/ppermute | solution.py:100
  178.0 4.3 reverse_select_fusion
  182.3 13.3 %reshape_reshape_reshape.3 = f32[32,2,32,16,64]{4,3,2,1,0:T(8,128)} reshape(f32[1,2,4,4,64,1024]{5,4,3,2,1,0:T(8,128)} %reverse_select_fusion) | data formatting | bytes 16777216 | tf_op jit(solution)/shard_map/reshape;reshape;reshape | solution.py:120
  195.6 15.8 %copy.24 = f32[2,32,16,32,64]{4,3,2,1,0:T(8,128)} copy(f32[2,32,16,32,64]{4,2,3,0,1:T(8,128)} %bitcast.83) | data formatting | bytes 16777216 | tf_op jit(solution)/shard_map/transpose | solution.py:120
  211.4 14.8 %reshape.21 = f32[1024,2048]{1,0:T(8,128)} reshape(f32[2,32,16,32,64]{4,3,2,1,0:T(8,128)} %copy.24) | data formatting | bytes 16777216 | tf_op jit(solution)/shard_map/reshape | solution.py:121
  226.2 5.2 fusion
  231.5 54.5 %shard_map.28.refs_0_ = f32[64,2048,128]{2,1,0:T(8,128)} custom-call(s32[2]{0:T(128)S(1)} %pad_add_fusion.21.at_ref, f32[16,4,128,1024]{3,2,1,0:T(8,128)} %bitcast.82, bf16[1024,2048]{1,0:T(8,128)(2,1)S(1)} %get-tuple-element.81.th_ref, bf16[1024,2048]{1,0:T(8,128)(2,1)S(1)} %get-tuple-element.80.tl_ref), custom_call_target="tpu_custom_call" | custom-call | flops 25769803776 | bytes 58720256 | tf_op jit(solution)/shard_map/pallas_call | solution.py:65
  286.2 7.8 shard_map.29.refs_0_
  297.4 7.8 shard_map.30.refs_0_
  305.2 7.8 shard_map.31.refs_0_
  313.5 8.9 %shard_map.32.refs_0_ = f32[64,2048,128]{2,1,0:T(8,128)} custom-call(s32[2]{0:T(128)S(1)} %pad_add_fusion.3.at_ref, f32[2,1,128,1024]{3,2,1,0:T(8,128)} %collective-permute-done.22.v_ref, bf16[1024,2048]{1,0:T(8,128)(2,1)S(1)} %get-tuple-element.81.th_ref, bf16[1024,2048]{1,0:T(8,128)(2,1)S(1)} %get-tuple-element.80.tl_ref, ...), custom_call_target="tpu_custom_call", output_to_operand_aliasing={{}: (4, {})} | custom-call | flops 3221225472 | bytes 11534336 | tf_op jit(solution)/shard_map/pallas_call | solution.py:65
  323.9 8.9 %shard_map.33.refs_0_ = f32[64,2048,128]{2,1,0:T(8,128)} custom-call(s32[2]{0:T(128)S(1)} %pad_add_fusion.4.at_ref, f32[2,1,128,1024]{3,2,1,0:T(8,128)} %collective-permute-done.21.v_ref, bf16[1024,2048]{1,0:T(8,128)(2,1)S(1)} %get-tuple-element.81.th_ref, bf16[1024,2048]{1,0:T(8,128)(2,1)S(1)} %get-tuple-element.80.tl_ref, ...), custom_call_target="tpu_custom_call", output_to_operand_aliasing={{}: (4, {})} | custom-call | flops 3221225472 | bytes 11534336 | tf_op jit(solution)/shard_map/pallas_call | solution.py:65
  332.8 115.3 %collective-permute-done.20.v_ref = f32[2,1,128,1024]{3,2,1,0:T(8,128)} collective-permute-done((f32[2,1,128,1024]{3,2,1,0:T(8,128)}, f32[2,1,128,1024]{3,2,1,0:T(8,128)}, u32[]{:S(2)}, u32[]{:S(2)}) %collective-permute-start.20) | collective-permute-done | bytes 1048608 | tf_op jit(solution)/shard_map/ppermute | solution.py:151
  448.1 8.9 %shard_map.34.refs_0_ = f32[64,2048,128]{2,1,0:T(8,128)} custom-call(s32[2]{0:T(128)S(1)} %pad_add_fusion.5.at_ref, f32[2,1,128,1024]{3,2,1,0:T(8,128)} %collective-permute-done.20.v_ref, bf16[1024,2048]{1,0:T(8,128)(2,1)S(1)} %get-tuple-element.81.th_ref, bf16[1024,2048]{1,0:T(8,128)(2,1)S(1)} %get-tuple-element.80.tl_ref, ...), custom_call_target="tpu_custom_call", output_to_operand_aliasing={{}: (4, {})} | custom-call | flops 3221225472 | bytes 11534336 | tf_op jit(solution)/shard_map/pallas_call | solution.py:65
  457.0 15.3 %shard_map.35.refs_0_ = f32[64,2048,128]{2,1,0:T(8,128)} custom-call(s32[2]{0:T(128)S(1)} %pad_add_fusion.6.at_ref, f32[4,1,128,1024]{3,2,1,0:T(8,128)} %collective-permute-done.19.v_ref, bf16[1024,2048]{1,0:T(8,128)(2,1)S(1)} %get-tuple-element.81.th_ref, bf16[1024,2048]{1,0:T(8,128)(2,1)S(1)} %get-tuple-element.80.tl_ref, ...), custom_call_target="tpu_custom_call", output_to_operand_aliasing={{}: (4, {})} | custom-call | flops 6442450944 | bytes 14680064 | tf_op jit(solution)/shard_map/pallas_call | solution.py:65
  472.3 3.3 collective-permute-start.13
  475.5 15.3 %shard_map.36.refs_0_ = f32[64,2048,128]{2,1,0:T(8,128)} custom-call(s32[2]{0:T(128)S(1)} %pad_add_fusion.7.at_ref, f32[4,1,128,1024]{3,2,1,0:T(8,128)} %collective-permute-done.18.v_ref, bf16[1024,2048]{1,0:T(8,128)(2,1)S(1)} %get-tuple-element.81.th_ref, bf16[1024,2048]{1,0:T(8,128)(2,1)S(1)} %get-tuple-element.80.tl_ref, ...), custom_call_target="tpu_custom_call", output_to_operand_aliasing={{}: (4, {})} | custom-call | flops 6442450944 | bytes 14680064 | tf_op jit(solution)/shard_map/pallas_call | solution.py:65
  490.8 92.1 %collective-permute-done.17.v_ref = f32[4,1,128,1024]{3,2,1,0:T(8,128)} collective-permute-done((f32[4,1,128,1024]{3,2,1,0:T(8,128)}, f32[4,1,128,1024]{3,2,1,0:T(8,128)}, u32[]{:S(2)}, u32[]{:S(2)}) %collective-permute-start.17) | collective-permute-done | bytes 2097184 | tf_op jit(solution)/shard_map/ppermute | solution.py:151
  583.0 17.4 %collective-permute-start.12 = (f32[2,1,128,1024]{3,2,1,0:T(8,128)}, f32[2,1,128,1024]{3,2,1,0:T(8,128)}, u32[]{:S(2)}, u32[]{:S(2)}) collective-permute-start(f32[2,1,128,1024]{3,2,1,0:T(8,128)} %get-tuple-element.45), channel_id=1, source_target_pairs={{0,3},{1,0},{2,1},{3,2},{4,7},{5,4},{6,5},{7,6},{8,11},{9,8},{10,9... | collective-permute-start | bytes 3145736 | tf_op jit(solution)/shard_map/ppermute | solution.py:151
  600.4 15.3 %shard_map.37.refs_0_ = f32[64,2048,128]{2,1,0:T(8,128)} custom-call(s32[2]{0:T(128)S(1)} %pad_add_fusion.8.at_ref, f32[4,1,128,1024]{3,2,1,0:T(8,128)} %collective-permute-done.17.v_ref, bf16[1024,2048]{1,0:T(8,128)(2,1)S(1)} %get-tuple-element.81.th_ref, bf16[1024,2048]{1,0:T(8,128)(2,1)S(1)} %get-tuple-element.80.tl_ref, ...), custom_call_target="tpu_custom_call", output_to_operand_aliasing={{}: (4, {})} | custom-call | flops 6442450944 | bytes 14680064 | tf_op jit(solution)/shard_map/pallas_call | solution.py:65
  615.7 33.9 %collective-permute-start.11 = (f32[2,1,128,1024]{3,2,1,0:T(8,128)}, f32[2,1,128,1024]{3,2,1,0:T(8,128)}, u32[]{:S(2)}, u32[]{:S(2)}) collective-permute-start(f32[2,1,128,1024]{3,2,1,0:T(8,128)} %get-tuple-element.44), channel_id=1, source_target_pairs={{0,2},{1,3},{2,0},{3,1},{4,6},{5,7},{6,4},{7,5},{8,10},{9,11},{10,... | collective-permute-start | bytes 3145736 | tf_op jit(solution)/shard_map/ppermute | solution.py:151
  649.6 15.3 %shard_map.38.refs_0_ = f32[64,2048,128]{2,1,0:T(8,128)} custom-call(s32[2]{0:T(128)S(1)} %pad_add_fusion.9.at_ref, f32[4,1,128,1024]{3,2,1,0:T(8,128)} %collective-permute-done.16.v_ref, bf16[1024,2048]{1,0:T(8,128)(2,1)S(1)} %get-tuple-element.81.th_ref, bf16[1024,2048]{1,0:T(8,128)(2,1)S(1)} %get-tuple-element.80.tl_ref, ...), custom_call_target="tpu_custom_call", output_to_operand_aliasing={{}: (4, {})} | custom-call | flops 6442450944 | bytes 14680064 | tf_op jit(solution)/shard_map/pallas_call | solution.py:65
  668.0 15.3 %shard_map.39.refs_0_ = f32[64,2048,128]{2,1,0:T(8,128)} custom-call(s32[2]{0:T(128)S(1)} %pad_add_fusion.10.at_ref, f32[4,1,128,1024]{3,2,1,0:T(8,128)} %collective-permute-done.15.v_ref, bf16[1024,2048]{1,0:T(8,128)(2,1)S(1)} %get-tuple-element.81.th_ref, bf16[1024,2048]{1,0:T(8,128)(2,1)S(1)} %get-tuple-element.80.tl_ref, ...), custom_call_target="tpu_custom_call", output_to_operand_aliasing={{}: (4, {})} | custom-call | flops 6442450944 | bytes 14680064 | tf_op jit(solution)/shard_map/pallas_call | solution.py:65
  683.3 34.5 %collective-permute-done.14.v_ref = f32[4,1,128,1024]{3,2,1,0:T(8,128)} collective-permute-done((f32[4,1,128,1024]{3,2,1,0:T(8,128)}, f32[4,1,128,1024]{3,2,1,0:T(8,128)}, u32[]{:S(2)}, u32[]{:S(2)}) %collective-permute-start.14) | collective-permute-done | bytes 2097184 | tf_op jit(solution)/shard_map/ppermute | solution.py:151
  717.8 6.2 collective-permute-start.9
  724.0 15.3 %shard_map.40.refs_0_ = f32[64,2048,128]{2,1,0:T(8,128)} custom-call(s32[2]{0:T(128)S(1)} %pad_add_fusion.11.at_ref, f32[4,1,128,1024]{3,2,1,0:T(8,128)} %collective-permute-done.14.v_ref, bf16[1024,2048]{1,0:T(8,128)(2,1)S(1)} %get-tuple-element.81.th_ref, bf16[1024,2048]{1,0:T(8,128)(2,1)S(1)} %get-tuple-element.80.tl_ref, ...), custom_call_target="tpu_custom_call", output_to_operand_aliasing={{}: (4, {})} | custom-call | flops 6442450944 | bytes 14680064 | tf_op jit(solution)/shard_map/pallas_call | solution.py:65
  739.3 11.5 %collective-permute-start.8 = (f32[1,1,128,1024]{3,2,1,0:T(8,128)}, f32[1,1,128,1024]{3,2,1,0:T(8,128)}, u32[]{:S(2)}, u32[]{:S(2)}) collective-permute-start(f32[1,1,128,1024]{3,2,1,0:T(8,128)} %get-tuple-element.41), channel_id=1, source_target_pairs={{0,2},{1,3},{2,0},{3,1},{4,6},{5,7},{6,4},{7,5},{8,10},{9,11},{10,... | collective-permute-start | bytes 1572872 | tf_op jit(solution)/shard_map/ppermute | solution.py:151
  750.8 8.9 %shard_map.41.refs_0_ = f32[64,2048,128]{2,1,0:T(8,128)} custom-call(s32[2]{0:T(128)S(1)} %pad_add_fusion.12.at_ref, f32[2,1,128,1024]{3,2,1,0:T(8,128)} %collective-permute-done.13.v_ref, bf16[1024,2048]{1,0:T(8,128)(2,1)S(1)} %get-tuple-element.81.th_ref, bf16[1024,2048]{1,0:T(8,128)(2,1)S(1)} %get-tuple-element.80.tl_ref, ...), custom_call_target="tpu_custom_call", output_to_operand_aliasing={{}: (4, {})} | custom-call | flops 3221225472 | bytes 11534336 | tf_op jit(solution)/shard_map/pallas_call | solution.py:65
  762.8 8.9 %shard_map.42.refs_0_ = f32[64,2048,128]{2,1,0:T(8,128)} custom-call(s32[2]{0:T(128)S(1)} %pad_add_fusion.13.at_ref, f32[2,1,128,1024]{3,2,1,0:T(8,128)} %collective-permute-done.12.v_ref, bf16[1024,2048]{1,0:T(8,128)(2,1)S(1)} %get-tuple-element.81.th_ref, bf16[1024,2048]{1,0:T(8,128)(2,1)S(1)} %get-tuple-element.80.tl_ref, ...), custom_call_target="tpu_custom_call", output_to_operand_aliasing={{}: (4, {})} | custom-call | flops 3221225472 | bytes 11534336 | tf_op jit(solution)/shard_map/pallas_call | solution.py:65
  771.6 13.6 %collective-permute-done.11.v_ref = f32[2,1,128,1024]{3,2,1,0:T(8,128)} collective-permute-done((f32[2,1,128,1024]{3,2,1,0:T(8,128)}, f32[2,1,128,1024]{3,2,1,0:T(8,128)}, u32[]{:S(2)}, u32[]{:S(2)}) %collective-permute-start.11) | collective-permute-done | bytes 1048608 | tf_op jit(solution)/shard_map/ppermute | solution.py:151
  785.3 6.1 collective-permute-start.6
  791.4 8.9 %shard_map.43.refs_0_ = f32[64,2048,128]{2,1,0:T(8,128)} custom-call(s32[2]{0:T(128)S(1)} %pad_add_fusion.14.at_ref, f32[2,1,128,1024]{3,2,1,0:T(8,128)} %collective-permute-done.11.v_ref, bf16[1024,2048]{1,0:T(8,128)(2,1)S(1)} %get-tuple-element.81.th_ref, bf16[1024,2048]{1,0:T(8,128)(2,1)S(1)} %get-tuple-element.80.tl_ref, ...), custom_call_target="tpu_custom_call", output_to_operand_aliasing={{}: (4, {})} | custom-call | flops 3221225472 | bytes 11534336 | tf_op jit(solution)/shard_map/pallas_call | solution.py:65
  803.4 6.8 shard_map.44.refs_0_
  810.2 6.8 shard_map.45.refs_0_
  817.0 13.2 %collective-permute-done.8.v_ref = f32[1,1,128,1024]{3,2,1,0:T(8,128)} collective-permute-done((f32[1,1,128,1024]{3,2,1,0:T(8,128)}, f32[1,1,128,1024]{3,2,1,0:T(8,128)}, u32[]{:S(2)}, u32[]{:S(2)}) %collective-permute-start.8) | collective-permute-done | bytes 524320 | tf_op jit(solution)/shard_map/ppermute | solution.py:151
  830.2 6.8 shard_map.46.refs_0_
  837.0 6.8 shard_map.47.refs_0_
  843.9 6.8 shard_map.48.refs_0_
  852.7 6.8 shard_map.49
  (85 shorter events, 49.8 us)
Async XLA Ops:
  0.0 9.3 %collective-permute-start.1 = (f32[1,64,1024]{2,1,0:T(8,128)}, f32[1,64,1024]{2,1,0:T(8,128)S(1)}, u32[]{:S(2)}, u32[]{:S(2)}) collective-permute-start(f32[1,64,1024]{2,1,0:T(8,128)} %bitcast.92), channel_id=1, source_target_pairs={{0,3},{1,2},{2,1},{3,0},{4,7},{5,6},{6,5},{7,4},{8,11},{9,10},{10,... | collective-permute-start | bytes 786440 | tf_op jit(solution)/shard_map/ppermute | solution.py:100
  10.3 14.7 %collective-permute-start.2 = (f32[2,64,1024]{2,1,0:T(8,128)S(1)}, f32[2,64,1024]{2,1,0:T(8,128)S(1)}, u32[]{:S(2)}, u32[]{:S(2)}) collective-permute-start(f32[2,64,1024]{2,1,0:T(8,128)S(1)} %pad_maximum_fusion.3), channel_id=1, source_target_pairs={{0,1},{1,0},{2,3},{3,2},{4,5},{5,4},{6,7},{7,6},{8,9},{9,8},{10,11... | collective-permute-start | bytes 1572872 | tf_op jit(solution)/shard_map/ppermute | solution.py:100
  26.4 11.0 %copy-start = (f32[1,2,2,1,64,1024]{5,4,2,1,3,0:T(8,128)}, f32[1,2,2,1,64,1024]{5,4,2,1,3,0:T(8,128)S(1)}, u32[]{:S(2)}) copy-start(f32[1,2,2,1,64,1024]{5,4,2,1,3,0:T(8,128)S(1)} %reverse_select_fusion.3) | copy-start | bytes 3145732
  26.4 4.5 collective-permute-start.3
  30.9 7.8 copy-start.2
  32.5 47.1 %collective-permute-start.4 = (f32[8,64,1024]{2,1,0:T(8,128)}, f32[8,64,1024]{2,1,0:T(8,128)}, u32[]{:S(2)}, u32[]{:S(2)}) collective-permute-start(f32[8,64,1024]{2,1,0:T(8,128)} %pad_maximum_fusion.1), channel_id=1, source_target_pairs={{0,8},{4,12},{8,0},{12,4},{16,24},{20,28},{24,16},{28,20},{1,9},{5... | collective-permute-start | bytes 6291464 | tf_op jit(solution)/shard_map/ppermute | solution.py:100
  37.4 248.6 %collective-permute-start.25 = (f32[2,1,128,1024]{3,2,1,0:T(8,128)}, f32[2,1,128,1024]{3,2,1,0:T(8,128)S(1)}, u32[]{:S(2)}, u32[]{:S(2)}) collective-permute-start(f32[2,1,128,1024]{3,2,1,0:T(8,128)} %get-tuple-element.58), channel_id=1, source_target_pairs={{0,1},{1,2},{2,3},{3,0},{4,5},{5,6},{6,7},{7,4},{8,9},{9,10},{10,1... | collective-permute-start | bytes 3145736 | tf_op jit(solution)/shard_map/ppermute | solution.py:151
  38.6 255.4 %collective-permute-start.24 = (f32[2,1,128,1024]{3,2,1,0:T(8,128)}, f32[2,1,128,1024]{3,2,1,0:T(8,128)S(1)}, u32[]{:S(2)}, u32[]{:S(2)}) collective-permute-start(f32[2,1,128,1024]{3,2,1,0:T(8,128)} %get-tuple-element.57), channel_id=1, source_target_pairs={{0,3},{1,0},{2,1},{3,2},{4,7},{5,4},{6,5},{7,6},{8,11},{9,8},{10,9... | collective-permute-start | bytes 3145736 | tf_op jit(solution)/shard_map/ppermute | solution.py:151
  38.9 256.7 %collective-permute-start.23 = (f32[2,1,128,1024]{3,2,1,0:T(8,128)}, f32[2,1,128,1024]{3,2,1,0:T(8,128)S(1)}, u32[]{:S(2)}, u32[]{:S(2)}) collective-permute-start(f32[2,1,128,1024]{3,2,1,0:T(8,128)} %get-tuple-element.56), channel_id=1, source_target_pairs={{0,2},{1,3},{2,0},{3,1},{4,6},{5,7},{6,4},{7,5},{8,10},{9,11},{10,... | collective-permute-start | bytes 3145736 | tf_op jit(solution)/shard_map/ppermute | solution.py:151
  44.0 268.9 %collective-permute-start.22 = (f32[2,1,128,1024]{3,2,1,0:T(8,128)}, f32[2,1,128,1024]{3,2,1,0:T(8,128)}, u32[]{:S(2)}, u32[]{:S(2)}) collective-permute-start(f32[2,1,128,1024]{3,2,1,0:T(8,128)} %get-tuple-element.55), channel_id=1, source_target_pairs={{0,1},{1,2},{2,3},{3,0},{4,5},{5,6},{6,7},{7,4},{8,9},{9,10},{10,1... | collective-permute-start | bytes 3145736 | tf_op jit(solution)/shard_map/ppermute | solution.py:151
  46.1 33.6 %copy-start.1 = (f32[1,2,2,1,64,1024]{5,4,2,1,3,0:T(8,128)S(1)}, f32[1,2,2,1,64,1024]{5,4,2,1,3,0:T(8,128)}, u32[]{:S(2)}) copy-start(f32[1,2,2,1,64,1024]{5,4,2,1,3,0:T(8,128)} %copy-done) | copy-start | bytes 3145732
  46.1 33.6 %copy-start.3 = (f32[4,64,1024]{2,1,0:T(8,128)S(1)}, f32[4,64,1024]{2,1,0:T(8,128)}, u32[]{:S(2)}) copy-start(f32[4,64,1024]{2,1,0:T(8,128)} %copy-done.2) | copy-start | bytes 3145732
  81.6 91.0 %collective-permute-start.5 = (f32[16,64,1024]{2,1,0:T(8,128)S(1)}, f32[16,64,1024]{2,1,0:T(8,128)S(1)}, u32[]{:S(2)}, u32[]{:S(2)}) collective-permute-start(f32[16,64,1024]{2,1,0:T(8,128)S(1)} %pad_maximum_fusion), channel_id=1, source_target_pairs={{0,16},{4,20},{8,24},{12,28},{16,0},{20,4},{24,8},{28,12},{1,17},{... | collective-permute-start | bytes 12582920 | tf_op jit(solution)/shard_map/ppermute | solution.py:100
  172.6 284.4 %collective-permute-start.19 = (f32[4,1,128,1024]{3,2,1,0:T(8,128)}, f32[4,1,128,1024]{3,2,1,0:T(8,128)}, u32[]{:S(2)}, u32[]{:S(2)}) collective-permute-start(f32[4,1,128,1024]{3,2,1,0:T(8,128)} %get-tuple-element.52), channel_id=1, source_target_pairs={{0,1},{1,2},{2,3},{3,0},{4,5},{5,6},{6,7},{7,4},{8,9},{9,10},{10,1... | collective-permute-start | bytes 6291464 | tf_op jit(solution)/shard_map/ppermute | solution.py:151
  286.0 36.3 %collective-permute-start.21 = (f32[2,1,128,1024]{3,2,1,0:T(8,128)}, f32[2,1,128,1024]{3,2,1,0:T(8,128)}, u32[]{:S(2)}, u32[]{:S(2)}) collective-permute-start(f32[2,1,128,1024]{3,2,1,0:T(8,128)} %get-tuple-element.54), channel_id=1, source_target_pairs={{0,3},{1,0},{2,1},{3,2},{4,7},{5,4},{6,5},{7,6},{8,11},{9,8},{10,9... | collective-permute-start | bytes 3145736 | tf_op jit(solution)/shard_map/ppermute | solution.py:151
  294.0 154.1 %collective-permute-start.20 = (f32[2,1,128,1024]{3,2,1,0:T(8,128)}, f32[2,1,128,1024]{3,2,1,0:T(8,128)}, u32[]{:S(2)}, u32[]{:S(2)}) collective-permute-start(f32[2,1,128,1024]{3,2,1,0:T(8,128)} %get-tuple-element.53), channel_id=1, source_target_pairs={{0,2},{1,3},{2,0},{3,1},{4,6},{5,7},{6,4},{7,5},{8,10},{9,11},{10,... | collective-permute-start | bytes 3145736 | tf_op jit(solution)/shard_map/ppermute | solution.py:151
  295.6 176.7 %collective-permute-start.18 = (f32[4,1,128,1024]{3,2,1,0:T(8,128)}, f32[4,1,128,1024]{3,2,1,0:T(8,128)}, u32[]{:S(2)}, u32[]{:S(2)}) collective-permute-start(f32[4,1,128,1024]{3,2,1,0:T(8,128)} %get-tuple-element.51), channel_id=1, source_target_pairs={{0,3},{1,0},{2,1},{3,2},{4,7},{5,4},{6,5},{7,6},{8,11},{9,8},{10,9... | collective-permute-start | bytes 6291464 | tf_op jit(solution)/shard_map/ppermute | solution.py:151
  313.0 270.0 %collective-permute-start.17 = (f32[4,1,128,1024]{3,2,1,0:T(8,128)}, f32[4,1,128,1024]{3,2,1,0:T(8,128)}, u32[]{:S(2)}, u32[]{:S(2)}) collective-permute-start(f32[4,1,128,1024]{3,2,1,0:T(8,128)} %get-tuple-element.50), channel_id=1, source_target_pairs={{0,2},{1,3},{2,0},{3,1},{4,6},{5,7},{6,4},{7,5},{8,10},{9,11},{10,... | collective-permute-start | bytes 6291464 | tf_op jit(solution)/shard_map/ppermute | solution.py:151
  322.3 293.4 %collective-permute-start.16 = (f32[4,1,128,1024]{3,2,1,0:T(8,128)}, f32[4,1,128,1024]{3,2,1,0:T(8,128)}, u32[]{:S(2)}, u32[]{:S(2)}) collective-permute-start(f32[4,1,128,1024]{3,2,1,0:T(8,128)} %get-tuple-element.49), channel_id=1, source_target_pairs={{0,1},{1,2},{2,3},{3,0},{4,5},{5,6},{6,7},{7,4},{8,9},{9,10},{10,1... | collective-permute-start | bytes 6291464 | tf_op jit(solution)/shard_map/ppermute | solution.py:151
  448.1 216.8 %collective-permute-start.15 = (f32[4,1,128,1024]{3,2,1,0:T(8,128)}, f32[4,1,128,1024]{3,2,1,0:T(8,128)}, u32[]{:S(2)}, u32[]{:S(2)}) collective-permute-start(f32[4,1,128,1024]{3,2,1,0:T(8,128)} %get-tuple-element.48), channel_id=1, source_target_pairs={{0,3},{1,0},{2,1},{3,2},{4,7},{5,4},{6,5},{7,6},{8,11},{9,8},{10,9... | collective-permute-start | bytes 6291464 | tf_op jit(solution)/shard_map/ppermute | solution.py:151
  457.0 260.9 %collective-permute-start.14 = (f32[4,1,128,1024]{3,2,1,0:T(8,128)}, f32[4,1,128,1024]{3,2,1,0:T(8,128)}, u32[]{:S(2)}, u32[]{:S(2)}) collective-permute-start(f32[4,1,128,1024]{3,2,1,0:T(8,128)} %get-tuple-element.47), channel_id=1, source_target_pairs={{0,2},{1,3},{2,0},{3,1},{4,6},{5,7},{6,4},{7,5},{8,10},{9,11},{10,... | collective-permute-start | bytes 6291464 | tf_op jit(solution)/shard_map/ppermute | solution.py:151
  472.3 267.0 %collective-permute-start.13 = (f32[2,1,128,1024]{3,2,1,0:T(8,128)}, f32[2,1,128,1024]{3,2,1,0:T(8,128)}, u32[]{:S(2)}, u32[]{:S(2)}) collective-permute-start(f32[2,1,128,1024]{3,2,1,0:T(8,128)} %get-tuple-element.46), channel_id=1, source_target_pairs={{0,1},{1,2},{2,3},{3,0},{4,5},{5,6},{6,7},{7,4},{8,9},{9,10},{10,1... | collective-permute-start | bytes 3145736 | tf_op jit(solution)/shard_map/ppermute | solution.py:151
  583.0 176.7 %collective-permute-start.12 = (f32[2,1,128,1024]{3,2,1,0:T(8,128)}, f32[2,1,128,1024]{3,2,1,0:T(8,128)}, u32[]{:S(2)}, u32[]{:S(2)}) collective-permute-start(f32[2,1,128,1024]{3,2,1,0:T(8,128)} %get-tuple-element.45), channel_id=1, source_target_pairs={{0,3},{1,0},{2,1},{3,2},{4,7},{5,4},{6,5},{7,6},{8,11},{9,8},{10,9... | collective-permute-start | bytes 3145736 | tf_op jit(solution)/shard_map/ppermute | solution.py:151
  615.7 169.6 %collective-permute-start.11 = (f32[2,1,128,1024]{3,2,1,0:T(8,128)}, f32[2,1,128,1024]{3,2,1,0:T(8,128)}, u32[]{:S(2)}, u32[]{:S(2)}) collective-permute-start(f32[2,1,128,1024]{3,2,1,0:T(8,128)} %get-tuple-element.44), channel_id=1, source_target_pairs={{0,2},{1,3},{2,0},{3,1},{4,6},{5,7},{6,4},{7,5},{8,10},{9,11},{10,... | collective-permute-start | bytes 3145736 | tf_op jit(solution)/shard_map/ppermute | solution.py:151
  664.9 135.3 %collective-permute-start.10 = (f32[1,1,128,1024]{3,2,1,0:T(8,128)}, f32[1,1,128,1024]{3,2,1,0:T(8,128)}, u32[]{:S(2)}, u32[]{:S(2)}) collective-permute-start(f32[1,1,128,1024]{3,2,1,0:T(8,128)} %get-tuple-element.43), channel_id=1, source_target_pairs={{0,1},{1,2},{2,3},{3,0},{4,5},{5,6},{6,7},{7,4},{8,9},{9,10},{10,1... | collective-permute-start | bytes 1572872 | tf_op jit(solution)/shard_map/ppermute | solution.py:151
  717.8 92.4 %collective-permute-start.9 = (f32[1,1,128,1024]{3,2,1,0:T(8,128)}, f32[1,1,128,1024]{3,2,1,0:T(8,128)}, u32[]{:S(2)}, u32[]{:S(2)}) collective-permute-start(f32[1,1,128,1024]{3,2,1,0:T(8,128)} %get-tuple-element.42), channel_id=1, source_target_pairs={{0,3},{1,0},{2,1},{3,2},{4,7},{5,4},{6,5},{7,6},{8,11},{9,8},{10,9... | collective-permute-start | bytes 1572872 | tf_op jit(solution)/shard_map/ppermute | solution.py:151
  739.3 90.9 %collective-permute-start.8 = (f32[1,1,128,1024]{3,2,1,0:T(8,128)}, f32[1,1,128,1024]{3,2,1,0:T(8,128)}, u32[]{:S(2)}, u32[]{:S(2)}) collective-permute-start(f32[1,1,128,1024]{3,2,1,0:T(8,128)} %get-tuple-element.41), channel_id=1, source_target_pairs={{0,2},{1,3},{2,0},{3,1},{4,6},{5,7},{6,4},{7,5},{8,10},{9,11},{10,... | collective-permute-start | bytes 1572872 | tf_op jit(solution)/shard_map/ppermute | solution.py:151
  759.7 77.4 %collective-permute-start.7 = (f32[1,1,128,1024]{3,2,1,0:T(8,128)}, f32[1,1,128,1024]{3,2,1,0:T(8,128)}, u32[]{:S(2)}, u32[]{:S(2)}) collective-permute-start(f32[1,1,128,1024]{3,2,1,0:T(8,128)} %get-tuple-element.40), channel_id=1, source_target_pairs={{0,1},{1,2},{2,3},{3,0},{4,5},{5,6},{6,7},{7,4},{8,9},{9,10},{10,1... | collective-permute-start | bytes 1572872 | tf_op jit(solution)/shard_map/ppermute | solution.py:151
  785.3 58.6 %collective-permute-start.6 = (f32[1,1,128,1024]{3,2,1,0:T(8,128)}, f32[1,1,128,1024]{3,2,1,0:T(8,128)}, u32[]{:S(2)}, u32[]{:S(2)}) collective-permute-start(f32[1,1,128,1024]{3,2,1,0:T(8,128)} %get-tuple-element.39), channel_id=1, source_target_pairs={{0,3},{1,0},{2,1},{3,2},{4,7},{5,4},{6,5},{7,6},{8,11},{9,8},{10,9... | collective-permute-start | bytes 1572872 | tf_op jit(solution)/shard_map/ppermute | solution.py:151
  800.3 52.4 %collective-permute-start = (f32[1,1,128,1024]{3,2,1,0:T(8,128)}, f32[1,1,128,1024]{3,2,1,0:T(8,128)}, u32[]{:S(2)}, u32[]{:S(2)}) collective-permute-start(f32[1,1,128,1024]{3,2,1,0:T(8,128)} %get-tuple-element.38), channel_id=1, source_target_pairs={{0,2},{1,3},{2,0},{3,1},{4,6},{5,7},{6,4},{7,5},{8,10},{9,11},{10,... | collective-permute-start | bytes 1572872 | tf_op jit(solution)/shard_map/ppermute | solution.py:151

commit v3 on v2

--- a/solution.py
+++ b/solution.py
@@ -14,7 +14,6 @@
 NC = 2
 LANES = 128
 SUBLANES = 8
-WIDTH = 256
 
 
 def split(values):
@@ -23,62 +22,62 @@
     return high, low
 
 
-def ladder_kernel(group, at_ref, v_ref, th_ref, tl_ref, *refs):
+def ladder_kernel(group, width, at_ref, v_ref, th_ref, tl_ref, *refs):
     o_ref, vh_ref, vl_ref, part_ref = refs[-4:]
     b_width, depth = v_ref.shape[2:]
     half = b_width // 2
     rows = group * half
-
-    @pl.when(pl.program_id(1) == 0)
-    def _():
-        vh_ref[...], vl_ref[...] = split(v_ref[...].reshape(group * b_width, depth))
-
-    pairs = WIDTH // LANES
+    vh_ref[...], vl_ref[...] = split(v_ref[...].reshape(group * b_width, depth))
     low_half = lax.broadcasted_iota(jnp.int32, (rows, LANES), 1) < NO
 
-    @pl.loop(0, SUBLANES * NO // WIDTH)
-    def _(n):
-        columns = pl.ds(pl.multiple_of(n * WIDTH, WIDTH), WIDTH)
+    def step(n, columns):
         th, tl = th_ref[:, columns], tl_ref[:, columns]
         vh, vl = vh_ref[...], vl_ref[...]
         dot = functools.partial(jnp.dot, preferred_element_type=jnp.float32)
         acc = dot(vh, tl) + dot(vl, th) + dot(vh, th)
-        for pair in range(pairs):
+        for pair in range(width // LANES):
             part_ref[pair] = acc[:, pair * LANES : (pair + 1) * LANES]
             even = part_ref[pair, pl.ds(0, rows, stride=2), :]
             odd = part_ref[pair, pl.ds(1, rows, stride=2), :]
             first = jnp.where(low_half, even, pltpu.roll(odd, NO, axis=1))
             second = jnp.where(low_half, pltpu.roll(even, NO, axis=1), odd)
-            i = 2 * (n * pairs + pair)
+            block, i = divmod(2 * pair, SUBLANES)
+            at = (n * (width // (SUBLANES * NO)) + block) * half * SUBLANES + i
             for a in range(group):
-                o_ref[a, pl.ds(i, half, stride=SUBLANES), :] = first[a * half : (a + 1) * half]
-                o_ref[a, pl.ds(i + 1, half, stride=SUBLANES), :] = second[a * half : (a + 1) * half]
+                o_ref[a, pl.ds(at, half, stride=SUBLANES), :] = first[a * half : (a + 1) * half]
+                o_ref[a, pl.ds(at + 1, half, stride=SUBLANES), :] = second[a * half : (a + 1) * half]
+
+    steps = NI * NO // width
+    if steps == 1:
+        step(0, slice(None))
+    else:
+
+        @pl.loop(0, steps)
+        def _(n):
+            step(n, pl.ds(pl.multiple_of(n * width, width), width))
 
 
-def multiply(at, integrals, th, tl, ladder, out_shape):
+def multiply(at, integrals, th, tl, ladder, out_shape, width=SUBLANES * NO):
     avals, _, b_width, depth = integrals.shape
     group = 2 if avals % 2 == 0 else 1
     aliased = ladder is not None
-    columns = SUBLANES * NO
-    spec = pl.BlockSpec((depth, columns), lambda g, n, at: (0, n))
+    spec = pl.BlockSpec((depth, NI * NO), lambda g, at: (0, 0), pipeline_mode=pl.Buffered(1))
     products = avals * b_width * depth * NI * NO
     return pl.pallas_call(
-        functools.partial(ladder_kernel, group),
+        functools.partial(ladder_kernel, group, width),
         out_shape=out_shape,
         grid_spec=pltpu.PrefetchScalarGridSpec(
             num_scalar_prefetch=1,
-            grid=(avals // group, NI // SUBLANES),
+            grid=(avals // group,),
             in_specs=[
-                pl.BlockSpec((group, 1, b_width, depth), lambda g, n, at: (g, at[1], 0, 0)),
+                pl.BlockSpec((group, 1, b_width, depth), lambda g, at: (g, at[1], 0, 0)),
                 spec,
                 spec,
             ]
             + [pl.BlockSpec(memory_space=pl.ANY)] * aliased,
-            out_specs=pl.BlockSpec(
-                (group, columns * b_width // LANES, LANES), lambda g, n, at: (at[0] // group + g, n, 0)
-            ),
+            out_specs=pl.BlockSpec((group,) + out_shape.shape[1:], lambda g, at: (at[0] // group + g, 0, 0)),
             scratch_shapes=[pltpu.VMEM((group * b_width, depth), jnp.bfloat16)] * 2
-            + [pltpu.VMEM((WIDTH // LANES, group * b_width, LANES), jnp.float32)],
+            + [pltpu.VMEM((width // LANES, group * b_width, LANES), jnp.float32)],
         ),
         input_output_aliases={4: 0} if aliased else {},
         compiler_params=pltpu.CompilerParams(vmem_limit_bytes=32 << 20),
@@ -121,11 +120,17 @@
     return panel.reshape(NC * NV, NI * NO)
 
 
-def chunks_of(avals):
+def rounds_of(avals, cols):
+    shifts = [s for pair in zip(range(1, cols), range(cols - 1, 0, -1)) for s in pair]
+    shifts = list(dict.fromkeys(shifts))
     if avals < 16:
-        return [1] * avals
+        sizes = [2] * (avals // 2 - 1) + [1, 1] if avals % 2 == 0 else [1] * avals
+        return [[(shift, sum(sizes[:k]), sizes[k]) for shift in shifts] for k in range(len(sizes))]
     unit = avals // 16
-    return [unit * count for count in (2, 2, 4, 4, 2, 1, 1)]
+    rounds = [[(shift, start * unit, count * unit) for shift in shifts] for start, count in ((0, 2), (2, 2), (4, 4))]
+    rounds.append([(shift, 8 * unit, 8 * unit) for shift in shifts[:-1]] + [(shifts[-1], 8 * unit, 4 * unit)])
+    rounds += [[(shifts[-1], start * unit, count * unit)] for start, count in ((12, 2), (14, 1), (15, 1))]
+    return rounds
 
 
 def body(integrals, amplitudes):
@@ -136,21 +141,18 @@
     depth = integrals.shape[1]
     blocks = integrals.reshape(avals, cols, b_width, depth)
 
-    shifts = [s for pair in zip(range(1, cols), range(cols - 1, 0, -1)) for s in pair]
-    shifts = list(dict.fromkeys(shifts))
     arrived = []
-    start = 0
     source = blocks
-    for count in chunks_of(avals):
+    for exchanges in rounds_of(avals, cols):
         pieces = [
             lax.dynamic_slice(source, (start, (here + shift) % cols, 0, 0), (count, 1, b_width, depth))
-            for shift in shifts
+            for shift, start, count in exchanges
         ]
         source, *pieces = lax.optimization_barrier((source, *pieces))
-        for shift, piece in zip(shifts, pieces):
+        for (shift, start, count), piece in zip(exchanges, pieces):
             got = lax.ppermute(piece, "col", [(k, (k + shift) % cols) for k in range(cols)])
-            arrived.append(((here - shift) % cols * avals + start, got))
-        start += count
+            width = NI * NO if len(exchanges) == 1 and count == 1 else SUBLANES * NO
+            arrived.append(((here - shift) % cols * avals + start, got, width))
 
     panel = gather_amplitudes(amplitudes)
     rounded = lax.reduce_precision(panel, 8, 7)
@@ -159,8 +161,8 @@
     rows = cols * avals * NI
     out_shape = jax.ShapeDtypeStruct((cols * avals, NI * b_width * NO // LANES, LANES), jnp.float32)
     ladder = multiply(jnp.stack([here * avals, here]), blocks, th, tl, None, out_shape)
-    for at, got in arrived:
-        ladder = multiply(jnp.stack([at, jnp.zeros_like(at)]), got, th, tl, ladder, out_shape)
+    for at, got, width in arrived:
+        ladder = multiply(jnp.stack([at, jnp.zeros_like(at)]), got, th, tl, ladder, out_shape, width)
     ladder = ladder.reshape(rows // SUBLANES, b_width * NO // LANES, SUBLANES, LANES)
     return ladder.transpose(0, 2, 1, 3).reshape(rows, b_width * NO)
 

time: 864 us -> 836 us (0.968)
  waiting for transfers between devices: 392 us -> 477 us
  Pallas kernels: 264 us -> 195 us
  starting transfers between devices: 108 us -> 51.5 us
  local copies, waits for them, and re-layouts: 74.7 us -> 85.2 us
    ppermute x21 -> x15, waiting for transfers between devices: 271 us -> 361 us  [body(): lax.ppermute(piece, 'col', [(k, (k + shift) % cols) for k in range(cols)])]
    pallas_call x22 -> x16, Pallas kernels: 264 us -> 195 us  [multiply(): pl.pallas_call(functools.partial(ladder_kernel, group, width), out_shape=...]
    ppermute x21 -> x15, starting transfers between devices: 99.6 us -> 42.9 us  [body(): lax.ppermute(piece, 'col', [(k, (k + shift) % cols) for k in range(cols)])]
    dynamic_slice x7 -> x8, local copies, waits for them, and re-layouts: 27.7 us -> 30.8 us  [body(): lax.dynamic_slice(source, (start, (here + shift) % cols, 0, 0), (count, 1...]
  transfers between devices with their start and end apart: 26 -> 20, of which waited for: 11 -> 11; matrix products, arithmetic and copies ran while one was open for 11% -> 12% of each run, Pallas kernels for 30% -> 23%
where the time goes in v3:
time: 836 us; the launch traced here: 832 us
  waiting for transfers between devices  477 us (57%)
  Pallas kernels  195 us (23%)
  local copies, waits for them, and re-layouts  85.2 us (10%)
  starting transfers between devices  51.5 us (6%)
  other arithmetic  22.7 us (3%)
    ppermute x15, waiting for transfers between devices, body(): lax.ppermute(piece, 'col', [(k, (k + shift) % cols) for k in range(cols)])  361 us
    pallas_call x16, Pallas kernels, multiply(): pl.pallas_call(functools.partial(ladder_kernel, group, width), out_shape=...  195 us
    ppermute x5, waiting for transfers between devices, gather_over(): got = lax.ppermute(block, axis, [(k, k ^ mask) for k in range(size)])  116 us
    ppermute x15, starting transfers between devices, body(): lax.ppermute(piece, 'col', [(k, (k + shift) % cols) for k in range(cols)])  42.9 us
    dynamic_slice x8, local copies, waits for them, and re-layouts, body(): lax.dynamic_slice(source, (start, (here + shift) % cols, 0, 0), (count, 1...  30.8 us
  transfers between devices with their start and end apart: 20, of which 11 were waited for; matrix products, arithmetic and copies ran while one was open for 12% of the time, Pallas kernels for 23%

profile of v3, /device:TPU:25, one launch (start us, length us, event | category | flops | bytes accessed | tf_op | source)
XLA Modules:
  0.0 831.7 jit_solution(5020075830328176812)
XLA Ops:
  0.0 9.3 %collective-permute-done.1 = f32[1,64,1024]{2,1,0:T(8,128)S(1)} collective-permute-done((f32[1,64,1024]{2,1,0:T(8,128)}, f32[1,64,1024]{2,1,0:T(8,128)S(1)}, u32[]{:S(2)}, u32[]{:S(2)}) %collective-permute-start.1) | collective-permute-done | bytes 262176 | tf_op jit(solution)/shard_map/ppermute | solution.py:99
  10.3 4.0 collective-permute-start.2
  14.3 10.8 %collective-permute-done.2 = f32[2,64,1024]{2,1,0:T(8,128)S(1)} collective-permute-done((f32[2,64,1024]{2,1,0:T(8,128)S(1)}, f32[2,64,1024]{2,1,0:T(8,128)S(1)}, u32[]{:S(2)}, u32[]{:S(2)}) %collective-permute-start.2) | collective-permute-done | bytes 524320 | tf_op jit(solution)/shard_map/ppermute | solution.py:99
  26.4 2.2 collective-permute-start.3
  28.6 2.3 collective-permute-done.3
  33.7 45.9 %collective-permute-done.4 = f32[8,64,1024]{2,1,0:T(8,128)} collective-permute-done((f32[8,64,1024]{2,1,0:T(8,128)}, f32[8,64,1024]{2,1,0:T(8,128)}, u32[]{:S(2)}, u32[]{:S(2)}) %collective-permute-start.4) | collective-permute-done | bytes 2097184 | tf_op jit(solution)/shard_map/ppermute | solution.py:99
  79.7 4.2 pad_maximum_fusion
  85.1 3.7 constant_dynamic-slice_fusion.12
  91.8 3.7 constant_dynamic-slice_fusion.9
  95.5 2.0 collective-permute-start.16
  97.5 5.7 constant_dynamic-slice_fusion.6
  103.2 3.2 constant_dynamic-slice_fusion.3
  106.4 8.4 %constant_dynamic-slice_fusion.4 = (f32[8,1,128,1024]{3,2,1,0:T(8,128)}, f32[8,1,128,1024]{3,2,1,0:T(8,128)}) fusion(f32[16,4,128,1024]{3,2,1,0:T(8,128)} %bitcast.73, s32[]{:T(128)S(6)} %select_n.140, s32[]{:T(128)S(6)} %select_n.138), kind=kLoop, calls=%fused_computation.33 | loop fusion | bytes 16777224 | tf_op jit(solution)/shard_map/dynamic_slice | solution.py:148
  114.8 2.3 constant_dynamic-slice_fusion.2
  127.3 47.7 %collective-permute-done.5 = f32[16,64,1024]{2,1,0:T(8,128)} collective-permute-done((f32[16,64,1024]{2,1,0:T(8,128)}, f32[16,64,1024]{2,1,0:T(8,128)}, u32[]{:S(2)}, u32[]{:S(2)}) %collective-permute-start.5) | collective-permute-done | bytes 4194336 | tf_op jit(solution)/shard_map/ppermute | solution.py:99
  181.7 1.9 reverse_select_fusion.2
  183.7 1.9 reverse_select_fusion.1
  185.6 4.3 reverse_select_fusion
  189.8 13.3 %reshape_reshape_reshape.3 = f32[32,2,32,16,64]{4,3,2,1,0:T(8,128)} reshape(f32[1,2,4,4,64,1024]{5,4,3,2,1,0:T(8,128)} %reverse_select_fusion) | data formatting | bytes 16777216 | tf_op jit(solution)/shard_map/reshape;reshape;reshape | solution.py:119
  203.2 15.8 %copy.18 = f32[2,32,16,32,64]{4,3,2,1,0:T(8,128)} copy(f32[2,32,16,32,64]{4,2,3,0,1:T(8,128)} %bitcast.78) | data formatting | bytes 16777216 | tf_op jit(solution)/shard_map/transpose | solution.py:119
  219.0 14.8 %reshape.21 = f32[1024,2048]{1,0:T(8,128)} reshape(f32[2,32,16,32,64]{4,3,2,1,0:T(8,128)} %copy.18) | data formatting | bytes 16777216 | tf_op jit(solution)/shard_map/reshape | solution.py:120
  233.8 5.2 fusion
  239.2 2.4 collective-permute-start.13
  242.7 41.0 %shard_map.28.refs_0_ = f32[64,2048,128]{2,1,0:T(8,128)} custom-call(s32[2]{0:T(128)S(1)} %pad_add_fusion.15.at_ref, f32[16,4,128,1024]{3,2,1,0:T(8,128)} %bitcast.77, bf16[1024,2048]{1,0:T(8,128)(2,1)S(1)} %get-tuple-element.59.th_ref, bf16[1024,2048]{1,0:T(8,128)(2,1)S(1)} %get-tuple-element.58.tl_ref), custom_call_target="tpu_custom_call" | custom-call | flops 25769803776 | bytes 58720256 | tf_op jit(solution)/shard_map/pallas_call | solution.py:66
  283.7 7.8 shard_map.29.refs_0_
  291.8 6.6 shard_map.30.refs_0_
  298.4 6.6 shard_map.31.refs_0_
  305.0 3.2 collective-permute-start.11
  308.1 6.6 shard_map.32.refs_0_
  314.7 7.8 shard_map.33.refs_0_
  322.5 7.8 shard_map.34.refs_0_
  332.1 12.5 %shard_map.35.refs_0_ = f32[64,2048,128]{2,1,0:T(8,128)} custom-call(s32[2]{0:T(128)S(1)} %pad_add_fusion.6.at_ref, f32[4,1,128,1024]{3,2,1,0:T(8,128)} %collective-permute-done.13.v_ref, bf16[1024,2048]{1,0:T(8,128)(2,1)S(1)} %get-tuple-element.59.th_ref, bf16[1024,2048]{1,0:T(8,128)(2,1)S(1)} %get-tuple-element.58.tl_ref, ...), custom_call_target="tpu_custom_call", output_to_operand_aliasing={{}: (4, {})} | custom-call | flops 6442450944 | bytes 14680064 | tf_op jit(solution)/shard_map/pallas_call | solution.py:66
  344.6 98.1 %collective-permute-done.12.v_ref = f32[4,1,128,1024]{3,2,1,0:T(8,128)} collective-permute-done((f32[4,1,128,1024]{3,2,1,0:T(8,128)}, f32[4,1,128,1024]{3,2,1,0:T(8,128)}, u32[]{:S(2)}, u32[]{:S(2)}) %collective-permute-start.12) | collective-permute-done | bytes 2097184 | tf_op jit(solution)/shard_map/ppermute | solution.py:153
  442.7 25.1 %collective-permute-start.7 = (f32[2,1,128,1024]{3,2,1,0:T(8,128)}, f32[2,1,128,1024]{3,2,1,0:T(8,128)}, u32[]{:S(2)}, u32[]{:S(2)}) collective-permute-start(f32[2,1,128,1024]{3,2,1,0:T(8,128)} %constant_dynamic-slice_fusion.2), channel_id=1, source_target_pairs={{0,2},{1,3},{2,0},{3,1},{4,6},{5,7},{6,4},{7,5},{8,10},{9,11},{10,... | collective-permute-start | bytes 3145736 | tf_op jit(solution)/shard_map/ppermute | solution.py:153
  467.8 12.5 %shard_map.36.refs_0_ = f32[64,2048,128]{2,1,0:T(8,128)} custom-call(s32[2]{0:T(128)S(1)} %pad_add_fusion.7.at_ref, f32[4,1,128,1024]{3,2,1,0:T(8,128)} %collective-permute-done.12.v_ref, bf16[1024,2048]{1,0:T(8,128)(2,1)S(1)} %get-tuple-element.59.th_ref, bf16[1024,2048]{1,0:T(8,128)(2,1)S(1)} %get-tuple-element.58.tl_ref, ...), custom_call_target="tpu_custom_call", output_to_operand_aliasing={{}: (4, {})} | custom-call | flops 6442450944 | bytes 14680064 | tf_op jit(solution)/shard_map/pallas_call | solution.py:66
  480.3 234.5 %collective-permute-done.11.v_ref = f32[4,1,128,1024]{3,2,1,0:T(8,128)} collective-permute-done((f32[4,1,128,1024]{3,2,1,0:T(8,128)}, f32[4,1,128,1024]{3,2,1,0:T(8,128)}, u32[]{:S(2)}, u32[]{:S(2)}) %collective-permute-start.11) | collective-permute-done | bytes 2097184 | tf_op jit(solution)/shard_map/ppermute | solution.py:153
  714.8 12.5 %shard_map.37.refs_0_ = f32[64,2048,128]{2,1,0:T(8,128)} custom-call(s32[2]{0:T(128)S(1)} %pad_add_fusion.8.at_ref, f32[4,1,128,1024]{3,2,1,0:T(8,128)} %collective-permute-done.11.v_ref, bf16[1024,2048]{1,0:T(8,128)(2,1)S(1)} %get-tuple-element.59.th_ref, bf16[1024,2048]{1,0:T(8,128)(2,1)S(1)} %get-tuple-element.58.tl_ref, ...), custom_call_target="tpu_custom_call", output_to_operand_aliasing={{}: (4, {})} | custom-call | flops 6442450944 | bytes 14680064 | tf_op jit(solution)/shard_map/pallas_call | solution.py:66
  727.4 2.4 collective-permute-start
  729.7 22.0 %shard_map.38.refs_0_ = f32[64,2048,128]{2,1,0:T(8,128)} custom-call(s32[2]{0:T(128)S(1)} %pad_add_fusion.9.at_ref, f32[8,1,128,1024]{3,2,1,0:T(8,128)} %collective-permute-done.10.v_ref, bf16[1024,2048]{1,0:T(8,128)(2,1)S(1)} %get-tuple-element.59.th_ref, bf16[1024,2048]{1,0:T(8,128)(2,1)S(1)} %get-tuple-element.58.tl_ref, ...), custom_call_target="tpu_custom_call", output_to_operand_aliasing={{}: (4, {})} | custom-call | flops 12884901888 | bytes 20971520 | tf_op jit(solution)/shard_map/pallas_call | solution.py:66
  751.8 22.0 %shard_map.39.refs_0_ = f32[64,2048,128]{2,1,0:T(8,128)} custom-call(s32[2]{0:T(128)S(1)} %pad_add_fusion.10.at_ref, f32[8,1,128,1024]{3,2,1,0:T(8,128)} %collective-permute-done.9.v_ref, bf16[1024,2048]{1,0:T(8,128)(2,1)S(1)} %get-tuple-element.59.th_ref, bf16[1024,2048]{1,0:T(8,128)(2,1)S(1)} %get-tuple-element.58.tl_ref, ...), custom_call_target="tpu_custom_call", output_to_operand_aliasing={{}: (4, {})} | custom-call | flops 12884901888 | bytes 20971520 | tf_op jit(solution)/shard_map/pallas_call | solution.py:66
  773.8 8.5 %collective-permute-done.8.v_ref = f32[4,1,128,1024]{3,2,1,0:T(8,128)} collective-permute-done((f32[4,1,128,1024]{3,2,1,0:T(8,128)}, f32[4,1,128,1024]{3,2,1,0:T(8,128)}, u32[]{:S(2)}, u32[]{:S(2)}) %collective-permute-start.8) | collective-permute-done | bytes 2097184 | tf_op jit(solution)/shard_map/ppermute | solution.py:153
  782.2 12.5 %shard_map.40.refs_0_ = f32[64,2048,128]{2,1,0:T(8,128)} custom-call(s32[2]{0:T(128)S(1)} %pad_add_fusion.11.at_ref, f32[4,1,128,1024]{3,2,1,0:T(8,128)} %collective-permute-done.8.v_ref, bf16[1024,2048]{1,0:T(8,128)(2,1)S(1)} %get-tuple-element.59.th_ref, bf16[1024,2048]{1,0:T(8,128)(2,1)S(1)} %get-tuple-element.58.tl_ref, ...), custom_call_target="tpu_custom_call", output_to_operand_aliasing={{}: (4, {})} | custom-call | flops 6442450944 | bytes 14680064 | tf_op jit(solution)/shard_map/pallas_call | solution.py:66
  794.8 9.9 %collective-permute-done.7.v_ref = f32[2,1,128,1024]{3,2,1,0:T(8,128)} collective-permute-done((f32[2,1,128,1024]{3,2,1,0:T(8,128)}, f32[2,1,128,1024]{3,2,1,0:T(8,128)}, u32[]{:S(2)}, u32[]{:S(2)}) %collective-permute-start.7) | collective-permute-done | bytes 1048608 | tf_op jit(solution)/shard_map/ppermute | solution.py:153
  804.7 8.1 shard_map.41.refs_0_
  812.8 3.2 collective-permute-done.6.v_ref
  815.9 4.5 shard_map.42.refs_0_
  820.4 6.7 collective-permute-done.v_ref
  827.2 4.5 shard_map.43
  (58 shorter events, 29.7 us)
Async XLA Ops:
  0.0 9.3 %collective-permute-start.1 = (f32[1,64,1024]{2,1,0:T(8,128)}, f32[1,64,1024]{2,1,0:T(8,128)S(1)}, u32[]{:S(2)}, u32[]{:S(2)}) collective-permute-start(f32[1,64,1024]{2,1,0:T(8,128)} %bitcast.87), channel_id=1, source_target_pairs={{0,3},{1,2},{2,1},{3,0},{4,7},{5,6},{6,5},{7,4},{8,11},{9,10},{10,... | collective-permute-start | bytes 786440 | tf_op jit(solution)/shard_map/ppermute | solution.py:99
  10.3 14.7 %collective-permute-start.2 = (f32[2,64,1024]{2,1,0:T(8,128)S(1)}, f32[2,64,1024]{2,1,0:T(8,128)S(1)}, u32[]{:S(2)}, u32[]{:S(2)}) collective-permute-start(f32[2,64,1024]{2,1,0:T(8,128)S(1)} %pad_maximum_fusion.3), channel_id=1, source_target_pairs={{0,1},{1,0},{2,3},{3,2},{4,5},{5,4},{6,7},{7,6},{8,9},{9,8},{10,11... | collective-permute-start | bytes 1572872 | tf_op jit(solution)/shard_map/ppermute | solution.py:99
  26.4 62.4 %copy-start = (f32[1,2,2,1,64,1024]{5,4,2,1,3,0:T(8,128)}, f32[1,2,2,1,64,1024]{5,4,2,1,3,0:T(8,128)S(1)}, u32[]{:S(2)}) copy-start(f32[1,2,2,1,64,1024]{5,4,2,1,3,0:T(8,128)S(1)} %reverse_select_fusion.3) | copy-start | bytes 3145732
  26.4 4.5 collective-permute-start.3
  30.9 57.9 %copy-start.1 = (f32[4,64,1024]{2,1,0:T(8,128)}, f32[4,64,1024]{2,1,0:T(8,128)S(1)}, u32[]{:S(2)}) copy-start(f32[4,64,1024]{2,1,0:T(8,128)S(1)} %collective-permute-done.3) | copy-start | bytes 3145732
  32.5 47.1 %collective-permute-start.4 = (f32[8,64,1024]{2,1,0:T(8,128)}, f32[8,64,1024]{2,1,0:T(8,128)}, u32[]{:S(2)}, u32[]{:S(2)}) collective-permute-start(f32[8,64,1024]{2,1,0:T(8,128)} %pad_maximum_fusion.1), channel_id=1, source_target_pairs={{0,8},{4,12},{8,0},{12,4},{16,24},{20,28},{24,16},{28,20},{1,9},{5... | collective-permute-start | bytes 6291464 | tf_op jit(solution)/shard_map/ppermute | solution.py:99
  83.8 91.2 %collective-permute-start.5 = (f32[16,64,1024]{2,1,0:T(8,128)}, f32[16,64,1024]{2,1,0:T(8,128)}, u32[]{:S(2)}, u32[]{:S(2)}) collective-permute-start(f32[16,64,1024]{2,1,0:T(8,128)} %pad_maximum_fusion), channel_id=1, source_target_pairs={{0,16},{4,20},{8,24},{12,28},{16,0},{20,4},{24,8},{28,12},{1,17},{... | collective-permute-start | bytes 12582920 | tf_op jit(solution)/shard_map/ppermute | solution.py:99
  88.8 150.3 %collective-permute-start.19 = (f32[2,1,128,1024]{3,2,1,0:T(8,128)}, f32[2,1,128,1024]{3,2,1,0:T(8,128)}, u32[]{:S(2)}, u32[]{:S(2)}) collective-permute-start(f32[2,1,128,1024]{3,2,1,0:T(8,128)} %get-tuple-element.46), channel_id=1, source_target_pairs={{0,1},{1,2},{2,3},{3,0},{4,5},{5,6},{6,7},{7,4},{8,9},{9,10},{10,1... | collective-permute-start | bytes 3145736 | tf_op jit(solution)/shard_map/ppermute | solution.py:153
  90.0 149.2 %collective-permute-start.18 = (f32[2,1,128,1024]{3,2,1,0:T(8,128)}, f32[2,1,128,1024]{3,2,1,0:T(8,128)S(1)}, u32[]{:S(2)}, u32[]{:S(2)}) collective-permute-start(f32[2,1,128,1024]{3,2,1,0:T(8,128)} %get-tuple-element.45), channel_id=1, source_target_pairs={{0,3},{1,0},{2,1},{3,2},{4,7},{5,4},{6,5},{7,6},{8,11},{9,8},{10,9... | collective-permute-start | bytes 3145736 | tf_op jit(solution)/shard_map/ppermute | solution.py:153
  90.3 151.3 %collective-permute-start.17 = (f32[2,1,128,1024]{3,2,1,0:T(8,128)}, f32[2,1,128,1024]{3,2,1,0:T(8,128)S(1)}, u32[]{:S(2)}, u32[]{:S(2)}) collective-permute-start(f32[2,1,128,1024]{3,2,1,0:T(8,128)} %get-tuple-element.44), channel_id=1, source_target_pairs={{0,2},{1,3},{2,0},{3,1},{4,6},{5,7},{6,4},{7,5},{8,10},{9,11},{10,... | collective-permute-start | bytes 3145736 | tf_op jit(solution)/shard_map/ppermute | solution.py:153
  95.5 196.0 %collective-permute-start.16 = (f32[2,1,128,1024]{3,2,1,0:T(8,128)}, f32[2,1,128,1024]{3,2,1,0:T(8,128)S(1)}, u32[]{:S(2)}, u32[]{:S(2)}) collective-permute-start(f32[2,1,128,1024]{3,2,1,0:T(8,128)} %get-tuple-element.43), channel_id=1, source_target_pairs={{0,1},{1,2},{2,3},{3,0},{4,5},{5,6},{6,7},{7,4},{8,9},{9,10},{10,1... | collective-permute-start | bytes 3145736 | tf_op jit(solution)/shard_map/ppermute | solution.py:153
  175.1 123.3 %collective-permute-start.15 = (f32[2,1,128,1024]{3,2,1,0:T(8,128)}, f32[2,1,128,1024]{3,2,1,0:T(8,128)}, u32[]{:S(2)}, u32[]{:S(2)}) collective-permute-start(f32[2,1,128,1024]{3,2,1,0:T(8,128)} %get-tuple-element.42), channel_id=1, source_target_pairs={{0,3},{1,0},{2,1},{3,2},{4,7},{5,4},{6,5},{7,6},{8,11},{9,8},{10,9... | collective-permute-start | bytes 3145736 | tf_op jit(solution)/shard_map/ppermute | solution.py:153
  239.1 65.9 %collective-permute-start.14 = (f32[2,1,128,1024]{3,2,1,0:T(8,128)}, f32[2,1,128,1024]{3,2,1,0:T(8,128)}, u32[]{:S(2)}, u32[]{:S(2)}) collective-permute-start(f32[2,1,128,1024]{3,2,1,0:T(8,128)} %get-tuple-element.41), channel_id=1, source_target_pairs={{0,2},{1,3},{2,0},{3,1},{4,6},{5,7},{6,4},{7,5},{8,10},{9,11},{10,... | collective-permute-start | bytes 3145736 | tf_op jit(solution)/shard_map/ppermute | solution.py:153
  239.2 91.1 %collective-permute-start.13 = (f32[4,1,128,1024]{3,2,1,0:T(8,128)}, f32[4,1,128,1024]{3,2,1,0:T(8,128)}, u32[]{:S(2)}, u32[]{:S(2)}) collective-permute-start(f32[4,1,128,1024]{3,2,1,0:T(8,128)} %get-tuple-element.40), channel_id=1, source_target_pairs={{0,1},{1,2},{2,3},{3,0},{4,5},{5,6},{6,7},{7,4},{8,9},{9,10},{10,1... | collective-permute-start | bytes 6291464 | tf_op jit(solution)/shard_map/ppermute | solution.py:153
  241.6 485.8 %collective-permute-start.10 = (f32[8,1,128,1024]{3,2,1,0:T(8,128)}, f32[8,1,128,1024]{3,2,1,0:T(8,128)}, u32[]{:S(2)}, u32[]{:S(2)}) collective-permute-start(f32[8,1,128,1024]{3,2,1,0:T(8,128)} %get-tuple-element.37), channel_id=1, source_target_pairs={{0,1},{1,2},{2,3},{3,0},{4,5},{5,6},{6,7},{7,4},{8,9},{9,10},{10,1... | collective-permute-start | bytes 12582920 | tf_op jit(solution)/shard_map/ppermute | solution.py:153
  291.5 151.2 %collective-permute-start.12 = (f32[4,1,128,1024]{3,2,1,0:T(8,128)}, f32[4,1,128,1024]{3,2,1,0:T(8,128)}, u32[]{:S(2)}, u32[]{:S(2)}) collective-permute-start(f32[4,1,128,1024]{3,2,1,0:T(8,128)} %get-tuple-element.39), channel_id=1, source_target_pairs={{0,3},{1,0},{2,1},{3,2},{4,7},{5,4},{6,5},{7,6},{8,11},{9,8},{10,9... | collective-permute-start | bytes 6291464 | tf_op jit(solution)/shard_map/ppermute | solution.py:153
  298.4 453.4 %collective-permute-start.9 = (f32[8,1,128,1024]{3,2,1,0:T(8,128)}, f32[8,1,128,1024]{3,2,1,0:T(8,128)}, u32[]{:S(2)}, u32[]{:S(2)}) collective-permute-start(f32[8,1,128,1024]{3,2,1,0:T(8,128)} %get-tuple-element.36), channel_id=1, source_target_pairs={{0,3},{1,0},{2,1},{3,2},{4,7},{5,4},{6,5},{7,6},{8,11},{9,8},{10,9... | collective-permute-start | bytes 12582920 | tf_op jit(solution)/shard_map/ppermute | solution.py:153
  305.0 409.9 %collective-permute-start.11 = (f32[4,1,128,1024]{3,2,1,0:T(8,128)}, f32[4,1,128,1024]{3,2,1,0:T(8,128)}, u32[]{:S(2)}, u32[]{:S(2)}) collective-permute-start(f32[4,1,128,1024]{3,2,1,0:T(8,128)} %get-tuple-element.38), channel_id=1, source_target_pairs={{0,2},{1,3},{2,0},{3,1},{4,6},{5,7},{6,4},{7,5},{8,10},{9,11},{10,... | collective-permute-start | bytes 6291464 | tf_op jit(solution)/shard_map/ppermute | solution.py:153
  330.3 452.0 %collective-permute-start.8 = (f32[4,1,128,1024]{3,2,1,0:T(8,128)}, f32[4,1,128,1024]{3,2,1,0:T(8,128)}, u32[]{:S(2)}, u32[]{:S(2)}) collective-permute-start(f32[4,1,128,1024]{3,2,1,0:T(8,128)} %constant_dynamic-slice_fusion.3), channel_id=1, source_target_pairs={{0,2},{1,3},{2,0},{3,1},{4,6},{5,7},{6,4},{7,5},{8,10},{9,11},{10,... | collective-permute-start | bytes 6291464 | tf_op jit(solution)/shard_map/ppermute | solution.py:153
  442.7 362.0 %collective-permute-start.7 = (f32[2,1,128,1024]{3,2,1,0:T(8,128)}, f32[2,1,128,1024]{3,2,1,0:T(8,128)}, u32[]{:S(2)}, u32[]{:S(2)}) collective-permute-start(f32[2,1,128,1024]{3,2,1,0:T(8,128)} %constant_dynamic-slice_fusion.2), channel_id=1, source_target_pairs={{0,2},{1,3},{2,0},{3,1},{4,6},{5,7},{6,4},{7,5},{8,10},{9,11},{10,... | collective-permute-start | bytes 3145736 | tf_op jit(solution)/shard_map/ppermute | solution.py:153
  714.8 101.1 %collective-permute-start.6 = (f32[1,1,128,1024]{3,2,1,0:T(8,128)}, f32[1,1,128,1024]{3,2,1,0:T(8,128)}, u32[]{:S(2)}, u32[]{:S(2)}) collective-permute-start(f32[1,1,128,1024]{3,2,1,0:T(8,128)} %constant_dynamic-slice_fusion.1), channel_id=1, source_target_pairs={{0,2},{1,3},{2,0},{3,1},{4,6},{5,7},{6,4},{7,5},{8,10},{9,11},{10,... | collective-permute-start | bytes 1572872 | tf_op jit(solution)/shard_map/ppermute | solution.py:153
  727.4 99.8 %collective-permute-start = (f32[1,1,128,1024]{3,2,1,0:T(8,128)}, f32[1,1,128,1024]{3,2,1,0:T(8,128)}, u32[]{:S(2)}, u32[]{:S(2)}) collective-permute-start(f32[1,1,128,1024]{3,2,1,0:T(8,128)} %constant_dynamic-slice_fusion), channel_id=1, source_target_pairs={{0,2},{1,3},{2,0},{3,1},{4,6},{5,7},{6,4},{7,5},{8,10},{9,11},{10,... | collective-permute-start | bytes 1572872 | tf_op jit(solution)/shard_map/ppermute | solution.py:153

commit v4 on v3

--- a/solution.py
+++ b/solution.py
@@ -57,9 +57,10 @@
             step(n, pl.ds(pl.multiple_of(n * width, width), width))
 
 
-def multiply(at, integrals, th, tl, ladder, out_shape, width=SUBLANES * NO):
+def multiply(at, integrals, th, tl, ladder, out_shape):
     avals, _, b_width, depth = integrals.shape
     group = 2 if avals % 2 == 0 else 1
+    width = SUBLANES * NO
     aliased = ladder is not None
     spec = pl.BlockSpec((depth, NI * NO), lambda g, at: (0, 0), pipeline_mode=pl.Buffered(1))
     products = avals * b_width * depth * NI * NO
@@ -89,6 +90,62 @@
     )(at, integrals, th, tl, *([ladder] if aliased else []))
 
 
+def last_kernel(part, parts, at_ref, v_ref, th_ref, tl_ref, _, o_ref, vs_ref, part_ref, tile_ref, sems):
+    b_width, depth = v_ref.shape[2:]
+    half = b_width // 2
+    vs_ref[:b_width, :], vs_ref[b_width:, :] = split(v_ref[...].reshape(b_width, depth))
+    dot = functools.partial(jnp.dot, preferred_element_type=jnp.float32)
+    both = dot(vs_ref[...], th_ref[...])
+    acc = dot(vs_ref[:b_width, :], tl_ref[...]) + both[b_width:] + both[:b_width]
+    low_half = lax.broadcasted_iota(jnp.int32, (half, LANES), 1) < NO
+    copies = []
+    for pair in range(NI * NO // LANES):
+        part_ref[pair] = acc[:, pair * LANES : (pair + 1) * LANES]
+        even = part_ref[pair, pl.ds(0, half, stride=2), :]
+        odd = part_ref[pair, pl.ds(1, half, stride=2), :]
+        block, i = divmod(2 * pair, SUBLANES)
+        at = block * half * SUBLANES + i
+        tile_ref[pl.ds(at, half, stride=SUBLANES), :] = jnp.where(low_half, even, pltpu.roll(odd, NO, axis=1))
+        tile_ref[pl.ds(at + 1, half, stride=SUBLANES), :] = jnp.where(low_half, pltpu.roll(even, NO, axis=1), odd)
+        if i == SUBLANES - 2:
+            size = half * SUBLANES
+            copy = pltpu.make_async_copy(
+                tile_ref.at[pl.ds(block * size, size)],
+                o_ref.at[at_ref[0], pl.ds((block * parts + part) * size, size)],
+                sems.at[block],
+            )
+            copy.start()
+            copies.append(copy)
+    for copy in copies:
+        copy.wait()
+
+
+def multiply_last(at, part, parts, integrals, th, tl, ladder):
+    b_width, depth = integrals.shape[2:]
+    held = pl.BlockSpec(memory_space=pltpu.VMEM)
+    anywhere = pl.BlockSpec(memory_space=pl.ANY)
+    products = b_width * depth * NI * NO
+    return pl.pallas_call(
+        functools.partial(last_kernel, part, parts),
+        out_shape=jax.ShapeDtypeStruct(ladder.shape, ladder.dtype),
+        in_specs=[pl.BlockSpec(memory_space=pltpu.SMEM), held, held, held, anywhere],
+        out_specs=anywhere,
+        scratch_shapes=[
+            pltpu.VMEM((2 * b_width, depth), jnp.bfloat16),
+            pltpu.VMEM((NI * NO // LANES, b_width, LANES), jnp.float32),
+            pltpu.VMEM((NI * NO * b_width // LANES, LANES), jnp.float32),
+            pltpu.SemaphoreType.DMA((NI // SUBLANES,)),
+        ],
+        input_output_aliases={4: 0},
+        compiler_params=pltpu.CompilerParams(vmem_limit_bytes=24 << 20),
+        cost_estimate=pl.CostEstimate(
+            flops=6 * products,
+            bytes_accessed=4 * (integrals.size + b_width * NI * NO),
+            transcendentals=0,
+        ),
+    )(at.reshape(1), integrals, th, tl, ladder)
+
+
 def gather_over(axis, pieces, masks):
     size = lax.axis_size(axis)
     here = lax.axis_index(axis)
@@ -144,15 +201,21 @@
     arrived = []
     source = blocks
     for exchanges in rounds_of(avals, cols):
+        parts = 2 if len(exchanges) == 1 and exchanges[0][2] == 1 else 1
+        part_width = b_width // parts
+        exchanges = [exchange + (part,) for exchange in exchanges for part in range(parts)]
         pieces = [
-            lax.dynamic_slice(source, (start, (here + shift) % cols, 0, 0), (count, 1, b_width, depth))
-            for shift, start, count in exchanges
+            lax.dynamic_slice(
+                source,
+                (start, (here + shift) % cols, part * part_width, 0),
+                (count, 1, part_width, depth),
+            )
+            for shift, start, count, part in exchanges
         ]
         source, *pieces = lax.optimization_barrier((source, *pieces))
-        for (shift, start, count), piece in zip(exchanges, pieces):
+        for (shift, start, count, part), piece in zip(exchanges, pieces):
             got = lax.ppermute(piece, "col", [(k, (k + shift) % cols) for k in range(cols)])
-            width = NI * NO if len(exchanges) == 1 and count == 1 else SUBLANES * NO
-            arrived.append(((here - shift) % cols * avals + start, got, width))
+            arrived.append(((here - shift) % cols * avals + start, part, parts, got))
 
     panel = gather_amplitudes(amplitudes)
     rounded = lax.reduce_precision(panel, 8, 7)
@@ -161,8 +224,11 @@
     rows = cols * avals * NI
     out_shape = jax.ShapeDtypeStruct((cols * avals, NI * b_width * NO // LANES, LANES), jnp.float32)
     ladder = multiply(jnp.stack([here * avals, here]), blocks, th, tl, None, out_shape)
-    for at, got, width in arrived:
-        ladder = multiply(jnp.stack([at, jnp.zeros_like(at)]), got, th, tl, ladder, out_shape, width)
+    for at, part, parts, got in arrived:
+        if parts > 1:
+            ladder = multiply_last(at, part, parts, got, th, tl, ladder)
+        else:
+            ladder = multiply(jnp.stack([at, jnp.zeros_like(at)]), got, th, tl, ladder, out_shape)
     ladder = ladder.reshape(rows // SUBLANES, b_width * NO // LANES, SUBLANES, LANES)
     return ladder.transpose(0, 2, 1, 3).reshape(rows, b_width * NO)
 

time: 836 us -> 833 us (level)
    pallas_call x0 -> x4, Pallas kernels: none -> 12.6 us  [multiply_last(): pl.pallas_call(functools.partial(last_kernel, part, parts), out_shape=jax...]
    pallas_call x16 -> x14, Pallas kernels: 195 us -> 186 us  [multiply(): pl.pallas_call(functools.partial(ladder_kernel, group, width), out_shape=...]
    ppermute x15 -> x17, waiting for transfers between devices: 361 us -> 356 us  [body(): lax.ppermute(piece, 'col', [(k, (k + shift) % cols) for k in range(cols)])]
    ppermute x15 -> x17, starting transfers between devices: 42.9 us -> 42.9 us  [body(): lax.ppermute(piece, 'col', [(k, (k + shift) % cols) for k in range(cols)])]
  transfers between devices with their start and end apart: 20 -> 22, of which waited for: 11 -> 11; matrix products, arithmetic and copies ran while one was open for 12% -> 12% of each run, Pallas kernels for 23% -> 24%
where the time goes in v4:
time: 833 us; the launch traced here: 828 us
  waiting for transfers between devices  472 us (57%)
  Pallas kernels  199 us (24%)
  local copies, waits for them, and re-layouts  86.6 us (10%)
  starting transfers between devices  51.6 us (6%)
  other arithmetic  19.2 us (2%)
    ppermute x17, waiting for transfers between devices, body(): lax.ppermute(piece, 'col', [(k, (k + shift) % cols) for k in range(cols)])  356 us
    pallas_call x14, Pallas kernels, multiply(): pl.pallas_call(functools.partial(ladder_kernel, group, width), out_shape=...  186 us
    ppermute x5, waiting for transfers between devices, gather_over(): got = lax.ppermute(block, axis, [(k, k ^ mask) for k in range(size)])  116 us
    ppermute x17, starting transfers between devices, body(): lax.ppermute(piece, 'col', [(k, (k + shift) % cols) for k in range(cols)])  42.9 us
    dynamic_slice x8, local copies, waits for them, and re-layouts, body(): lax.dynamic_slice(source, (start, (here + shift) % cols, part * part_widt...  30.8 us
  transfers between devices with their start and end apart: 22, of which 11 were waited for; matrix products, arithmetic and copies ran while one was open for 12% of the time, Pallas kernels for 24%

profile of v4, /device:TPU:25, one launch (start us, length us, event | category | flops | bytes accessed | tf_op | source)
XLA Modules:
  0.0 828.4 jit_solution(12135592171155131880)
XLA Ops:
  0.0 9.3 %collective-permute-done.1 = f32[1,64,1024]{2,1,0:T(8,128)S(1)} collective-permute-done((f32[1,64,1024]{2,1,0:T(8,128)}, f32[1,64,1024]{2,1,0:T(8,128)S(1)}, u32[]{:S(2)}, u32[]{:S(2)}) %collective-permute-start.1) | collective-permute-done | bytes 262176 | tf_op jit(solution)/shard_map/ppermute | solution.py:156
  10.3 4.0 collective-permute-start.2
  14.3 10.8 %collective-permute-done.2 = f32[2,64,1024]{2,1,0:T(8,128)S(1)} collective-permute-done((f32[2,64,1024]{2,1,0:T(8,128)S(1)}, f32[2,64,1024]{2,1,0:T(8,128)S(1)}, u32[]{:S(2)}, u32[]{:S(2)}) %collective-permute-start.2) | collective-permute-done | bytes 524320 | tf_op jit(solution)/shard_map/ppermute | solution.py:156
  26.4 2.2 collective-permute-start.3
  28.6 2.3 collective-permute-done.3
  32.3 45.6 %collective-permute-done.4 = f32[8,64,1024]{2,1,0:T(8,128)S(1)} collective-permute-done((f32[8,64,1024]{2,1,0:T(8,128)S(1)}, f32[8,64,1024]{2,1,0:T(8,128)S(1)}, u32[]{:S(2)}, u32[]{:S(2)}) %collective-permute-start.4) | collective-permute-done | bytes 2097184 | tf_op jit(solution)/shard_map/ppermute | solution.py:156
  79.2 2.5 pad_maximum_fusion
  82.9 3.7 constant_dynamic-slice_fusion.14
  89.7 3.7 constant_dynamic-slice_fusion.11
  93.3 2.0 collective-permute-start.18
  95.3 5.8 constant_dynamic-slice_fusion.8
  101.1 3.2 constant_dynamic-slice_fusion.5
  104.3 8.4 %constant_dynamic-slice_fusion.6 = (f32[8,1,128,1024]{3,2,1,0:T(8,128)}, f32[8,1,128,1024]{3,2,1,0:T(8,128)}) fusion(f32[16,4,128,1024]{3,2,1,0:T(8,128)} %bitcast.73, s32[]{:T(128)S(6)} %select_n.150, s32[]{:T(128)S(6)} %select_n.148), kind=kLoop, calls=%fused_computation.35 | loop fusion | bytes 16777224 | tf_op jit(solution)/shard_map/dynamic_slice | solution.py:208
  112.7 2.3 constant_dynamic-slice_fusion.4
  125.0 47.9 %collective-permute-done.5 = f32[16,64,1024]{2,1,0:T(8,128)} collective-permute-done((f32[16,64,1024]{2,1,0:T(8,128)}, f32[16,64,1024]{2,1,0:T(8,128)}, u32[]{:S(2)}, u32[]{:S(2)}) %collective-permute-start.5) | collective-permute-done | bytes 4194336 | tf_op jit(solution)/shard_map/ppermute | solution.py:156
  183.4 4.2 reverse_select_fusion
  187.7 13.3 %reshape_reshape_reshape.3 = f32[32,2,32,16,64]{4,3,2,1,0:T(8,128)} reshape(f32[1,2,4,4,64,1024]{5,4,3,2,1,0:T(8,128)} %reverse_select_fusion) | data formatting | bytes 16777216 | tf_op jit(solution)/shard_map/reshape;reshape;reshape | solution.py:176
  201.0 15.8 %copy.20 = f32[2,32,16,32,64]{4,3,2,1,0:T(8,128)} copy(f32[2,32,16,32,64]{4,2,3,0,1:T(8,128)} %bitcast.78) | data formatting | bytes 16777216 | tf_op jit(solution)/shard_map/transpose | solution.py:176
  216.9 14.8 %reshape.30 = f32[1024,2048]{1,0:T(8,128)} reshape(f32[2,32,16,32,64]{4,3,2,1,0:T(8,128)} %copy.20) | data formatting | bytes 16777216 | tf_op jit(solution)/shard_map/reshape | solution.py:177
  231.7 5.2 fusion
  237.1 2.4 collective-permute-start.15
  240.5 41.0 %shard_map.28.refs_0_ = f32[64,2048,128]{2,1,0:T(8,128)} custom-call(s32[2]{0:T(128)S(1)} %pad_add_fusion.13.at_ref, f32[16,4,128,1024]{3,2,1,0:T(8,128)} %bitcast.77, bf16[1024,2048]{1,0:T(8,128)(2,1)S(1)} %get-tuple-element.67.th_ref, bf16[1024,2048]{1,0:T(8,128)(2,1)S(1)} %get-tuple-element.66.tl_ref), custom_call_target="tpu_custom_call" | custom-call | flops 25769803776 | bytes 58720256 | tf_op jit(solution)/shard_map/pallas_call | solution.py:67
  281.5 7.8 shard_map.29.refs_0_
  289.7 6.6 shard_map.30.refs_0_
  296.2 6.6 shard_map.31.refs_0_
  302.8 3.2 collective-permute-start.13
  306.0 6.6 shard_map.32.refs_0_
  312.6 7.8 shard_map.33.refs_0_
  320.4 7.8 shard_map.34.refs_0_
  329.9 12.5 %shard_map.35.refs_0_ = f32[64,2048,128]{2,1,0:T(8,128)} custom-call(s32[2]{0:T(128)S(1)} %pad_add_fusion.6.at_ref, f32[4,1,128,1024]{3,2,1,0:T(8,128)} %collective-permute-done.15.v_ref, bf16[1024,2048]{1,0:T(8,128)(2,1)S(1)} %get-tuple-element.67.th_ref, bf16[1024,2048]{1,0:T(8,128)(2,1)S(1)} %get-tuple-element.66.tl_ref, ...), custom_call_target="tpu_custom_call", output_to_operand_aliasing={{}: (4, {})} | custom-call | flops 6442450944 | bytes 14680064 | tf_op jit(solution)/shard_map/pallas_call | solution.py:67
  342.5 98.1 %collective-permute-done.14.v_ref = f32[4,1,128,1024]{3,2,1,0:T(8,128)} collective-permute-done((f32[4,1,128,1024]{3,2,1,0:T(8,128)}, f32[4,1,128,1024]{3,2,1,0:T(8,128)}, u32[]{:S(2)}, u32[]{:S(2)}) %collective-permute-start.14) | collective-permute-done | bytes 2097184 | tf_op jit(solution)/shard_map/ppermute | solution.py:217
  440.5 25.1 %collective-permute-start.9 = (f32[2,1,128,1024]{3,2,1,0:T(8,128)}, f32[2,1,128,1024]{3,2,1,0:T(8,128)}, u32[]{:S(2)}, u32[]{:S(2)}) collective-permute-start(f32[2,1,128,1024]{3,2,1,0:T(8,128)} %constant_dynamic-slice_fusion.4), channel_id=1, source_target_pairs={{0,2},{1,3},{2,0},{3,1},{4,6},{5,7},{6,4},{7,5},{8,10},{9,11},{10,... | collective-permute-start | bytes 3145736 | tf_op jit(solution)/shard_map/ppermute | solution.py:217
  465.6 12.5 %shard_map.36.refs_0_ = f32[64,2048,128]{2,1,0:T(8,128)} custom-call(s32[2]{0:T(128)S(1)} %pad_add_fusion.7.at_ref, f32[4,1,128,1024]{3,2,1,0:T(8,128)} %collective-permute-done.14.v_ref, bf16[1024,2048]{1,0:T(8,128)(2,1)S(1)} %get-tuple-element.67.th_ref, bf16[1024,2048]{1,0:T(8,128)(2,1)S(1)} %get-tuple-element.66.tl_ref, ...), custom_call_target="tpu_custom_call", output_to_operand_aliasing={{}: (4, {})} | custom-call | flops 6442450944 | bytes 14680064 | tf_op jit(solution)/shard_map/pallas_call | solution.py:67
  478.2 234.5 %collective-permute-done.13.v_ref = f32[4,1,128,1024]{3,2,1,0:T(8,128)} collective-permute-done((f32[4,1,128,1024]{3,2,1,0:T(8,128)}, f32[4,1,128,1024]{3,2,1,0:T(8,128)}, u32[]{:S(2)}, u32[]{:S(2)}) %collective-permute-start.13) | collective-permute-done | bytes 2097184 | tf_op jit(solution)/shard_map/ppermute | solution.py:217
  712.7 12.5 %shard_map.37.refs_0_ = f32[64,2048,128]{2,1,0:T(8,128)} custom-call(s32[2]{0:T(128)S(1)} %pad_add_fusion.8.at_ref, f32[4,1,128,1024]{3,2,1,0:T(8,128)} %collective-permute-done.13.v_ref, bf16[1024,2048]{1,0:T(8,128)(2,1)S(1)} %get-tuple-element.67.th_ref, bf16[1024,2048]{1,0:T(8,128)(2,1)S(1)} %get-tuple-element.66.tl_ref, ...), custom_call_target="tpu_custom_call", output_to_operand_aliasing={{}: (4, {})} | custom-call | flops 6442450944 | bytes 14680064 | tf_op jit(solution)/shard_map/pallas_call | solution.py:67
  725.2 2.4 collective-permute-start.7
  727.6 22.0 %shard_map.38.refs_0_ = f32[64,2048,128]{2,1,0:T(8,128)} custom-call(s32[2]{0:T(128)S(1)} %pad_add_fusion.9.at_ref, f32[8,1,128,1024]{3,2,1,0:T(8,128)} %collective-permute-done.12.v_ref, bf16[1024,2048]{1,0:T(8,128)(2,1)S(1)} %get-tuple-element.67.th_ref, bf16[1024,2048]{1,0:T(8,128)(2,1)S(1)} %get-tuple-element.66.tl_ref, ...), custom_call_target="tpu_custom_call", output_to_operand_aliasing={{}: (4, {})} | custom-call | flops 12884901888 | bytes 20971520 | tf_op jit(solution)/shard_map/pallas_call | solution.py:67
  749.6 22.0 %shard_map.39.refs_0_ = f32[64,2048,128]{2,1,0:T(8,128)} custom-call(s32[2]{0:T(128)S(1)} %pad_add_fusion.10.at_ref, f32[8,1,128,1024]{3,2,1,0:T(8,128)} %collective-permute-done.11.v_ref, bf16[1024,2048]{1,0:T(8,128)(2,1)S(1)} %get-tuple-element.67.th_ref, bf16[1024,2048]{1,0:T(8,128)(2,1)S(1)} %get-tuple-element.66.tl_ref, ...), custom_call_target="tpu_custom_call", output_to_operand_aliasing={{}: (4, {})} | custom-call | flops 12884901888 | bytes 20971520 | tf_op jit(solution)/shard_map/pallas_call | solution.py:67
  771.6 2.9 collective-permute-done.10.v_ref
  774.5 12.5 %shard_map.40.refs_0_ = f32[64,2048,128]{2,1,0:T(8,128)} custom-call(s32[2]{0:T(128)S(1)} %pad_add_fusion.11.at_ref, f32[4,1,128,1024]{3,2,1,0:T(8,128)} %collective-permute-done.10.v_ref, bf16[1024,2048]{1,0:T(8,128)(2,1)S(1)} %get-tuple-element.67.th_ref, bf16[1024,2048]{1,0:T(8,128)(2,1)S(1)} %get-tuple-element.66.tl_ref, ...), custom_call_target="tpu_custom_call", output_to_operand_aliasing={{}: (4, {})} | custom-call | flops 6442450944 | bytes 14680064 | tf_op jit(solution)/shard_map/pallas_call | solution.py:67
  787.0 15.5 %collective-permute-done.9.v_ref = f32[2,1,128,1024]{3,2,1,0:T(8,128)} collective-permute-done((f32[2,1,128,1024]{3,2,1,0:T(8,128)}, f32[2,1,128,1024]{3,2,1,0:T(8,128)}, u32[]{:S(2)}, u32[]{:S(2)}) %collective-permute-start.9) | collective-permute-done | bytes 1048608 | tf_op jit(solution)/shard_map/ppermute | solution.py:217
  802.6 8.0 shard_map.41._
  810.6 3.2 shard_map.42._
  813.8 3.2 shard_map.43._
  817.0 2.4 collective-permute-done.6.v_ref
  819.4 3.2 shard_map.44._
  822.6 2.4 collective-permute-done.v_ref
  825.0 3.2 shard_map.45
  (64 shorter events, 33.3 us)
Async XLA Ops:
  0.0 9.3 %collective-permute-start.1 = (f32[1,64,1024]{2,1,0:T(8,128)}, f32[1,64,1024]{2,1,0:T(8,128)S(1)}, u32[]{:S(2)}, u32[]{:S(2)}) collective-permute-start(f32[1,64,1024]{2,1,0:T(8,128)} %bitcast.87), channel_id=1, source_target_pairs={{0,3},{1,2},{2,1},{3,0},{4,7},{5,6},{6,5},{7,4},{8,11},{9,10},{10,... | collective-permute-start | bytes 786440 | tf_op jit(solution)/shard_map/ppermute | solution.py:156
  10.3 14.7 %collective-permute-start.2 = (f32[2,64,1024]{2,1,0:T(8,128)S(1)}, f32[2,64,1024]{2,1,0:T(8,128)S(1)}, u32[]{:S(2)}, u32[]{:S(2)}) collective-permute-start(f32[2,64,1024]{2,1,0:T(8,128)S(1)} %pad_maximum_fusion.3), channel_id=1, source_target_pairs={{0,1},{1,0},{2,3},{3,2},{4,5},{5,4},{6,7},{7,6},{8,9},{9,8},{10,11... | collective-permute-start | bytes 1572872 | tf_op jit(solution)/shard_map/ppermute | solution.py:156
  26.4 60.3 %copy-start = (f32[1,2,2,1,64,1024]{5,4,2,1,3,0:T(8,128)}, f32[1,2,2,1,64,1024]{5,4,2,1,3,0:T(8,128)S(1)}, u32[]{:S(2)}) copy-start(f32[1,2,2,1,64,1024]{5,4,2,1,3,0:T(8,128)S(1)} %reverse_select_fusion.3) | copy-start | bytes 3145732
  26.4 4.5 collective-permute-start.3
  30.9 55.8 %copy-start.1 = (f32[4,64,1024]{2,1,0:T(8,128)}, f32[4,64,1024]{2,1,0:T(8,128)S(1)}, u32[]{:S(2)}) copy-start(f32[4,64,1024]{2,1,0:T(8,128)S(1)} %collective-permute-done.3) | copy-start | bytes 3145732
  31.0 46.9 %collective-permute-start.4 = (f32[8,64,1024]{2,1,0:T(8,128)S(1)}, f32[8,64,1024]{2,1,0:T(8,128)S(1)}, u32[]{:S(2)}, u32[]{:S(2)}) collective-permute-start(f32[8,64,1024]{2,1,0:T(8,128)S(1)} %pad_maximum_fusion.1), channel_id=1, source_target_pairs={{0,8},{4,12},{8,0},{12,4},{16,24},{20,28},{24,16},{28,20},{1,9},{5... | collective-permute-start | bytes 6291464 | tf_op jit(solution)/shard_map/ppermute | solution.py:156
  77.9 1.4 copy-start.2
  81.7 91.2 %collective-permute-start.5 = (f32[16,64,1024]{2,1,0:T(8,128)}, f32[16,64,1024]{2,1,0:T(8,128)}, u32[]{:S(2)}, u32[]{:S(2)}) collective-permute-start(f32[16,64,1024]{2,1,0:T(8,128)} %pad_maximum_fusion), channel_id=1, source_target_pairs={{0,16},{4,20},{8,24},{12,28},{16,0},{20,4},{24,8},{28,12},{1,17},{... | collective-permute-start | bytes 12582920 | tf_op jit(solution)/shard_map/ppermute | solution.py:156
  86.7 150.3 %collective-permute-start.21 = (f32[2,1,128,1024]{3,2,1,0:T(8,128)}, f32[2,1,128,1024]{3,2,1,0:T(8,128)}, u32[]{:S(2)}, u32[]{:S(2)}) collective-permute-start(f32[2,1,128,1024]{3,2,1,0:T(8,128)} %get-tuple-element.50), channel_id=1, source_target_pairs={{0,1},{1,2},{2,3},{3,0},{4,5},{5,6},{6,7},{7,4},{8,9},{9,10},{10,1... | collective-permute-start | bytes 3145736 | tf_op jit(solution)/shard_map/ppermute | solution.py:217
  87.9 149.2 %collective-permute-start.20 = (f32[2,1,128,1024]{3,2,1,0:T(8,128)}, f32[2,1,128,1024]{3,2,1,0:T(8,128)S(1)}, u32[]{:S(2)}, u32[]{:S(2)}) collective-permute-start(f32[2,1,128,1024]{3,2,1,0:T(8,128)} %get-tuple-element.49), channel_id=1, source_target_pairs={{0,3},{1,0},{2,1},{3,2},{4,7},{5,4},{6,5},{7,6},{8,11},{9,8},{10,9... | collective-permute-start | bytes 3145736 | tf_op jit(solution)/shard_map/ppermute | solution.py:217
  88.2 151.3 %collective-permute-start.19 = (f32[2,1,128,1024]{3,2,1,0:T(8,128)}, f32[2,1,128,1024]{3,2,1,0:T(8,128)S(1)}, u32[]{:S(2)}, u32[]{:S(2)}) collective-permute-start(f32[2,1,128,1024]{3,2,1,0:T(8,128)} %get-tuple-element.48), channel_id=1, source_target_pairs={{0,2},{1,3},{2,0},{3,1},{4,6},{5,7},{6,4},{7,5},{8,10},{9,11},{10,... | collective-permute-start | bytes 3145736 | tf_op jit(solution)/shard_map/ppermute | solution.py:217
  93.3 196.0 %collective-permute-start.18 = (f32[2,1,128,1024]{3,2,1,0:T(8,128)}, f32[2,1,128,1024]{3,2,1,0:T(8,128)S(1)}, u32[]{:S(2)}, u32[]{:S(2)}) collective-permute-start(f32[2,1,128,1024]{3,2,1,0:T(8,128)} %get-tuple-element.47), channel_id=1, source_target_pairs={{0,1},{1,2},{2,3},{3,0},{4,5},{5,6},{6,7},{7,4},{8,9},{9,10},{10,1... | collective-permute-start | bytes 3145736 | tf_op jit(solution)/shard_map/ppermute | solution.py:217
  172.9 123.3 %collective-permute-start.17 = (f32[2,1,128,1024]{3,2,1,0:T(8,128)}, f32[2,1,128,1024]{3,2,1,0:T(8,128)}, u32[]{:S(2)}, u32[]{:S(2)}) collective-permute-start(f32[2,1,128,1024]{3,2,1,0:T(8,128)} %get-tuple-element.46), channel_id=1, source_target_pairs={{0,3},{1,0},{2,1},{3,2},{4,7},{5,4},{6,5},{7,6},{8,11},{9,8},{10,9... | collective-permute-start | bytes 3145736 | tf_op jit(solution)/shard_map/ppermute | solution.py:217
  236.9 65.9 %collective-permute-start.16 = (f32[2,1,128,1024]{3,2,1,0:T(8,128)}, f32[2,1,128,1024]{3,2,1,0:T(8,128)}, u32[]{:S(2)}, u32[]{:S(2)}) collective-permute-start(f32[2,1,128,1024]{3,2,1,0:T(8,128)} %get-tuple-element.45), channel_id=1, source_target_pairs={{0,2},{1,3},{2,0},{3,1},{4,6},{5,7},{6,4},{7,5},{8,10},{9,11},{10,... | collective-permute-start | bytes 3145736 | tf_op jit(solution)/shard_map/ppermute | solution.py:217
  237.1 91.1 %collective-permute-start.15 = (f32[4,1,128,1024]{3,2,1,0:T(8,128)}, f32[4,1,128,1024]{3,2,1,0:T(8,128)}, u32[]{:S(2)}, u32[]{:S(2)}) collective-permute-start(f32[4,1,128,1024]{3,2,1,0:T(8,128)} %get-tuple-element.44), channel_id=1, source_target_pairs={{0,1},{1,2},{2,3},{3,0},{4,5},{5,6},{6,7},{7,4},{8,9},{9,10},{10,1... | collective-permute-start | bytes 6291464 | tf_op jit(solution)/shard_map/ppermute | solution.py:217
  239.4 485.8 %collective-permute-start.12 = (f32[8,1,128,1024]{3,2,1,0:T(8,128)}, f32[8,1,128,1024]{3,2,1,0:T(8,128)}, u32[]{:S(2)}, u32[]{:S(2)}) collective-permute-start(f32[8,1,128,1024]{3,2,1,0:T(8,128)} %get-tuple-element.41), channel_id=1, source_target_pairs={{0,1},{1,2},{2,3},{3,0},{4,5},{5,6},{6,7},{7,4},{8,9},{9,10},{10,1... | collective-permute-start | bytes 12582920 | tf_op jit(solution)/shard_map/ppermute | solution.py:217
  289.3 151.2 %collective-permute-start.14 = (f32[4,1,128,1024]{3,2,1,0:T(8,128)}, f32[4,1,128,1024]{3,2,1,0:T(8,128)}, u32[]{:S(2)}, u32[]{:S(2)}) collective-permute-start(f32[4,1,128,1024]{3,2,1,0:T(8,128)} %get-tuple-element.43), channel_id=1, source_target_pairs={{0,3},{1,0},{2,1},{3,2},{4,7},{5,4},{6,5},{7,6},{8,11},{9,8},{10,9... | collective-permute-start | bytes 6291464 | tf_op jit(solution)/shard_map/ppermute | solution.py:217
  296.2 453.4 %collective-permute-start.11 = (f32[8,1,128,1024]{3,2,1,0:T(8,128)}, f32[8,1,128,1024]{3,2,1,0:T(8,128)}, u32[]{:S(2)}, u32[]{:S(2)}) collective-permute-start(f32[8,1,128,1024]{3,2,1,0:T(8,128)} %get-tuple-element.40), channel_id=1, source_target_pairs={{0,3},{1,0},{2,1},{3,2},{4,7},{5,4},{6,5},{7,6},{8,11},{9,8},{10,9... | collective-permute-start | bytes 12582920 | tf_op jit(solution)/shard_map/ppermute | solution.py:217
  302.8 409.9 %collective-permute-start.13 = (f32[4,1,128,1024]{3,2,1,0:T(8,128)}, f32[4,1,128,1024]{3,2,1,0:T(8,128)}, u32[]{:S(2)}, u32[]{:S(2)}) collective-permute-start(f32[4,1,128,1024]{3,2,1,0:T(8,128)} %get-tuple-element.42), channel_id=1, source_target_pairs={{0,2},{1,3},{2,0},{3,1},{4,6},{5,7},{6,4},{7,5},{8,10},{9,11},{10,... | collective-permute-start | bytes 6291464 | tf_op jit(solution)/shard_map/ppermute | solution.py:217
  328.1 446.3 %collective-permute-start.10 = (f32[4,1,128,1024]{3,2,1,0:T(8,128)}, f32[4,1,128,1024]{3,2,1,0:T(8,128)}, u32[]{:S(2)}, u32[]{:S(2)}) collective-permute-start(f32[4,1,128,1024]{3,2,1,0:T(8,128)} %constant_dynamic-slice_fusion.5), channel_id=1, source_target_pairs={{0,2},{1,3},{2,0},{3,1},{4,6},{5,7},{6,4},{7,5},{8,10},{9,11},{10,... | collective-permute-start | bytes 6291464 | tf_op jit(solution)/shard_map/ppermute | solution.py:217
  440.5 362.0 %collective-permute-start.9 = (f32[2,1,128,1024]{3,2,1,0:T(8,128)}, f32[2,1,128,1024]{3,2,1,0:T(8,128)}, u32[]{:S(2)}, u32[]{:S(2)}) collective-permute-start(f32[2,1,128,1024]{3,2,1,0:T(8,128)} %constant_dynamic-slice_fusion.4), channel_id=1, source_target_pairs={{0,2},{1,3},{2,0},{3,1},{4,6},{5,7},{6,4},{7,5},{8,10},{9,11},{10,... | collective-permute-start | bytes 3145736 | tf_op jit(solution)/shard_map/ppermute | solution.py:217
  712.7 97.9 %collective-permute-start.8 = (f32[1,1,64,1024]{3,2,1,0:T(8,128)}, f32[1,1,64,1024]{3,2,1,0:T(8,128)}, u32[]{:S(2)}, u32[]{:S(2)}) collective-permute-start(f32[1,1,64,1024]{3,2,1,0:T(8,128)} %get-tuple-element.37), channel_id=1, source_target_pairs={{0,2},{1,3},{2,0},{3,1},{4,6},{5,7},{6,4},{7,5},{8,10},{9,11},{10,... | collective-permute-start | bytes 786440 | tf_op jit(solution)/shard_map/ppermute | solution.py:217
  725.2 88.6 %collective-permute-start.7 = (f32[1,1,64,1024]{3,2,1,0:T(8,128)}, f32[1,1,64,1024]{3,2,1,0:T(8,128)}, u32[]{:S(2)}, u32[]{:S(2)}) collective-permute-start(f32[1,1,64,1024]{3,2,1,0:T(8,128)} %get-tuple-element.36), channel_id=1, source_target_pairs={{0,2},{1,3},{2,0},{3,1},{4,6},{5,7},{6,4},{7,5},{8,10},{9,11},{10,... | collective-permute-start | bytes 786440 | tf_op jit(solution)/shard_map/ppermute | solution.py:217
  749.6 69.8 %collective-permute-start.6 = (f32[1,1,64,1024]{3,2,1,0:T(8,128)}, f32[1,1,64,1024]{3,2,1,0:T(8,128)}, u32[]{:S(2)}, u32[]{:S(2)}) collective-permute-start(f32[1,1,64,1024]{3,2,1,0:T(8,128)} %get-tuple-element.35), channel_id=1, source_target_pairs={{0,2},{1,3},{2,0},{3,1},{4,6},{5,7},{6,4},{7,5},{8,10},{9,11},{10,... | collective-permute-start | bytes 786440 | tf_op jit(solution)/shard_map/ppermute | solution.py:217
  774.5 50.6 %collective-permute-start = (f32[1,1,64,1024]{3,2,1,0:T(8,128)}, f32[1,1,64,1024]{3,2,1,0:T(8,128)}, u32[]{:S(2)}, u32[]{:S(2)}) collective-permute-start(f32[1,1,64,1024]{3,2,1,0:T(8,128)} %get-tuple-element.34), channel_id=1, source_target_pairs={{0,2},{1,3},{2,0},{3,1},{4,6},{5,7},{6,4},{7,5},{8,10},{9,11},{10,... | collective-permute-start | bytes 786440 | tf_op jit(solution)/shard_map/ppermute | solution.py:217

commit v5 on v4

--- a/solution.py
+++ b/solution.py
@@ -90,17 +90,27 @@
     )(at, integrals, th, tl, *([ladder] if aliased else []))
 
 
-def last_kernel(part, parts, at_ref, v_ref, th_ref, tl_ref, _, o_ref, vs_ref, part_ref, tile_ref, sems):
+def part_products(part, v_ref, th_ref, tl_ref, vs_ref):
     b_width, depth = v_ref.shape[2:]
-    half = b_width // 2
     vs_ref[:b_width, :], vs_ref[b_width:, :] = split(v_ref[...].reshape(b_width, depth))
+    rows = slice(part * depth, (part + 1) * depth)
     dot = functools.partial(jnp.dot, preferred_element_type=jnp.float32)
-    both = dot(vs_ref[...], th_ref[...])
-    acc = dot(vs_ref[:b_width, :], tl_ref[...]) + both[b_width:] + both[:b_width]
+    both = dot(vs_ref[...], th_ref[rows, :])
+    return dot(vs_ref[:b_width, :], tl_ref[rows, :]) + both[b_width:] + both[:b_width]
+
+
+def first_kernel(v_ref, th_ref, tl_ref, _, sum_ref, __, vs_ref):
+    sum_ref[...] = part_products(0, v_ref, th_ref, tl_ref, vs_ref)
+
+
+def last_kernel(at_ref, v_ref, th_ref, tl_ref, sum_ref, _, o_ref, vs_ref, part_ref, tile_ref, sems):
+    half = v_ref.shape[2] // 2
+    acc = part_products(1, v_ref, th_ref, tl_ref, vs_ref)
     low_half = lax.broadcasted_iota(jnp.int32, (half, LANES), 1) < NO
     copies = []
     for pair in range(NI * NO // LANES):
-        part_ref[pair] = acc[:, pair * LANES : (pair + 1) * LANES]
+        columns = slice(pair * LANES, (pair + 1) * LANES)
+        part_ref[pair] = acc[:, columns] + sum_ref[:, columns]
         even = part_ref[pair, pl.ds(0, half, stride=2), :]
         odd = part_ref[pair, pl.ds(1, half, stride=2), :]
         block, i = divmod(2 * pair, SUBLANES)
@@ -108,42 +118,51 @@
         tile_ref[pl.ds(at, half, stride=SUBLANES), :] = jnp.where(low_half, even, pltpu.roll(odd, NO, axis=1))
         tile_ref[pl.ds(at + 1, half, stride=SUBLANES), :] = jnp.where(low_half, pltpu.roll(even, NO, axis=1), odd)
         if i == SUBLANES - 2:
-            size = half * SUBLANES
-            copy = pltpu.make_async_copy(
-                tile_ref.at[pl.ds(block * size, size)],
-                o_ref.at[at_ref[0], pl.ds((block * parts + part) * size, size)],
-                sems.at[block],
-            )
+            place = pl.ds(block * half * SUBLANES, half * SUBLANES)
+            copy = pltpu.make_async_copy(tile_ref.at[place], o_ref.at[at_ref[0], place], sems.at[block])
             copy.start()
             copies.append(copy)
     for copy in copies:
         copy.wait()
 
 
-def multiply_last(at, part, parts, integrals, th, tl, ladder):
-    b_width, depth = integrals.shape[2:]
+def multiply_last(at, parts, th, tl, ladder):
+    b_width, depth = parts[0].shape[2:]
     held = pl.BlockSpec(memory_space=pltpu.VMEM)
     anywhere = pl.BlockSpec(memory_space=pl.ANY)
-    products = b_width * depth * NI * NO
+    cost = pl.CostEstimate(
+        flops=6 * b_width * depth * NI * NO,
+        bytes_accessed=4 * b_width * (depth + NI * NO),
+        transcendentals=0,
+    )
+    stacked = pltpu.VMEM((2 * b_width, depth), jnp.bfloat16)
+    params = pltpu.CompilerParams(vmem_limit_bytes=24 << 20)
+    written = jax.ShapeDtypeStruct(ladder.shape, ladder.dtype)
+    sums, ladder = pl.pallas_call(
+        first_kernel,
+        out_shape=(jax.ShapeDtypeStruct((b_width, NI * NO), jnp.float32), written),
+        in_specs=[held, held, held, anywhere],
+        out_specs=(held, anywhere),
+        scratch_shapes=[stacked],
+        input_output_aliases={3: 1},
+        compiler_params=params,
+        cost_estimate=cost,
+    )(parts[0], th, tl, ladder)
     return pl.pallas_call(
-        functools.partial(last_kernel, part, parts),
-        out_shape=jax.ShapeDtypeStruct(ladder.shape, ladder.dtype),
-        in_specs=[pl.BlockSpec(memory_space=pltpu.SMEM), held, held, held, anywhere],
+        last_kernel,
+        out_shape=written,
+        in_specs=[pl.BlockSpec(memory_space=pltpu.SMEM), held, held, held, held, anywhere],
         out_specs=anywhere,
         scratch_shapes=[
-            pltpu.VMEM((2 * b_width, depth), jnp.bfloat16),
+            stacked,
             pltpu.VMEM((NI * NO // LANES, b_width, LANES), jnp.float32),
             pltpu.VMEM((NI * NO * b_width // LANES, LANES), jnp.float32),
             pltpu.SemaphoreType.DMA((NI // SUBLANES,)),
         ],
-        input_output_aliases={4: 0},
-        compiler_params=pltpu.CompilerParams(vmem_limit_bytes=24 << 20),
-        cost_estimate=pl.CostEstimate(
-            flops=6 * products,
-            bytes_accessed=4 * (integrals.size + b_width * NI * NO),
-            transcendentals=0,
-        ),
-    )(at.reshape(1), integrals, th, tl, ladder)
+        input_output_aliases={5: 0},
+        compiler_params=params,
+        cost_estimate=cost,
+    )(at.reshape(1), parts[1], th, tl, sums, ladder)
 
 
 def gather_over(axis, pieces, masks):
@@ -202,20 +221,23 @@
     source = blocks
     for exchanges in rounds_of(avals, cols):
         parts = 2 if len(exchanges) == 1 and exchanges[0][2] == 1 else 1
-        part_width = b_width // parts
-        exchanges = [exchange + (part,) for exchange in exchanges for part in range(parts)]
+        width = depth // parts
+        sent = [exchange + (part,) for exchange in exchanges for part in range(parts)]
         pieces = [
             lax.dynamic_slice(
                 source,
-                (start, (here + shift) % cols, part * part_width, 0),
-                (count, 1, part_width, depth),
+                (start, (here + shift) % cols, 0, part * width),
+                (count, 1, b_width, width),
             )
-            for shift, start, count, part in exchanges
+            for shift, start, count, part in sent
         ]
         source, *pieces = lax.optimization_barrier((source, *pieces))
-        for (shift, start, count, part), piece in zip(exchanges, pieces):
-            got = lax.ppermute(piece, "col", [(k, (k + shift) % cols) for k in range(cols)])
-            arrived.append(((here - shift) % cols * avals + start, part, parts, got))
+        got = [
+            lax.ppermute(piece, "col", [(k, (k + shift) % cols) for k in range(cols)])
+            for (shift, *_), piece in zip(sent, pieces)
+        ]
+        for n, (shift, start, _) in enumerate(exchanges):
+            arrived.append(((here - shift) % cols * avals + start, got[n * parts : (n + 1) * parts]))
 
     panel = gather_amplitudes(amplitudes)
     rounded = lax.reduce_precision(panel, 8, 7)
@@ -224,11 +246,11 @@
     rows = cols * avals * NI
     out_shape = jax.ShapeDtypeStruct((cols * avals, NI * b_width * NO // LANES, LANES), jnp.float32)
     ladder = multiply(jnp.stack([here * avals, here]), blocks, th, tl, None, out_shape)
-    for at, part, parts, got in arrived:
-        if parts > 1:
-            ladder = multiply_last(at, part, parts, got, th, tl, ladder)
+    for at, parts in arrived:
+        if len(parts) > 1:
+            ladder = multiply_last(at, parts, th, tl, ladder)
         else:
-            ladder = multiply(jnp.stack([at, jnp.zeros_like(at)]), got, th, tl, ladder, out_shape)
+            ladder = multiply(jnp.stack([at, jnp.zeros_like(at)]), parts[0], th, tl, ladder, out_shape)
     ladder = ladder.reshape(rows // SUBLANES, b_width * NO // LANES, SUBLANES, LANES)
     return ladder.transpose(0, 2, 1, 3).reshape(rows, b_width * NO)
 

time: 833 us -> 832 us (level)
  transfers between devices with their start and end apart: 22 -> 22, of which waited for: 11 -> 12; matrix products, arithmetic and copies ran while one was open for 12% -> 12% of each run, Pallas kernels for 24% -> 23%
where the time goes in v5:
time: 832 us; the launch traced here: 828 us
  waiting for transfers between devices  475 us (57%)
  Pallas kernels  196 us (24%)
  local copies, waits for them, and re-layouts  86.5 us (10%)
  starting transfers between devices  51.6 us (6%)
  other arithmetic  19.2 us (2%)
    ppermute x17, waiting for transfers between devices, body(): lax.ppermute(piece, 'col', [(k, (k + shift) % cols) for k in range(cols)])  359 us
    pallas_call x14, Pallas kernels, multiply(): pl.pallas_call(functools.partial(ladder_kernel, group, width), out_shape=...  186 us
    ppermute x5, waiting for transfers between devices, gather_over(): got = lax.ppermute(block, axis, [(k, k ^ mask) for k in range(size)])  116 us
    ppermute x17, starting transfers between devices, body(): lax.ppermute(piece, 'col', [(k, (k + shift) % cols) for k in range(cols)])  42.9 us
    dynamic_slice x8, local copies, waits for them, and re-layouts, body(): lax.dynamic_slice(source, (start, (here + shift) % cols, 0, part * width)...  30.7 us
  transfers between devices with their start and end apart: 22, of which 12 were waited for; matrix products, arithmetic and copies ran while one was open for 12% of the time, Pallas kernels for 23%

profile of v5, /device:TPU:25, one launch (start us, length us, event | category | flops | bytes accessed | tf_op | source)
XLA Modules:
  0.0 828.1 jit_solution(480717895986973054)
XLA Ops:
  0.0 9.3 %collective-permute-done.1 = f32[1,64,1024]{2,1,0:T(8,128)S(1)} collective-permute-done((f32[1,64,1024]{2,1,0:T(8,128)}, f32[1,64,1024]{2,1,0:T(8,128)S(1)}, u32[]{:S(2)}, u32[]{:S(2)}) %collective-permute-start.1) | collective-permute-done | bytes 262176 | tf_op jit(solution)/shard_map/ppermute | solution.py:175
  10.3 4.0 collective-permute-start.2
  14.3 10.8 %collective-permute-done.2 = f32[2,64,1024]{2,1,0:T(8,128)S(1)} collective-permute-done((f32[2,64,1024]{2,1,0:T(8,128)S(1)}, f32[2,64,1024]{2,1,0:T(8,128)S(1)}, u32[]{:S(2)}, u32[]{:S(2)}) %collective-permute-start.2) | collective-permute-done | bytes 524320 | tf_op jit(solution)/shard_map/ppermute | solution.py:175
  26.4 2.2 collective-permute-start.3
  28.6 2.3 collective-permute-done.3
  32.3 45.6 %collective-permute-done.4 = f32[8,64,1024]{2,1,0:T(8,128)S(1)} collective-permute-done((f32[8,64,1024]{2,1,0:T(8,128)S(1)}, f32[8,64,1024]{2,1,0:T(8,128)S(1)}, u32[]{:S(2)}, u32[]{:S(2)}) %collective-permute-start.4) | collective-permute-done | bytes 2097184 | tf_op jit(solution)/shard_map/ppermute | solution.py:175
  79.3 2.5 pad_maximum_fusion
  83.0 3.7 constant_dynamic-slice_fusion.14
  89.7 3.6 constant_dynamic-slice_fusion.11
  93.3 2.0 collective-permute-start.18
  95.3 5.7 constant_dynamic-slice_fusion.8
  101.0 3.2 constant_dynamic-slice_fusion.5
  104.2 8.4 %constant_dynamic-slice_fusion.6 = (f32[8,1,128,1024]{3,2,1,0:T(8,128)}, f32[8,1,128,1024]{3,2,1,0:T(8,128)}) fusion(f32[16,4,128,1024]{3,2,1,0:T(8,128)} %bitcast.73, s32[]{:T(128)S(6)} %select_n.146, s32[]{:T(128)S(6)} %select_n.144), kind=kLoop, calls=%fused_computation.35 | loop fusion | bytes 16777224 | tf_op jit(solution)/shard_map/dynamic_slice | solution.py:227
  112.7 2.3 constant_dynamic-slice_fusion.4
  125.0 48.0 %collective-permute-done.5 = f32[16,64,1024]{2,1,0:T(8,128)} collective-permute-done((f32[16,64,1024]{2,1,0:T(8,128)}, f32[16,64,1024]{2,1,0:T(8,128)}, u32[]{:S(2)}, u32[]{:S(2)}) %collective-permute-start.5) | collective-permute-done | bytes 4194336 | tf_op jit(solution)/shard_map/ppermute | solution.py:175
  183.4 4.3 reverse_select_fusion
  187.7 13.3 %reshape_reshape_reshape.3 = f32[32,2,32,16,64]{4,3,2,1,0:T(8,128)} reshape(f32[1,2,4,4,64,1024]{5,4,3,2,1,0:T(8,128)} %reverse_select_fusion) | data formatting | bytes 16777216 | tf_op jit(solution)/shard_map/reshape;reshape;reshape | solution.py:195
  201.1 15.8 %copy.20 = f32[2,32,16,32,64]{4,3,2,1,0:T(8,128)} copy(f32[2,32,16,32,64]{4,2,3,0,1:T(8,128)} %bitcast.78) | data formatting | bytes 16777216 | tf_op jit(solution)/shard_map/transpose | solution.py:195
  216.9 14.8 %reshape.28 = f32[1024,2048]{1,0:T(8,128)} reshape(f32[2,32,16,32,64]{4,3,2,1,0:T(8,128)} %copy.20) | data formatting | bytes 16777216 | tf_op jit(solution)/shard_map/reshape | solution.py:196
  231.7 5.2 fusion
  237.1 2.4 collective-permute-start.15
  240.6 41.0 %shard_map.28.refs_0_ = f32[64,2048,128]{2,1,0:T(8,128)} custom-call(s32[2]{0:T(128)S(1)} %pad_add_fusion.13.at_ref, f32[16,4,128,1024]{3,2,1,0:T(8,128)} %bitcast.77, bf16[1024,2048]{1,0:T(8,128)(2,1)S(1)} %get-tuple-element.75.th_ref, bf16[1024,2048]{1,0:T(8,128)(2,1)S(1)} %get-tuple-element.74.tl_ref), custom_call_target="tpu_custom_call" | custom-call | flops 25769803776 | bytes 58720256 | tf_op jit(solution)/shard_map/pallas_call | solution.py:67
  281.5 7.8 shard_map.29.refs_0_
  289.7 6.6 shard_map.30.refs_0_
  296.2 6.6 shard_map.31.refs_0_
  302.8 3.2 collective-permute-start.13
  306.0 6.6 shard_map.32.refs_0_
  312.6 7.8 shard_map.33.refs_0_
  320.3 7.8 shard_map.34.refs_0_
  329.9 12.5 %shard_map.35.refs_0_ = f32[64,2048,128]{2,1,0:T(8,128)} custom-call(s32[2]{0:T(128)S(1)} %pad_add_fusion.6.at_ref, f32[4,1,128,1024]{3,2,1,0:T(8,128)} %collective-permute-done.15.v_ref, bf16[1024,2048]{1,0:T(8,128)(2,1)S(1)} %get-tuple-element.75.th_ref, bf16[1024,2048]{1,0:T(8,128)(2,1)S(1)} %get-tuple-element.74.tl_ref, ...), custom_call_target="tpu_custom_call", output_to_operand_aliasing={{}: (4, {})} | custom-call | flops 6442450944 | bytes 14680064 | tf_op jit(solution)/shard_map/pallas_call | solution.py:67
  342.5 98.1 %collective-permute-done.14.v_ref = f32[4,1,128,1024]{3,2,1,0:T(8,128)} collective-permute-done((f32[4,1,128,1024]{3,2,1,0:T(8,128)}, f32[4,1,128,1024]{3,2,1,0:T(8,128)}, u32[]{:S(2)}, u32[]{:S(2)}) %collective-permute-start.14) | collective-permute-done | bytes 2097184 | tf_op jit(solution)/shard_map/ppermute | solution.py:236
  440.5 25.1 %collective-permute-start.9 = (f32[2,1,128,1024]{3,2,1,0:T(8,128)}, f32[2,1,128,1024]{3,2,1,0:T(8,128)}, u32[]{:S(2)}, u32[]{:S(2)}) collective-permute-start(f32[2,1,128,1024]{3,2,1,0:T(8,128)} %constant_dynamic-slice_fusion.4), channel_id=1, source_target_pairs={{0,2},{1,3},{2,0},{3,1},{4,6},{5,7},{6,4},{7,5},{8,10},{9,11},{10,... | collective-permute-start | bytes 3145736 | tf_op jit(solution)/shard_map/ppermute | solution.py:236
  465.7 12.5 %shard_map.36.refs_0_ = f32[64,2048,128]{2,1,0:T(8,128)} custom-call(s32[2]{0:T(128)S(1)} %pad_add_fusion.7.at_ref, f32[4,1,128,1024]{3,2,1,0:T(8,128)} %collective-permute-done.14.v_ref, bf16[1024,2048]{1,0:T(8,128)(2,1)S(1)} %get-tuple-element.75.th_ref, bf16[1024,2048]{1,0:T(8,128)(2,1)S(1)} %get-tuple-element.74.tl_ref, ...), custom_call_target="tpu_custom_call", output_to_operand_aliasing={{}: (4, {})} | custom-call | flops 6442450944 | bytes 14680064 | tf_op jit(solution)/shard_map/pallas_call | solution.py:67
  478.2 234.5 %collective-permute-done.13.v_ref = f32[4,1,128,1024]{3,2,1,0:T(8,128)} collective-permute-done((f32[4,1,128,1024]{3,2,1,0:T(8,128)}, f32[4,1,128,1024]{3,2,1,0:T(8,128)}, u32[]{:S(2)}, u32[]{:S(2)}) %collective-permute-start.13) | collective-permute-done | bytes 2097184 | tf_op jit(solution)/shard_map/ppermute | solution.py:236
  712.7 12.5 %shard_map.37.refs_0_ = f32[64,2048,128]{2,1,0:T(8,128)} custom-call(s32[2]{0:T(128)S(1)} %pad_add_fusion.8.at_ref, f32[4,1,128,1024]{3,2,1,0:T(8,128)} %collective-permute-done.13.v_ref, bf16[1024,2048]{1,0:T(8,128)(2,1)S(1)} %get-tuple-element.75.th_ref, bf16[1024,2048]{1,0:T(8,128)(2,1)S(1)} %get-tuple-element.74.tl_ref, ...), custom_call_target="tpu_custom_call", output_to_operand_aliasing={{}: (4, {})} | custom-call | flops 6442450944 | bytes 14680064 | tf_op jit(solution)/shard_map/pallas_call | solution.py:67
  725.2 2.4 collective-permute-start.7
  727.6 22.0 %shard_map.38.refs_0_ = f32[64,2048,128]{2,1,0:T(8,128)} custom-call(s32[2]{0:T(128)S(1)} %pad_add_fusion.9.at_ref, f32[8,1,128,1024]{3,2,1,0:T(8,128)} %collective-permute-done.12.v_ref, bf16[1024,2048]{1,0:T(8,128)(2,1)S(1)} %get-tuple-element.75.th_ref, bf16[1024,2048]{1,0:T(8,128)(2,1)S(1)} %get-tuple-element.74.tl_ref, ...), custom_call_target="tpu_custom_call", output_to_operand_aliasing={{}: (4, {})} | custom-call | flops 12884901888 | bytes 20971520 | tf_op jit(solution)/shard_map/pallas_call | solution.py:67
  749.6 22.0 %shard_map.39.refs_0_ = f32[64,2048,128]{2,1,0:T(8,128)} custom-call(s32[2]{0:T(128)S(1)} %pad_add_fusion.10.at_ref, f32[8,1,128,1024]{3,2,1,0:T(8,128)} %collective-permute-done.11.v_ref, bf16[1024,2048]{1,0:T(8,128)(2,1)S(1)} %get-tuple-element.75.th_ref, bf16[1024,2048]{1,0:T(8,128)(2,1)S(1)} %get-tuple-element.74.tl_ref, ...), custom_call_target="tpu_custom_call", output_to_operand_aliasing={{}: (4, {})} | custom-call | flops 12884901888 | bytes 20971520 | tf_op jit(solution)/shard_map/pallas_call | solution.py:67
  771.6 2.9 collective-permute-done.10.v_ref
  774.5 12.5 %shard_map.40.refs_0_ = f32[64,2048,128]{2,1,0:T(8,128)} custom-call(s32[2]{0:T(128)S(1)} %pad_add_fusion.11.at_ref, f32[4,1,128,1024]{3,2,1,0:T(8,128)} %collective-permute-done.10.v_ref, bf16[1024,2048]{1,0:T(8,128)(2,1)S(1)} %get-tuple-element.75.th_ref, bf16[1024,2048]{1,0:T(8,128)(2,1)S(1)} %get-tuple-element.74.tl_ref, ...), custom_call_target="tpu_custom_call", output_to_operand_aliasing={{}: (4, {})} | custom-call | flops 6442450944 | bytes 14680064 | tf_op jit(solution)/shard_map/pallas_call | solution.py:67
  787.0 15.6 %collective-permute-done.9.v_ref = f32[2,1,128,1024]{3,2,1,0:T(8,128)} collective-permute-done((f32[2,1,128,1024]{3,2,1,0:T(8,128)}, f32[2,1,128,1024]{3,2,1,0:T(8,128)}, u32[]{:S(2)}, u32[]{:S(2)}) %collective-permute-start.9) | collective-permute-done | bytes 1048608 | tf_op jit(solution)/shard_map/ppermute | solution.py:236
  802.6 8.1 shard_map.41._
  810.6 1.9 shard_map.42
  813.8 2.8 shard_map.43._
  816.6 2.8 collective-permute-done.6.v_ref
  819.4 1.9 shard_map.44
  821.3 3.7 collective-permute-done.v_ref
  825.0 2.8 shard_map.45
  (64 shorter events, 34.5 us)
Async XLA Ops:
  0.0 9.3 %collective-permute-start.1 = (f32[1,64,1024]{2,1,0:T(8,128)}, f32[1,64,1024]{2,1,0:T(8,128)S(1)}, u32[]{:S(2)}, u32[]{:S(2)}) collective-permute-start(f32[1,64,1024]{2,1,0:T(8,128)} %bitcast.87), channel_id=1, source_target_pairs={{0,3},{1,2},{2,1},{3,0},{4,7},{5,6},{6,5},{7,4},{8,11},{9,10},{10,... | collective-permute-start | bytes 786440 | tf_op jit(solution)/shard_map/ppermute | solution.py:175
  10.3 14.7 %collective-permute-start.2 = (f32[2,64,1024]{2,1,0:T(8,128)S(1)}, f32[2,64,1024]{2,1,0:T(8,128)S(1)}, u32[]{:S(2)}, u32[]{:S(2)}) collective-permute-start(f32[2,64,1024]{2,1,0:T(8,128)S(1)} %pad_maximum_fusion.3), channel_id=1, source_target_pairs={{0,1},{1,0},{2,3},{3,2},{4,5},{5,4},{6,7},{7,6},{8,9},{9,8},{10,11... | collective-permute-start | bytes 1572872 | tf_op jit(solution)/shard_map/ppermute | solution.py:175
  26.4 60.3 %copy-start = (f32[1,2,2,1,64,1024]{5,4,2,1,3,0:T(8,128)}, f32[1,2,2,1,64,1024]{5,4,2,1,3,0:T(8,128)S(1)}, u32[]{:S(2)}) copy-start(f32[1,2,2,1,64,1024]{5,4,2,1,3,0:T(8,128)S(1)} %reverse_select_fusion.3) | copy-start | bytes 3145732
  26.4 4.5 collective-permute-start.3
  30.9 55.8 %copy-start.1 = (f32[4,64,1024]{2,1,0:T(8,128)}, f32[4,64,1024]{2,1,0:T(8,128)S(1)}, u32[]{:S(2)}) copy-start(f32[4,64,1024]{2,1,0:T(8,128)S(1)} %collective-permute-done.3) | copy-start | bytes 3145732
  31.0 46.9 %collective-permute-start.4 = (f32[8,64,1024]{2,1,0:T(8,128)S(1)}, f32[8,64,1024]{2,1,0:T(8,128)S(1)}, u32[]{:S(2)}, u32[]{:S(2)}) collective-permute-start(f32[8,64,1024]{2,1,0:T(8,128)S(1)} %pad_maximum_fusion.1), channel_id=1, source_target_pairs={{0,8},{4,12},{8,0},{12,4},{16,24},{20,28},{24,16},{28,20},{1,9},{5... | collective-permute-start | bytes 6291464 | tf_op jit(solution)/shard_map/ppermute | solution.py:175
  77.9 1.4 copy-start.2
  81.7 91.2 %collective-permute-start.5 = (f32[16,64,1024]{2,1,0:T(8,128)}, f32[16,64,1024]{2,1,0:T(8,128)}, u32[]{:S(2)}, u32[]{:S(2)}) collective-permute-start(f32[16,64,1024]{2,1,0:T(8,128)} %pad_maximum_fusion), channel_id=1, source_target_pairs={{0,16},{4,20},{8,24},{12,28},{16,0},{20,4},{24,8},{28,12},{1,17},{... | collective-permute-start | bytes 12582920 | tf_op jit(solution)/shard_map/ppermute | solution.py:175
  86.7 150.3 %collective-permute-start.21 = (f32[2,1,128,1024]{3,2,1,0:T(8,128)}, f32[2,1,128,1024]{3,2,1,0:T(8,128)}, u32[]{:S(2)}, u32[]{:S(2)}) collective-permute-start(f32[2,1,128,1024]{3,2,1,0:T(8,128)} %get-tuple-element.54), channel_id=1, source_target_pairs={{0,1},{1,2},{2,3},{3,0},{4,5},{5,6},{6,7},{7,4},{8,9},{9,10},{10,1... | collective-permute-start | bytes 3145736 | tf_op jit(solution)/shard_map/ppermute | solution.py:236
  87.9 149.2 %collective-permute-start.20 = (f32[2,1,128,1024]{3,2,1,0:T(8,128)}, f32[2,1,128,1024]{3,2,1,0:T(8,128)S(1)}, u32[]{:S(2)}, u32[]{:S(2)}) collective-permute-start(f32[2,1,128,1024]{3,2,1,0:T(8,128)} %get-tuple-element.53), channel_id=1, source_target_pairs={{0,3},{1,0},{2,1},{3,2},{4,7},{5,4},{6,5},{7,6},{8,11},{9,8},{10,9... | collective-permute-start | bytes 3145736 | tf_op jit(solution)/shard_map/ppermute | solution.py:236
  88.2 151.3 %collective-permute-start.19 = (f32[2,1,128,1024]{3,2,1,0:T(8,128)}, f32[2,1,128,1024]{3,2,1,0:T(8,128)S(1)}, u32[]{:S(2)}, u32[]{:S(2)}) collective-permute-start(f32[2,1,128,1024]{3,2,1,0:T(8,128)} %get-tuple-element.52), channel_id=1, source_target_pairs={{0,2},{1,3},{2,0},{3,1},{4,6},{5,7},{6,4},{7,5},{8,10},{9,11},{10,... | collective-permute-start | bytes 3145736 | tf_op jit(solution)/shard_map/ppermute | solution.py:236
  93.3 196.0 %collective-permute-start.18 = (f32[2,1,128,1024]{3,2,1,0:T(8,128)}, f32[2,1,128,1024]{3,2,1,0:T(8,128)S(1)}, u32[]{:S(2)}, u32[]{:S(2)}) collective-permute-start(f32[2,1,128,1024]{3,2,1,0:T(8,128)} %get-tuple-element.51), channel_id=1, source_target_pairs={{0,1},{1,2},{2,3},{3,0},{4,5},{5,6},{6,7},{7,4},{8,9},{9,10},{10,1... | collective-permute-start | bytes 3145736 | tf_op jit(solution)/shard_map/ppermute | solution.py:236
  172.9 123.3 %collective-permute-start.17 = (f32[2,1,128,1024]{3,2,1,0:T(8,128)}, f32[2,1,128,1024]{3,2,1,0:T(8,128)}, u32[]{:S(2)}, u32[]{:S(2)}) collective-permute-start(f32[2,1,128,1024]{3,2,1,0:T(8,128)} %get-tuple-element.50), channel_id=1, source_target_pairs={{0,3},{1,0},{2,1},{3,2},{4,7},{5,4},{6,5},{7,6},{8,11},{9,8},{10,9... | collective-permute-start | bytes 3145736 | tf_op jit(solution)/shard_map/ppermute | solution.py:236
  236.9 65.9 %collective-permute-start.16 = (f32[2,1,128,1024]{3,2,1,0:T(8,128)}, f32[2,1,128,1024]{3,2,1,0:T(8,128)}, u32[]{:S(2)}, u32[]{:S(2)}) collective-permute-start(f32[2,1,128,1024]{3,2,1,0:T(8,128)} %get-tuple-element.49), channel_id=1, source_target_pairs={{0,2},{1,3},{2,0},{3,1},{4,6},{5,7},{6,4},{7,5},{8,10},{9,11},{10,... | collective-permute-start | bytes 3145736 | tf_op jit(solution)/shard_map/ppermute | solution.py:236
  237.1 91.1 %collective-permute-start.15 = (f32[4,1,128,1024]{3,2,1,0:T(8,128)}, f32[4,1,128,1024]{3,2,1,0:T(8,128)}, u32[]{:S(2)}, u32[]{:S(2)}) collective-permute-start(f32[4,1,128,1024]{3,2,1,0:T(8,128)} %get-tuple-element.48), channel_id=1, source_target_pairs={{0,1},{1,2},{2,3},{3,0},{4,5},{5,6},{6,7},{7,4},{8,9},{9,10},{10,1... | collective-permute-start | bytes 6291464 | tf_op jit(solution)/shard_map/ppermute | solution.py:236
  239.4 485.8 %collective-permute-start.12 = (f32[8,1,128,1024]{3,2,1,0:T(8,128)}, f32[8,1,128,1024]{3,2,1,0:T(8,128)}, u32[]{:S(2)}, u32[]{:S(2)}) collective-permute-start(f32[8,1,128,1024]{3,2,1,0:T(8,128)} %get-tuple-element.45), channel_id=1, source_target_pairs={{0,1},{1,2},{2,3},{3,0},{4,5},{5,6},{6,7},{7,4},{8,9},{9,10},{10,1... | collective-permute-start | bytes 12582920 | tf_op jit(solution)/shard_map/ppermute | solution.py:236
  289.3 151.2 %collective-permute-start.14 = (f32[4,1,128,1024]{3,2,1,0:T(8,128)}, f32[4,1,128,1024]{3,2,1,0:T(8,128)}, u32[]{:S(2)}, u32[]{:S(2)}) collective-permute-start(f32[4,1,128,1024]{3,2,1,0:T(8,128)} %get-tuple-element.47), channel_id=1, source_target_pairs={{0,3},{1,0},{2,1},{3,2},{4,7},{5,4},{6,5},{7,6},{8,11},{9,8},{10,9... | collective-permute-start | bytes 6291464 | tf_op jit(solution)/shard_map/ppermute | solution.py:236
  296.2 453.4 %collective-permute-start.11 = (f32[8,1,128,1024]{3,2,1,0:T(8,128)}, f32[8,1,128,1024]{3,2,1,0:T(8,128)}, u32[]{:S(2)}, u32[]{:S(2)}) collective-permute-start(f32[8,1,128,1024]{3,2,1,0:T(8,128)} %get-tuple-element.44), channel_id=1, source_target_pairs={{0,3},{1,0},{2,1},{3,2},{4,7},{5,4},{6,5},{7,6},{8,11},{9,8},{10,9... | collective-permute-start | bytes 12582920 | tf_op jit(solution)/shard_map/ppermute | solution.py:236
  302.8 409.9 %collective-permute-start.13 = (f32[4,1,128,1024]{3,2,1,0:T(8,128)}, f32[4,1,128,1024]{3,2,1,0:T(8,128)}, u32[]{:S(2)}, u32[]{:S(2)}) collective-permute-start(f32[4,1,128,1024]{3,2,1,0:T(8,128)} %get-tuple-element.46), channel_id=1, source_target_pairs={{0,2},{1,3},{2,0},{3,1},{4,6},{5,7},{6,4},{7,5},{8,10},{9,11},{10,... | collective-permute-start | bytes 6291464 | tf_op jit(solution)/shard_map/ppermute | solution.py:236
  328.1 446.3 %collective-permute-start.10 = (f32[4,1,128,1024]{3,2,1,0:T(8,128)}, f32[4,1,128,1024]{3,2,1,0:T(8,128)}, u32[]{:S(2)}, u32[]{:S(2)}) collective-permute-start(f32[4,1,128,1024]{3,2,1,0:T(8,128)} %constant_dynamic-slice_fusion.5), channel_id=1, source_target_pairs={{0,2},{1,3},{2,0},{3,1},{4,6},{5,7},{6,4},{7,5},{8,10},{9,11},{10,... | collective-permute-start | bytes 6291464 | tf_op jit(solution)/shard_map/ppermute | solution.py:236
  440.5 362.0 %collective-permute-start.9 = (f32[2,1,128,1024]{3,2,1,0:T(8,128)}, f32[2,1,128,1024]{3,2,1,0:T(8,128)}, u32[]{:S(2)}, u32[]{:S(2)}) collective-permute-start(f32[2,1,128,1024]{3,2,1,0:T(8,128)} %constant_dynamic-slice_fusion.4), channel_id=1, source_target_pairs={{0,2},{1,3},{2,0},{3,1},{4,6},{5,7},{6,4},{7,5},{8,10},{9,11},{10,... | collective-permute-start | bytes 3145736 | tf_op jit(solution)/shard_map/ppermute | solution.py:236
  712.7 97.9 %collective-permute-start.8 = (f32[1,1,128,512]{3,2,1,0:T(8,128)}, f32[1,1,128,512]{3,2,1,0:T(8,128)}, u32[]{:S(2)}, u32[]{:S(2)}) collective-permute-start(f32[1,1,128,512]{3,2,1,0:T(8,128)} %get-tuple-element.41), channel_id=1, source_target_pairs={{0,2},{1,3},{2,0},{3,1},{4,6},{5,7},{6,4},{7,5},{8,10},{9,11},{10,... | collective-permute-start | bytes 786440 | tf_op jit(solution)/shard_map/ppermute | solution.py:236
  725.2 88.6 %collective-permute-start.7 = (f32[1,1,128,512]{3,2,1,0:T(8,128)}, f32[1,1,128,512]{3,2,1,0:T(8,128)}, u32[]{:S(2)}, u32[]{:S(2)}) collective-permute-start(f32[1,1,128,512]{3,2,1,0:T(8,128)} %get-tuple-element.40), channel_id=1, source_target_pairs={{0,2},{1,3},{2,0},{3,1},{4,6},{5,7},{6,4},{7,5},{8,10},{9,11},{10,... | collective-permute-start | bytes 786440 | tf_op jit(solution)/shard_map/ppermute | solution.py:236
  749.6 69.8 %collective-permute-start.6 = (f32[1,1,128,512]{3,2,1,0:T(8,128)}, f32[1,1,128,512]{3,2,1,0:T(8,128)}, u32[]{:S(2)}, u32[]{:S(2)}) collective-permute-start(f32[1,1,128,512]{3,2,1,0:T(8,128)} %get-tuple-element.39), channel_id=1, source_target_pairs={{0,2},{1,3},{2,0},{3,1},{4,6},{5,7},{6,4},{7,5},{8,10},{9,11},{10,... | collective-permute-start | bytes 786440 | tf_op jit(solution)/shard_map/ppermute | solution.py:236
  774.5 50.6 %collective-permute-start = (f32[1,1,128,512]{3,2,1,0:T(8,128)}, f32[1,1,128,512]{3,2,1,0:T(8,128)}, u32[]{:S(2)}, u32[]{:S(2)}) collective-permute-start(f32[1,1,128,512]{3,2,1,0:T(8,128)} %get-tuple-element.38), channel_id=1, source_target_pairs={{0,2},{1,3},{2,0},{3,1},{4,6},{5,7},{6,4},{7,5},{8,10},{9,11},{10,... | collective-permute-start | bytes 786440 | tf_op jit(solution)/shard_map/ppermute | solution.py:236

commit v6 on v5

--- a/solution.py
+++ b/solution.py
@@ -99,13 +99,15 @@
     return dot(vs_ref[:b_width, :], tl_ref[rows, :]) + both[b_width:] + both[:b_width]
 
 
-def first_kernel(v_ref, th_ref, tl_ref, _, sum_ref, __, vs_ref):
-    sum_ref[...] = part_products(0, v_ref, th_ref, tl_ref, vs_ref)
-
-
-def last_kernel(at_ref, v_ref, th_ref, tl_ref, sum_ref, _, o_ref, vs_ref, part_ref, tile_ref, sems):
+def sum_kernel(part, v_ref, th_ref, tl_ref, *refs):
+    sum_ref, _, vs_ref = refs[-3:]
+    acc = part_products(part, v_ref, th_ref, tl_ref, vs_ref)
+    sum_ref[...] = acc if part == 0 else acc + refs[0][...]
+
+
+def last_kernel(part, at_ref, v_ref, th_ref, tl_ref, sum_ref, _, o_ref, vs_ref, part_ref, tile_ref, sems):
     half = v_ref.shape[2] // 2
-    acc = part_products(1, v_ref, th_ref, tl_ref, vs_ref)
+    acc = part_products(part, v_ref, th_ref, tl_ref, vs_ref)
     low_half = lax.broadcasted_iota(jnp.int32, (half, LANES), 1) < NO
     copies = []
     for pair in range(NI * NO // LANES):
@@ -138,18 +140,20 @@
     stacked = pltpu.VMEM((2 * b_width, depth), jnp.bfloat16)
     params = pltpu.CompilerParams(vmem_limit_bytes=24 << 20)
     written = jax.ShapeDtypeStruct(ladder.shape, ladder.dtype)
-    sums, ladder = pl.pallas_call(
-        first_kernel,
-        out_shape=(jax.ShapeDtypeStruct((b_width, NI * NO), jnp.float32), written),
-        in_specs=[held, held, held, anywhere],
-        out_specs=(held, anywhere),
-        scratch_shapes=[stacked],
-        input_output_aliases={3: 1},
-        compiler_params=params,
-        cost_estimate=cost,
-    )(parts[0], th, tl, ladder)
+    sums = []
+    for part, piece in enumerate(parts[:-1]):
+        *sums, ladder = pl.pallas_call(
+            functools.partial(sum_kernel, part),
+            out_shape=(jax.ShapeDtypeStruct((b_width, NI * NO), jnp.float32), written),
+            in_specs=[held] * (3 + len(sums)) + [anywhere],
+            out_specs=(held, anywhere),
+            scratch_shapes=[stacked],
+            input_output_aliases={3 + len(sums): 1},
+            compiler_params=params,
+            cost_estimate=cost,
+        )(piece, th, tl, *sums, ladder)
     return pl.pallas_call(
-        last_kernel,
+        functools.partial(last_kernel, len(parts) - 1),
         out_shape=written,
         in_specs=[pl.BlockSpec(memory_space=pltpu.SMEM), held, held, held, held, anywhere],
         out_specs=anywhere,
@@ -162,7 +166,7 @@
         input_output_aliases={5: 0},
         compiler_params=params,
         cost_estimate=cost,
-    )(at.reshape(1), parts[1], th, tl, sums, ladder)
+    )(at.reshape(1), parts[-1], th, tl, *sums, ladder)
 
 
 def gather_over(axis, pieces, masks):
@@ -220,7 +224,9 @@
     arrived = []
     source = blocks
     for exchanges in rounds_of(avals, cols):
-        parts = 2 if len(exchanges) == 1 and exchanges[0][2] == 1 else 1
+        parts = 1
+        if len(exchanges) == 1 and exchanges[0][2] == 1:
+            parts = 4 if exchanges[0][1] == avals - 1 else 2
         width = depth // parts
         sent = [exchange + (part,) for exchange in exchanges for part in range(parts)]
         pieces = [

time: 832 us -> 830 us (level)
    ppermute x17 -> x19, waiting for transfers between devices: 359 us -> 353 us  [body(): lax.ppermute(piece, 'col', [(k, (k + shift) % cols) for k in range(cols)])]
    ppermute x17 -> x19, starting transfers between devices: 42.9 us -> 47.2 us  [body(): lax.ppermute(piece, 'col', [(k, (k + shift) % cols) for k in range(cols)])]
  transfers between devices with their start and end apart: 22 -> 24, of which waited for: 12 -> 14; matrix products, arithmetic and copies ran while one was open for 12% -> 12% of each run, Pallas kernels for 23% -> 24%
where the time goes in v6:
time: 830 us; the launch traced here: 826 us
  waiting for transfers between devices  469 us (57%)
  Pallas kernels  196 us (24%)
  local copies, waits for them, and re-layouts  85.3 us (10%)
  starting transfers between devices  55.9 us (7%)
  other arithmetic  19.4 us (2%)
    ppermute x19, waiting for transfers between devices, body(): lax.ppermute(piece, 'col', [(k, (k + shift) % cols) for k in range(cols)])  353 us
    pallas_call x14, Pallas kernels, multiply(): pl.pallas_call(functools.partial(ladder_kernel, group, width), out_shape=...  186 us
    ppermute x5, waiting for transfers between devices, gather_over(): got = lax.ppermute(block, axis, [(k, k ^ mask) for k in range(size)])  116 us
    ppermute x19, starting transfers between devices, body(): lax.ppermute(piece, 'col', [(k, (k + shift) % cols) for k in range(cols)])  47.2 us
    dynamic_slice x8, local copies, waits for them, and re-layouts, body(): lax.dynamic_slice(source, (start, (here + shift) % cols, 0, part * width)...  30.8 us
  transfers between devices with their start and end apart: 24, of which 14 were waited for; matrix products, arithmetic and copies ran while one was open for 12% of the time, Pallas kernels for 24%

profile of v6, /device:TPU:25, one launch (start us, length us, event | category | flops | bytes accessed | tf_op | source)
XLA Modules:
  0.0 825.6 jit_solution(2215854051745188410)
XLA Ops:
  0.0 9.3 %collective-permute-done.1 = f32[1,64,1024]{2,1,0:T(8,128)S(1)} collective-permute-done((f32[1,64,1024]{2,1,0:T(8,128)}, f32[1,64,1024]{2,1,0:T(8,128)S(1)}, u32[]{:S(2)}, u32[]{:S(2)}) %collective-permute-start.1) | collective-permute-done | bytes 262176 | tf_op jit(solution)/shard_map/ppermute | solution.py:179
  10.3 4.0 collective-permute-start.2
  14.2 10.8 %collective-permute-done.2 = f32[2,64,1024]{2,1,0:T(8,128)S(1)} collective-permute-done((f32[2,64,1024]{2,1,0:T(8,128)S(1)}, f32[2,64,1024]{2,1,0:T(8,128)S(1)}, u32[]{:S(2)}, u32[]{:S(2)}) %collective-permute-start.2) | collective-permute-done | bytes 524320 | tf_op jit(solution)/shard_map/ppermute | solution.py:179
  26.4 2.2 collective-permute-start.3
  28.6 2.3 collective-permute-done.3
  32.3 45.6 %collective-permute-done.4 = f32[8,64,1024]{2,1,0:T(8,128)S(1)} collective-permute-done((f32[8,64,1024]{2,1,0:T(8,128)S(1)}, f32[8,64,1024]{2,1,0:T(8,128)S(1)}, u32[]{:S(2)}, u32[]{:S(2)}) %collective-permute-start.4) | collective-permute-done | bytes 2097184 | tf_op jit(solution)/shard_map/ppermute | solution.py:179
  77.9 2.6 pad_maximum_fusion
  81.8 3.7 constant_dynamic-slice_fusion.16
  88.5 3.6 constant_dynamic-slice_fusion.13
  92.1 2.0 collective-permute-start.20
  94.1 5.8 constant_dynamic-slice_fusion.10
  99.9 3.2 constant_dynamic-slice_fusion.7
  103.1 8.4 %constant_dynamic-slice_fusion.8 = (f32[8,1,128,1024]{3,2,1,0:T(8,128)}, f32[8,1,128,1024]{3,2,1,0:T(8,128)}) fusion(f32[16,4,128,1024]{3,2,1,0:T(8,128)} %bitcast.73, s32[]{:T(128)S(6)} %select_n.152, s32[]{:T(128)S(6)} %select_n.150), kind=kLoop, calls=%fused_computation.37 | loop fusion | bytes 16777224 | tf_op jit(solution)/shard_map/dynamic_slice | solution.py:233
  111.5 2.3 constant_dynamic-slice_fusion.6
  123.9 47.9 %collective-permute-done.5 = f32[16,64,1024]{2,1,0:T(8,128)} collective-permute-done((f32[16,64,1024]{2,1,0:T(8,128)}, f32[16,64,1024]{2,1,0:T(8,128)}, u32[]{:S(2)}, u32[]{:S(2)}) %collective-permute-start.5) | collective-permute-done | bytes 4194336 | tf_op jit(solution)/shard_map/ppermute | solution.py:179
  178.5 1.9 reverse_select_fusion.2
  182.3 4.3 reverse_select_fusion
  186.6 13.3 %reshape_reshape_reshape.3 = f32[32,2,32,16,64]{4,3,2,1,0:T(8,128)} reshape(f32[1,2,4,4,64,1024]{5,4,3,2,1,0:T(8,128)} %reverse_select_fusion) | data formatting | bytes 16777216 | tf_op jit(solution)/shard_map/reshape;reshape;reshape | solution.py:199
  199.9 15.8 %copy.22 = f32[2,32,16,32,64]{4,3,2,1,0:T(8,128)} copy(f32[2,32,16,32,64]{4,2,3,0,1:T(8,128)} %bitcast.78) | data formatting | bytes 16777216 | tf_op jit(solution)/shard_map/transpose | solution.py:199
  215.8 14.8 %reshape.28 = f32[1024,2048]{1,0:T(8,128)} reshape(f32[2,32,16,32,64]{4,3,2,1,0:T(8,128)} %copy.22) | data formatting | bytes 16777216 | tf_op jit(solution)/shard_map/reshape | solution.py:200
  230.6 5.2 fusion
  236.0 2.4 collective-permute-start.17
  239.4 41.0 %shard_map.28.refs_0_ = f32[64,2048,128]{2,1,0:T(8,128)} custom-call(s32[2]{0:T(128)S(1)} %pad_add_fusion.13.at_ref, f32[16,4,128,1024]{3,2,1,0:T(8,128)} %bitcast.77, bf16[1024,2048]{1,0:T(8,128)(2,1)S(1)} %get-tuple-element.89.th_ref, bf16[1024,2048]{1,0:T(8,128)(2,1)S(1)} %get-tuple-element.88.tl_ref), custom_call_target="tpu_custom_call" | custom-call | flops 25769803776 | bytes 58720256 | tf_op jit(solution)/shard_map/pallas_call | solution.py:67
  280.4 7.8 shard_map.29.refs_0_
  288.6 6.6 shard_map.30.refs_0_
  295.1 6.6 shard_map.31.refs_0_
  301.7 3.2 collective-permute-start.15
  304.9 6.6 shard_map.32.refs_0_
  311.4 7.8 shard_map.33.refs_0_
  319.2 7.8 shard_map.34.refs_0_
  328.8 12.5 %shard_map.35.refs_0_ = f32[64,2048,128]{2,1,0:T(8,128)} custom-call(s32[2]{0:T(128)S(1)} %pad_add_fusion.6.at_ref, f32[4,1,128,1024]{3,2,1,0:T(8,128)} %collective-permute-done.17.v_ref, bf16[1024,2048]{1,0:T(8,128)(2,1)S(1)} %get-tuple-element.89.th_ref, bf16[1024,2048]{1,0:T(8,128)(2,1)S(1)} %get-tuple-element.88.tl_ref, ...), custom_call_target="tpu_custom_call", output_to_operand_aliasing={{}: (4, {})} | custom-call | flops 6442450944 | bytes 14680064 | tf_op jit(solution)/shard_map/pallas_call | solution.py:67
  341.4 98.1 %collective-permute-done.16.v_ref = f32[4,1,128,1024]{3,2,1,0:T(8,128)} collective-permute-done((f32[4,1,128,1024]{3,2,1,0:T(8,128)}, f32[4,1,128,1024]{3,2,1,0:T(8,128)}, u32[]{:S(2)}, u32[]{:S(2)}) %collective-permute-start.16) | collective-permute-done | bytes 2097184 | tf_op jit(solution)/shard_map/ppermute | solution.py:242
  439.4 25.1 %collective-permute-start.11 = (f32[2,1,128,1024]{3,2,1,0:T(8,128)}, f32[2,1,128,1024]{3,2,1,0:T(8,128)}, u32[]{:S(2)}, u32[]{:S(2)}) collective-permute-start(f32[2,1,128,1024]{3,2,1,0:T(8,128)} %constant_dynamic-slice_fusion.6), channel_id=1, source_target_pairs={{0,2},{1,3},{2,0},{3,1},{4,6},{5,7},{6,4},{7,5},{8,10},{9,11},{10,... | collective-permute-start | bytes 3145736 | tf_op jit(solution)/shard_map/ppermute | solution.py:242
  464.5 12.5 %shard_map.36.refs_0_ = f32[64,2048,128]{2,1,0:T(8,128)} custom-call(s32[2]{0:T(128)S(1)} %pad_add_fusion.7.at_ref, f32[4,1,128,1024]{3,2,1,0:T(8,128)} %collective-permute-done.16.v_ref, bf16[1024,2048]{1,0:T(8,128)(2,1)S(1)} %get-tuple-element.89.th_ref, bf16[1024,2048]{1,0:T(8,128)(2,1)S(1)} %get-tuple-element.88.tl_ref, ...), custom_call_target="tpu_custom_call", output_to_operand_aliasing={{}: (4, {})} | custom-call | flops 6442450944 | bytes 14680064 | tf_op jit(solution)/shard_map/pallas_call | solution.py:67
  477.1 234.5 %collective-permute-done.15.v_ref = f32[4,1,128,1024]{3,2,1,0:T(8,128)} collective-permute-done((f32[4,1,128,1024]{3,2,1,0:T(8,128)}, f32[4,1,128,1024]{3,2,1,0:T(8,128)}, u32[]{:S(2)}, u32[]{:S(2)}) %collective-permute-start.15) | collective-permute-done | bytes 2097184 | tf_op jit(solution)/shard_map/ppermute | solution.py:242
  711.6 12.5 %shard_map.37.refs_0_ = f32[64,2048,128]{2,1,0:T(8,128)} custom-call(s32[2]{0:T(128)S(1)} %pad_add_fusion.8.at_ref, f32[4,1,128,1024]{3,2,1,0:T(8,128)} %collective-permute-done.15.v_ref, bf16[1024,2048]{1,0:T(8,128)(2,1)S(1)} %get-tuple-element.89.th_ref, bf16[1024,2048]{1,0:T(8,128)(2,1)S(1)} %get-tuple-element.88.tl_ref, ...), custom_call_target="tpu_custom_call", output_to_operand_aliasing={{}: (4, {})} | custom-call | flops 6442450944 | bytes 14680064 | tf_op jit(solution)/shard_map/pallas_call | solution.py:67
  724.1 2.4 collective-permute-start.9
  726.5 22.0 %shard_map.38.refs_0_ = f32[64,2048,128]{2,1,0:T(8,128)} custom-call(s32[2]{0:T(128)S(1)} %pad_add_fusion.9.at_ref, f32[8,1,128,1024]{3,2,1,0:T(8,128)} %collective-permute-done.14.v_ref, bf16[1024,2048]{1,0:T(8,128)(2,1)S(1)} %get-tuple-element.89.th_ref, bf16[1024,2048]{1,0:T(8,128)(2,1)S(1)} %get-tuple-element.88.tl_ref, ...), custom_call_target="tpu_custom_call", output_to_operand_aliasing={{}: (4, {})} | custom-call | flops 12884901888 | bytes 20971520 | tf_op jit(solution)/shard_map/pallas_call | solution.py:67
  748.5 22.0 %shard_map.39.refs_0_ = f32[64,2048,128]{2,1,0:T(8,128)} custom-call(s32[2]{0:T(128)S(1)} %pad_add_fusion.10.at_ref, f32[8,1,128,1024]{3,2,1,0:T(8,128)} %collective-permute-done.13.v_ref, bf16[1024,2048]{1,0:T(8,128)(2,1)S(1)} %get-tuple-element.89.th_ref, bf16[1024,2048]{1,0:T(8,128)(2,1)S(1)} %get-tuple-element.88.tl_ref, ...), custom_call_target="tpu_custom_call", output_to_operand_aliasing={{}: (4, {})} | custom-call | flops 12884901888 | bytes 20971520 | tf_op jit(solution)/shard_map/pallas_call | solution.py:67
  770.5 2.3 collective-permute-start.7
  772.8 12.5 %shard_map.40.refs_0_ = f32[64,2048,128]{2,1,0:T(8,128)} custom-call(s32[2]{0:T(128)S(1)} %pad_add_fusion.11.at_ref, f32[4,1,128,1024]{3,2,1,0:T(8,128)} %collective-permute-done.12.v_ref, bf16[1024,2048]{1,0:T(8,128)(2,1)S(1)} %get-tuple-element.89.th_ref, bf16[1024,2048]{1,0:T(8,128)(2,1)S(1)} %get-tuple-element.88.tl_ref, ...), custom_call_target="tpu_custom_call", output_to_operand_aliasing={{}: (4, {})} | custom-call | flops 6442450944 | bytes 14680064 | tf_op jit(solution)/shard_map/pallas_call | solution.py:67
  785.4 10.4 %collective-permute-done.11.v_ref = f32[2,1,128,1024]{3,2,1,0:T(8,128)} collective-permute-done((f32[2,1,128,1024]{3,2,1,0:T(8,128)}, f32[2,1,128,1024]{3,2,1,0:T(8,128)}, u32[]{:S(2)}, u32[]{:S(2)}) %collective-permute-start.11) | collective-permute-done | bytes 1048608 | tf_op jit(solution)/shard_map/ppermute | solution.py:242
  795.8 8.1 shard_map.41.refs_0_
  804.3 2.0 collective-permute-start
  806.2 1.9 shard_map.42
  808.2 4.5 collective-permute-done.9.v_ref
  812.7 2.8 shard_map.43.refs_0_
  821.6 2.2 collective-permute-done.v_ref
  (74 shorter events, 38.1 us)
Async XLA Ops:
  0.0 9.3 %collective-permute-start.1 = (f32[1,64,1024]{2,1,0:T(8,128)}, f32[1,64,1024]{2,1,0:T(8,128)S(1)}, u32[]{:S(2)}, u32[]{:S(2)}) collective-permute-start(f32[1,64,1024]{2,1,0:T(8,128)} %bitcast.87), channel_id=1, source_target_pairs={{0,3},{1,2},{2,1},{3,0},{4,7},{5,6},{6,5},{7,4},{8,11},{9,10},{10,... | collective-permute-start | bytes 786440 | tf_op jit(solution)/shard_map/ppermute | solution.py:179
  10.3 14.7 %collective-permute-start.2 = (f32[2,64,1024]{2,1,0:T(8,128)S(1)}, f32[2,64,1024]{2,1,0:T(8,128)S(1)}, u32[]{:S(2)}, u32[]{:S(2)}) collective-permute-start(f32[2,64,1024]{2,1,0:T(8,128)S(1)} %pad_maximum_fusion.3), channel_id=1, source_target_pairs={{0,1},{1,0},{2,3},{3,2},{4,5},{5,4},{6,7},{7,6},{8,9},{9,8},{10,11... | collective-permute-start | bytes 1572872 | tf_op jit(solution)/shard_map/ppermute | solution.py:179
  26.4 59.1 %copy-start = (f32[1,2,2,1,64,1024]{5,4,2,1,3,0:T(8,128)}, f32[1,2,2,1,64,1024]{5,4,2,1,3,0:T(8,128)S(1)}, u32[]{:S(2)}) copy-start(f32[1,2,2,1,64,1024]{5,4,2,1,3,0:T(8,128)S(1)} %reverse_select_fusion.3) | copy-start | bytes 3145732
  26.4 4.5 collective-permute-start.3
  30.8 47.0 %copy-start.1 = (f32[4,64,1024]{2,1,0:T(8,128)}, f32[4,64,1024]{2,1,0:T(8,128)S(1)}, u32[]{:S(2)}) copy-start(f32[4,64,1024]{2,1,0:T(8,128)S(1)} %collective-permute-done.3) | copy-start | bytes 3145732
  31.0 46.9 %collective-permute-start.4 = (f32[8,64,1024]{2,1,0:T(8,128)S(1)}, f32[8,64,1024]{2,1,0:T(8,128)S(1)}, u32[]{:S(2)}, u32[]{:S(2)}) collective-permute-start(f32[8,64,1024]{2,1,0:T(8,128)S(1)} %pad_maximum_fusion.1), channel_id=1, source_target_pairs={{0,8},{4,12},{8,0},{12,4},{16,24},{20,28},{24,16},{28,20},{1,9},{5... | collective-permute-start | bytes 6291464 | tf_op jit(solution)/shard_map/ppermute | solution.py:179
  77.9 2.7 copy-start.2
  80.6 91.2 %collective-permute-start.5 = (f32[16,64,1024]{2,1,0:T(8,128)}, f32[16,64,1024]{2,1,0:T(8,128)}, u32[]{:S(2)}, u32[]{:S(2)}) collective-permute-start(f32[16,64,1024]{2,1,0:T(8,128)} %pad_maximum_fusion), channel_id=1, source_target_pairs={{0,16},{4,20},{8,24},{12,28},{16,0},{20,4},{24,8},{28,12},{1,17},{... | collective-permute-start | bytes 12582920 | tf_op jit(solution)/shard_map/ppermute | solution.py:179
  85.5 150.3 %collective-permute-start.23 = (f32[2,1,128,1024]{3,2,1,0:T(8,128)}, f32[2,1,128,1024]{3,2,1,0:T(8,128)}, u32[]{:S(2)}, u32[]{:S(2)}) collective-permute-start(f32[2,1,128,1024]{3,2,1,0:T(8,128)} %get-tuple-element.62), channel_id=1, source_target_pairs={{0,1},{1,2},{2,3},{3,0},{4,5},{5,6},{6,7},{7,4},{8,9},{9,10},{10,1... | collective-permute-start | bytes 3145736 | tf_op jit(solution)/shard_map/ppermute | solution.py:242
  86.7 149.2 %collective-permute-start.22 = (f32[2,1,128,1024]{3,2,1,0:T(8,128)}, f32[2,1,128,1024]{3,2,1,0:T(8,128)S(1)}, u32[]{:S(2)}, u32[]{:S(2)}) collective-permute-start(f32[2,1,128,1024]{3,2,1,0:T(8,128)} %get-tuple-element.61), channel_id=1, source_target_pairs={{0,3},{1,0},{2,1},{3,2},{4,7},{5,4},{6,5},{7,6},{8,11},{9,8},{10,9... | collective-permute-start | bytes 3145736 | tf_op jit(solution)/shard_map/ppermute | solution.py:242
  87.0 151.4 %collective-permute-start.21 = (f32[2,1,128,1024]{3,2,1,0:T(8,128)}, f32[2,1,128,1024]{3,2,1,0:T(8,128)S(1)}, u32[]{:S(2)}, u32[]{:S(2)}) collective-permute-start(f32[2,1,128,1024]{3,2,1,0:T(8,128)} %get-tuple-element.60), channel_id=1, source_target_pairs={{0,2},{1,3},{2,0},{3,1},{4,6},{5,7},{6,4},{7,5},{8,10},{9,11},{10,... | collective-permute-start | bytes 3145736 | tf_op jit(solution)/shard_map/ppermute | solution.py:242
  92.1 196.1 %collective-permute-start.20 = (f32[2,1,128,1024]{3,2,1,0:T(8,128)}, f32[2,1,128,1024]{3,2,1,0:T(8,128)S(1)}, u32[]{:S(2)}, u32[]{:S(2)}) collective-permute-start(f32[2,1,128,1024]{3,2,1,0:T(8,128)} %get-tuple-element.59), channel_id=1, source_target_pairs={{0,1},{1,2},{2,3},{3,0},{4,5},{5,6},{6,7},{7,4},{8,9},{9,10},{10,1... | collective-permute-start | bytes 3145736 | tf_op jit(solution)/shard_map/ppermute | solution.py:242
  171.8 123.3 %collective-permute-start.19 = (f32[2,1,128,1024]{3,2,1,0:T(8,128)}, f32[2,1,128,1024]{3,2,1,0:T(8,128)}, u32[]{:S(2)}, u32[]{:S(2)}) collective-permute-start(f32[2,1,128,1024]{3,2,1,0:T(8,128)} %get-tuple-element.58), channel_id=1, source_target_pairs={{0,3},{1,0},{2,1},{3,2},{4,7},{5,4},{6,5},{7,6},{8,11},{9,8},{10,9... | collective-permute-start | bytes 3145736 | tf_op jit(solution)/shard_map/ppermute | solution.py:242
  235.8 65.9 %collective-permute-start.18 = (f32[2,1,128,1024]{3,2,1,0:T(8,128)}, f32[2,1,128,1024]{3,2,1,0:T(8,128)}, u32[]{:S(2)}, u32[]{:S(2)}) collective-permute-start(f32[2,1,128,1024]{3,2,1,0:T(8,128)} %get-tuple-element.57), channel_id=1, source_target_pairs={{0,2},{1,3},{2,0},{3,1},{4,6},{5,7},{6,4},{7,5},{8,10},{9,11},{10,... | collective-permute-start | bytes 3145736 | tf_op jit(solution)/shard_map/ppermute | solution.py:242
  236.0 91.1 %collective-permute-start.17 = (f32[4,1,128,1024]{3,2,1,0:T(8,128)}, f32[4,1,128,1024]{3,2,1,0:T(8,128)}, u32[]{:S(2)}, u32[]{:S(2)}) collective-permute-start(f32[4,1,128,1024]{3,2,1,0:T(8,128)} %get-tuple-element.56), channel_id=1, source_target_pairs={{0,1},{1,2},{2,3},{3,0},{4,5},{5,6},{6,7},{7,4},{8,9},{9,10},{10,1... | collective-permute-start | bytes 6291464 | tf_op jit(solution)/shard_map/ppermute | solution.py:242
  238.3 485.8 %collective-permute-start.14 = (f32[8,1,128,1024]{3,2,1,0:T(8,128)}, f32[8,1,128,1024]{3,2,1,0:T(8,128)}, u32[]{:S(2)}, u32[]{:S(2)}) collective-permute-start(f32[8,1,128,1024]{3,2,1,0:T(8,128)} %get-tuple-element.53), channel_id=1, source_target_pairs={{0,1},{1,2},{2,3},{3,0},{4,5},{5,6},{6,7},{7,4},{8,9},{9,10},{10,1... | collective-permute-start | bytes 12582920 | tf_op jit(solution)/shard_map/ppermute | solution.py:242
  288.2 151.2 %collective-permute-start.16 = (f32[4,1,128,1024]{3,2,1,0:T(8,128)}, f32[4,1,128,1024]{3,2,1,0:T(8,128)}, u32[]{:S(2)}, u32[]{:S(2)}) collective-permute-start(f32[4,1,128,1024]{3,2,1,0:T(8,128)} %get-tuple-element.55), channel_id=1, source_target_pairs={{0,3},{1,0},{2,1},{3,2},{4,7},{5,4},{6,5},{7,6},{8,11},{9,8},{10,9... | collective-permute-start | bytes 6291464 | tf_op jit(solution)/shard_map/ppermute | solution.py:242
  295.1 453.4 %collective-permute-start.13 = (f32[8,1,128,1024]{3,2,1,0:T(8,128)}, f32[8,1,128,1024]{3,2,1,0:T(8,128)}, u32[]{:S(2)}, u32[]{:S(2)}) collective-permute-start(f32[8,1,128,1024]{3,2,1,0:T(8,128)} %get-tuple-element.52), channel_id=1, source_target_pairs={{0,3},{1,0},{2,1},{3,2},{4,7},{5,4},{6,5},{7,6},{8,11},{9,8},{10,9... | collective-permute-start | bytes 12582920 | tf_op jit(solution)/shard_map/ppermute | solution.py:242
  301.7 409.9 %collective-permute-start.15 = (f32[4,1,128,1024]{3,2,1,0:T(8,128)}, f32[4,1,128,1024]{3,2,1,0:T(8,128)}, u32[]{:S(2)}, u32[]{:S(2)}) collective-permute-start(f32[4,1,128,1024]{3,2,1,0:T(8,128)} %get-tuple-element.54), channel_id=1, source_target_pairs={{0,2},{1,3},{2,0},{3,1},{4,6},{5,7},{6,4},{7,5},{8,10},{9,11},{10,... | collective-permute-start | bytes 6291464 | tf_op jit(solution)/shard_map/ppermute | solution.py:242
  327.0 443.5 %collective-permute-start.12 = (f32[4,1,128,1024]{3,2,1,0:T(8,128)}, f32[4,1,128,1024]{3,2,1,0:T(8,128)}, u32[]{:S(2)}, u32[]{:S(2)}) collective-permute-start(f32[4,1,128,1024]{3,2,1,0:T(8,128)} %constant_dynamic-slice_fusion.7), channel_id=1, source_target_pairs={{0,2},{1,3},{2,0},{3,1},{4,6},{5,7},{6,4},{7,5},{8,10},{9,11},{10,... | collective-permute-start | bytes 6291464 | tf_op jit(solution)/shard_map/ppermute | solution.py:242
  439.4 356.4 %collective-permute-start.11 = (f32[2,1,128,1024]{3,2,1,0:T(8,128)}, f32[2,1,128,1024]{3,2,1,0:T(8,128)}, u32[]{:S(2)}, u32[]{:S(2)}) collective-permute-start(f32[2,1,128,1024]{3,2,1,0:T(8,128)} %constant_dynamic-slice_fusion.6), channel_id=1, source_target_pairs={{0,2},{1,3},{2,0},{3,1},{4,6},{5,7},{6,4},{7,5},{8,10},{9,11},{10,... | collective-permute-start | bytes 3145736 | tf_op jit(solution)/shard_map/ppermute | solution.py:242
  711.6 92.7 %collective-permute-start.10 = (f32[1,1,128,512]{3,2,1,0:T(8,128)}, f32[1,1,128,512]{3,2,1,0:T(8,128)}, u32[]{:S(2)}, u32[]{:S(2)}) collective-permute-start(f32[1,1,128,512]{3,2,1,0:T(8,128)} %get-tuple-element.49), channel_id=1, source_target_pairs={{0,2},{1,3},{2,0},{3,1},{4,6},{5,7},{6,4},{7,5},{8,10},{9,11},{10,... | collective-permute-start | bytes 786440 | tf_op jit(solution)/shard_map/ppermute | solution.py:242
  724.1 88.6 %collective-permute-start.9 = (f32[1,1,128,512]{3,2,1,0:T(8,128)}, f32[1,1,128,512]{3,2,1,0:T(8,128)}, u32[]{:S(2)}, u32[]{:S(2)}) collective-permute-start(f32[1,1,128,512]{3,2,1,0:T(8,128)} %get-tuple-element.48), channel_id=1, source_target_pairs={{0,2},{1,3},{2,0},{3,1},{4,6},{5,7},{6,4},{7,5},{8,10},{9,11},{10,... | collective-permute-start | bytes 786440 | tf_op jit(solution)/shard_map/ppermute | solution.py:242
  748.5 67.0 %collective-permute-start.8 = (f32[1,1,128,256]{3,2,1,0:T(8,128)}, f32[1,1,128,256]{3,2,1,0:T(8,128)}, u32[]{:S(2)}, u32[]{:S(2)}) collective-permute-start(f32[1,1,128,256]{3,2,1,0:T(8,128)} %get-tuple-element.47), channel_id=1, source_target_pairs={{0,2},{1,3},{2,0},{3,1},{4,6},{5,7},{6,4},{7,5},{8,10},{9,11},{10,... | collective-permute-start | bytes 393224 | tf_op jit(solution)/shard_map/ppermute | solution.py:242
  770.5 25.3 %copy-start.4 = (f32[1,1,128,256]{3,2,1,0:T(8,128)S(1)}, f32[1,1,128,256]{3,2,1,0:T(8,128)}, u32[]{:S(2)}) copy-start(f32[1,1,128,256]{3,2,1,0:T(8,128)} %get-tuple-element.45) | copy-start | bytes 393220
  770.5 47.8 %collective-permute-start.7 = (f32[1,1,128,256]{3,2,1,0:T(8,128)}, f32[1,1,128,256]{3,2,1,0:T(8,128)}, u32[]{:S(2)}, u32[]{:S(2)}) collective-permute-start(f32[1,1,128,256]{3,2,1,0:T(8,128)} %get-tuple-element.46), channel_id=1, source_target_pairs={{0,2},{1,3},{2,0},{3,1},{4,6},{5,7},{6,4},{7,5},{8,10},{9,11},{10,... | collective-permute-start | bytes 393224 | tf_op jit(solution)/shard_map/ppermute | solution.py:242
  785.4 18.9 %copy-start.3 = (f32[1,1,128,256]{3,2,1,0:T(8,128)S(1)}, f32[1,1,128,256]{3,2,1,0:T(8,128)}, u32[]{:S(2)}) copy-start(f32[1,1,128,256]{3,2,1,0:T(8,128)} %get-tuple-element.44) | copy-start | bytes 393220
  795.8 25.2 %collective-permute-start.6 = (f32[1,1,128,256]{3,2,1,0:T(8,128)S(1)}, f32[1,1,128,256]{3,2,1,0:T(8,128)S(1)}, u32[]{:S(2)}, u32[]{:S(2)}) collective-permute-start(f32[1,1,128,256]{3,2,1,0:T(8,128)S(1)} %copy-done.4), channel_id=1, source_target_pairs={{0,2},{1,3},{2,0},{3,1},{4,6},{5,7},{6,4},{7,5},{8,10},{9,11},{10,... | collective-permute-start | bytes 393224 | tf_op jit(solution)/shard_map/ppermute | solution.py:242
  804.3 19.6 %collective-permute-start = (f32[1,1,128,256]{3,2,1,0:T(8,128)S(1)}, f32[1,1,128,256]{3,2,1,0:T(8,128)S(1)}, u32[]{:S(2)}, u32[]{:S(2)}) collective-permute-start(f32[1,1,128,256]{3,2,1,0:T(8,128)S(1)} %copy-done.3), channel_id=1, source_target_pairs={{0,2},{1,3},{2,0},{3,1},{4,6},{5,7},{6,4},{7,5},{8,10},{9,11},{10,... | collective-permute-start | bytes 393224 | tf_op jit(solution)/shard_map/ppermute | solution.py:242

commit v7 on v6

--- a/solution.py
+++ b/solution.py
@@ -90,29 +90,38 @@
     )(at, integrals, th, tl, *([ladder] if aliased else []))
 
 
-def part_products(part, v_ref, th_ref, tl_ref, vs_ref):
+def stack_halves(v_ref, vs_ref):
     b_width, depth = v_ref.shape[2:]
     vs_ref[:b_width, :], vs_ref[b_width:, :] = split(v_ref[...].reshape(b_width, depth))
+
+
+def part_products(part, columns, vs_ref, th_ref, tl_ref):
+    b_width, depth = vs_ref.shape[0] // 2, vs_ref.shape[1]
     rows = slice(part * depth, (part + 1) * depth)
     dot = functools.partial(jnp.dot, preferred_element_type=jnp.float32)
-    both = dot(vs_ref[...], th_ref[rows, :])
-    return dot(vs_ref[:b_width, :], tl_ref[rows, :]) + both[b_width:] + both[:b_width]
+    both = dot(vs_ref[...], th_ref[rows, columns])
+    return dot(vs_ref[:b_width, :], tl_ref[rows, columns]) + both[b_width:] + both[:b_width]
 
 
 def sum_kernel(part, v_ref, th_ref, tl_ref, *refs):
     sum_ref, _, vs_ref = refs[-3:]
-    acc = part_products(part, v_ref, th_ref, tl_ref, vs_ref)
+    stack_halves(v_ref, vs_ref)
+    acc = part_products(part, slice(None), vs_ref, th_ref, tl_ref)
     sum_ref[...] = acc if part == 0 else acc + refs[0][...]
 
 
 def last_kernel(part, at_ref, v_ref, th_ref, tl_ref, sum_ref, _, o_ref, vs_ref, part_ref, tile_ref, sems):
     half = v_ref.shape[2] // 2
-    acc = part_products(part, v_ref, th_ref, tl_ref, vs_ref)
+    stack_halves(v_ref, vs_ref)
+    width = SUBLANES * NO
     low_half = lax.broadcasted_iota(jnp.int32, (half, LANES), 1) < NO
     copies = []
     for pair in range(NI * NO // LANES):
+        if pair * LANES % width == 0:
+            acc = part_products(part, slice(pair * LANES, pair * LANES + width), vs_ref, th_ref, tl_ref)
         columns = slice(pair * LANES, (pair + 1) * LANES)
-        part_ref[pair] = acc[:, columns] + sum_ref[:, columns]
+        inner = pair * LANES % width
+        part_ref[pair] = acc[:, inner : inner + LANES] + sum_ref[:, columns]
         even = part_ref[pair, pl.ds(0, half, stride=2), :]
         odd = part_ref[pair, pl.ds(1, half, stride=2), :]
         block, i = divmod(2 * pair, SUBLANES)

time: 830 us -> 830 us (level)
  no operation moved by 1% of the time
where the time goes in v7:
time: 830 us; the launch traced here: 825 us
  waiting for transfers between devices  469 us (57%)
  Pallas kernels  196 us (24%)
  local copies, waits for them, and re-layouts  85.3 us (10%)
  starting transfers between devices  55.9 us (7%)
  other arithmetic  19.4 us (2%)
    ppermute x19, waiting for transfers between devices, body(): lax.ppermute(piece, 'col', [(k, (k + shift) % cols) for k in range(cols)])  353 us
    pallas_call x14, Pallas kernels, multiply(): pl.pallas_call(functools.partial(ladder_kernel, group, width), out_shape=...  186 us
    ppermute x5, waiting for transfers between devices, gather_over(): got = lax.ppermute(block, axis, [(k, k ^ mask) for k in range(size)])  116 us
    ppermute x19, starting transfers between devices, body(): lax.ppermute(piece, 'col', [(k, (k + shift) % cols) for k in range(cols)])  47.2 us
    dynamic_slice x8, local copies, waits for them, and re-layouts, body(): lax.dynamic_slice(source, (start, (here + shift) % cols, 0, part * width)...  30.8 us
  transfers between devices with their start and end apart: 24, of which 14 were waited for; matrix products, arithmetic and copies ran while one was open for 12% of the time, Pallas kernels for 24%

profile of v7, /device:TPU:25, one launch (start us, length us, event | category | flops | bytes accessed | tf_op | source)
XLA Modules:
  0.0 825.5 jit_solution(9551483727224479085)
XLA Ops:
  0.0 9.3 %collective-permute-done.1 = f32[1,64,1024]{2,1,0:T(8,128)S(1)} collective-permute-done((f32[1,64,1024]{2,1,0:T(8,128)}, f32[1,64,1024]{2,1,0:T(8,128)S(1)}, u32[]{:S(2)}, u32[]{:S(2)}) %collective-permute-start.1) | collective-permute-done | bytes 262176 | tf_op jit(solution)/shard_map/ppermute | solution.py:188
  10.3 4.0 collective-permute-start.2
  14.2 10.8 %collective-permute-done.2 = f32[2,64,1024]{2,1,0:T(8,128)S(1)} collective-permute-done((f32[2,64,1024]{2,1,0:T(8,128)S(1)}, f32[2,64,1024]{2,1,0:T(8,128)S(1)}, u32[]{:S(2)}, u32[]{:S(2)}) %collective-permute-start.2) | collective-permute-done | bytes 524320 | tf_op jit(solution)/shard_map/ppermute | solution.py:188
  26.4 2.2 collective-permute-start.3
  28.6 2.3 collective-permute-done.3
  32.3 45.6 %collective-permute-done.4 = f32[8,64,1024]{2,1,0:T(8,128)S(1)} collective-permute-done((f32[8,64,1024]{2,1,0:T(8,128)S(1)}, f32[8,64,1024]{2,1,0:T(8,128)S(1)}, u32[]{:S(2)}, u32[]{:S(2)}) %collective-permute-start.4) | collective-permute-done | bytes 2097184 | tf_op jit(solution)/shard_map/ppermute | solution.py:188
  77.9 2.6 pad_maximum_fusion
  81.8 3.7 constant_dynamic-slice_fusion.16
  88.5 3.6 constant_dynamic-slice_fusion.13
  92.1 2.0 collective-permute-start.20
  94.1 5.8 constant_dynamic-slice_fusion.10
  99.9 3.2 constant_dynamic-slice_fusion.7
  103.1 8.4 %constant_dynamic-slice_fusion.8 = (f32[8,1,128,1024]{3,2,1,0:T(8,128)}, f32[8,1,128,1024]{3,2,1,0:T(8,128)}) fusion(f32[16,4,128,1024]{3,2,1,0:T(8,128)} %bitcast.73, s32[]{:T(128)S(6)} %select_n.152, s32[]{:T(128)S(6)} %select_n.150), kind=kLoop, calls=%fused_computation.37 | loop fusion | bytes 16777224 | tf_op jit(solution)/shard_map/dynamic_slice | solution.py:242
  111.5 2.3 constant_dynamic-slice_fusion.6
  123.9 47.9 %collective-permute-done.5 = f32[16,64,1024]{2,1,0:T(8,128)} collective-permute-done((f32[16,64,1024]{2,1,0:T(8,128)}, f32[16,64,1024]{2,1,0:T(8,128)}, u32[]{:S(2)}, u32[]{:S(2)}) %collective-permute-start.5) | collective-permute-done | bytes 4194336 | tf_op jit(solution)/shard_map/ppermute | solution.py:188
  178.5 1.9 reverse_select_fusion.2
  182.3 4.3 reverse_select_fusion
  186.6 13.3 %reshape_reshape_reshape.3 = f32[32,2,32,16,64]{4,3,2,1,0:T(8,128)} reshape(f32[1,2,4,4,64,1024]{5,4,3,2,1,0:T(8,128)} %reverse_select_fusion) | data formatting | bytes 16777216 | tf_op jit(solution)/shard_map/reshape;reshape;reshape | solution.py:208
  199.9 15.8 %copy.22 = f32[2,32,16,32,64]{4,3,2,1,0:T(8,128)} copy(f32[2,32,16,32,64]{4,2,3,0,1:T(8,128)} %bitcast.78) | data formatting | bytes 16777216 | tf_op jit(solution)/shard_map/transpose | solution.py:208
  215.8 14.8 %reshape.28 = f32[1024,2048]{1,0:T(8,128)} reshape(f32[2,32,16,32,64]{4,3,2,1,0:T(8,128)} %copy.22) | data formatting | bytes 16777216 | tf_op jit(solution)/shard_map/reshape | solution.py:209
  230.6 5.2 fusion
  236.0 2.4 collective-permute-start.17
  239.4 41.0 %shard_map.28.refs_0_ = f32[64,2048,128]{2,1,0:T(8,128)} custom-call(s32[2]{0:T(128)S(1)} %pad_add_fusion.13.at_ref, f32[16,4,128,1024]{3,2,1,0:T(8,128)} %bitcast.77, bf16[1024,2048]{1,0:T(8,128)(2,1)S(1)} %get-tuple-element.89.th_ref, bf16[1024,2048]{1,0:T(8,128)(2,1)S(1)} %get-tuple-element.88.tl_ref), custom_call_target="tpu_custom_call" | custom-call | flops 25769803776 | bytes 58720256 | tf_op jit(solution)/shard_map/pallas_call | solution.py:67
  280.4 7.8 shard_map.29.refs_0_
  288.6 6.6 shard_map.30.refs_0_
  295.1 6.6 shard_map.31.refs_0_
  301.7 3.2 collective-permute-start.15
  304.9 6.6 shard_map.32.refs_0_
  311.4 7.8 shard_map.33.refs_0_
  319.2 7.8 shard_map.34.refs_0_
  328.8 12.5 %shard_map.35.refs_0_ = f32[64,2048,128]{2,1,0:T(8,128)} custom-call(s32[2]{0:T(128)S(1)} %pad_add_fusion.6.at_ref, f32[4,1,128,1024]{3,2,1,0:T(8,128)} %collective-permute-done.17.v_ref, bf16[1024,2048]{1,0:T(8,128)(2,1)S(1)} %get-tuple-element.89.th_ref, bf16[1024,2048]{1,0:T(8,128)(2,1)S(1)} %get-tuple-element.88.tl_ref, ...), custom_call_target="tpu_custom_call", output_to_operand_aliasing={{}: (4, {})} | custom-call | flops 6442450944 | bytes 14680064 | tf_op jit(solution)/shard_map/pallas_call | solution.py:67
  341.4 98.1 %collective-permute-done.16.v_ref = f32[4,1,128,1024]{3,2,1,0:T(8,128)} collective-permute-done((f32[4,1,128,1024]{3,2,1,0:T(8,128)}, f32[4,1,128,1024]{3,2,1,0:T(8,128)}, u32[]{:S(2)}, u32[]{:S(2)}) %collective-permute-start.16) | collective-permute-done | bytes 2097184 | tf_op jit(solution)/shard_map/ppermute | solution.py:251
  439.4 25.1 %collective-permute-start.11 = (f32[2,1,128,1024]{3,2,1,0:T(8,128)}, f32[2,1,128,1024]{3,2,1,0:T(8,128)}, u32[]{:S(2)}, u32[]{:S(2)}) collective-permute-start(f32[2,1,128,1024]{3,2,1,0:T(8,128)} %constant_dynamic-slice_fusion.6), channel_id=1, source_target_pairs={{0,2},{1,3},{2,0},{3,1},{4,6},{5,7},{6,4},{7,5},{8,10},{9,11},{10,... | collective-permute-start | bytes 3145736 | tf_op jit(solution)/shard_map/ppermute | solution.py:251
  464.5 12.5 %shard_map.36.refs_0_ = f32[64,2048,128]{2,1,0:T(8,128)} custom-call(s32[2]{0:T(128)S(1)} %pad_add_fusion.7.at_ref, f32[4,1,128,1024]{3,2,1,0:T(8,128)} %collective-permute-done.16.v_ref, bf16[1024,2048]{1,0:T(8,128)(2,1)S(1)} %get-tuple-element.89.th_ref, bf16[1024,2048]{1,0:T(8,128)(2,1)S(1)} %get-tuple-element.88.tl_ref, ...), custom_call_target="tpu_custom_call", output_to_operand_aliasing={{}: (4, {})} | custom-call | flops 6442450944 | bytes 14680064 | tf_op jit(solution)/shard_map/pallas_call | solution.py:67
  477.1 234.5 %collective-permute-done.15.v_ref = f32[4,1,128,1024]{3,2,1,0:T(8,128)} collective-permute-done((f32[4,1,128,1024]{3,2,1,0:T(8,128)}, f32[4,1,128,1024]{3,2,1,0:T(8,128)}, u32[]{:S(2)}, u32[]{:S(2)}) %collective-permute-start.15) | collective-permute-done | bytes 2097184 | tf_op jit(solution)/shard_map/ppermute | solution.py:251
  711.6 12.5 %shard_map.37.refs_0_ = f32[64,2048,128]{2,1,0:T(8,128)} custom-call(s32[2]{0:T(128)S(1)} %pad_add_fusion.8.at_ref, f32[4,1,128,1024]{3,2,1,0:T(8,128)} %collective-permute-done.15.v_ref, bf16[1024,2048]{1,0:T(8,128)(2,1)S(1)} %get-tuple-element.89.th_ref, bf16[1024,2048]{1,0:T(8,128)(2,1)S(1)} %get-tuple-element.88.tl_ref, ...), custom_call_target="tpu_custom_call", output_to_operand_aliasing={{}: (4, {})} | custom-call | flops 6442450944 | bytes 14680064 | tf_op jit(solution)/shard_map/pallas_call | solution.py:67
  724.1 2.4 collective-permute-start.9
  726.5 22.0 %shard_map.38.refs_0_ = f32[64,2048,128]{2,1,0:T(8,128)} custom-call(s32[2]{0:T(128)S(1)} %pad_add_fusion.9.at_ref, f32[8,1,128,1024]{3,2,1,0:T(8,128)} %collective-permute-done.14.v_ref, bf16[1024,2048]{1,0:T(8,128)(2,1)S(1)} %get-tuple-element.89.th_ref, bf16[1024,2048]{1,0:T(8,128)(2,1)S(1)} %get-tuple-element.88.tl_ref, ...), custom_call_target="tpu_custom_call", output_to_operand_aliasing={{}: (4, {})} | custom-call | flops 12884901888 | bytes 20971520 | tf_op jit(solution)/shard_map/pallas_call | solution.py:67
  748.5 22.0 %shard_map.39.refs_0_ = f32[64,2048,128]{2,1,0:T(8,128)} custom-call(s32[2]{0:T(128)S(1)} %pad_add_fusion.10.at_ref, f32[8,1,128,1024]{3,2,1,0:T(8,128)} %collective-permute-done.13.v_ref, bf16[1024,2048]{1,0:T(8,128)(2,1)S(1)} %get-tuple-element.89.th_ref, bf16[1024,2048]{1,0:T(8,128)(2,1)S(1)} %get-tuple-element.88.tl_ref, ...), custom_call_target="tpu_custom_call", output_to_operand_aliasing={{}: (4, {})} | custom-call | flops 12884901888 | bytes 20971520 | tf_op jit(solution)/shard_map/pallas_call | solution.py:67
  770.5 2.3 collective-permute-start.7
  772.8 12.5 %shard_map.40.refs_0_ = f32[64,2048,128]{2,1,0:T(8,128)} custom-call(s32[2]{0:T(128)S(1)} %pad_add_fusion.11.at_ref, f32[4,1,128,1024]{3,2,1,0:T(8,128)} %collective-permute-done.12.v_ref, bf16[1024,2048]{1,0:T(8,128)(2,1)S(1)} %get-tuple-element.89.th_ref, bf16[1024,2048]{1,0:T(8,128)(2,1)S(1)} %get-tuple-element.88.tl_ref, ...), custom_call_target="tpu_custom_call", output_to_operand_aliasing={{}: (4, {})} | custom-call | flops 6442450944 | bytes 14680064 | tf_op jit(solution)/shard_map/pallas_call | solution.py:67
  785.4 10.4 %collective-permute-done.11.v_ref = f32[2,1,128,1024]{3,2,1,0:T(8,128)} collective-permute-done((f32[2,1,128,1024]{3,2,1,0:T(8,128)}, f32[2,1,128,1024]{3,2,1,0:T(8,128)}, u32[]{:S(2)}, u32[]{:S(2)}) %collective-permute-start.11) | collective-permute-done | bytes 1048608 | tf_op jit(solution)/shard_map/ppermute | solution.py:251
  795.8 8.1 shard_map.41.refs_0_
  804.3 2.0 collective-permute-start
  806.2 1.9 shard_map.42
  808.2 4.5 collective-permute-done.9.v_ref
  812.7 2.8 shard_map.43.refs_0_
  821.6 2.2 collective-permute-done.v_ref
  (74 shorter events, 38.0 us)
Async XLA Ops:
  0.0 9.3 %collective-permute-start.1 = (f32[1,64,1024]{2,1,0:T(8,128)}, f32[1,64,1024]{2,1,0:T(8,128)S(1)}, u32[]{:S(2)}, u32[]{:S(2)}) collective-permute-start(f32[1,64,1024]{2,1,0:T(8,128)} %bitcast.87), channel_id=1, source_target_pairs={{0,3},{1,2},{2,1},{3,0},{4,7},{5,6},{6,5},{7,4},{8,11},{9,10},{10,... | collective-permute-start | bytes 786440 | tf_op jit(solution)/shard_map/ppermute | solution.py:188
  10.3 14.7 %collective-permute-start.2 = (f32[2,64,1024]{2,1,0:T(8,128)S(1)}, f32[2,64,1024]{2,1,0:T(8,128)S(1)}, u32[]{:S(2)}, u32[]{:S(2)}) collective-permute-start(f32[2,64,1024]{2,1,0:T(8,128)S(1)} %pad_maximum_fusion.3), channel_id=1, source_target_pairs={{0,1},{1,0},{2,3},{3,2},{4,5},{5,4},{6,7},{7,6},{8,9},{9,8},{10,11... | collective-permute-start | bytes 1572872 | tf_op jit(solution)/shard_map/ppermute | solution.py:188
  26.4 59.1 %copy-start = (f32[1,2,2,1,64,1024]{5,4,2,1,3,0:T(8,128)}, f32[1,2,2,1,64,1024]{5,4,2,1,3,0:T(8,128)S(1)}, u32[]{:S(2)}) copy-start(f32[1,2,2,1,64,1024]{5,4,2,1,3,0:T(8,128)S(1)} %reverse_select_fusion.3) | copy-start | bytes 3145732
  26.4 4.5 collective-permute-start.3
  30.8 47.0 %copy-start.1 = (f32[4,64,1024]{2,1,0:T(8,128)}, f32[4,64,1024]{2,1,0:T(8,128)S(1)}, u32[]{:S(2)}) copy-start(f32[4,64,1024]{2,1,0:T(8,128)S(1)} %collective-permute-done.3) | copy-start | bytes 3145732
  31.0 46.9 %collective-permute-start.4 = (f32[8,64,1024]{2,1,0:T(8,128)S(1)}, f32[8,64,1024]{2,1,0:T(8,128)S(1)}, u32[]{:S(2)}, u32[]{:S(2)}) collective-permute-start(f32[8,64,1024]{2,1,0:T(8,128)S(1)} %pad_maximum_fusion.1), channel_id=1, source_target_pairs={{0,8},{4,12},{8,0},{12,4},{16,24},{20,28},{24,16},{28,20},{1,9},{5... | collective-permute-start | bytes 6291464 | tf_op jit(solution)/shard_map/ppermute | solution.py:188
  77.9 2.7 copy-start.2
  80.6 91.2 %collective-permute-start.5 = (f32[16,64,1024]{2,1,0:T(8,128)}, f32[16,64,1024]{2,1,0:T(8,128)}, u32[]{:S(2)}, u32[]{:S(2)}) collective-permute-start(f32[16,64,1024]{2,1,0:T(8,128)} %pad_maximum_fusion), channel_id=1, source_target_pairs={{0,16},{4,20},{8,24},{12,28},{16,0},{20,4},{24,8},{28,12},{1,17},{... | collective-permute-start | bytes 12582920 | tf_op jit(solution)/shard_map/ppermute | solution.py:188
  85.5 150.3 %collective-permute-start.23 = (f32[2,1,128,1024]{3,2,1,0:T(8,128)}, f32[2,1,128,1024]{3,2,1,0:T(8,128)}, u32[]{:S(2)}, u32[]{:S(2)}) collective-permute-start(f32[2,1,128,1024]{3,2,1,0:T(8,128)} %get-tuple-element.62), channel_id=1, source_target_pairs={{0,1},{1,2},{2,3},{3,0},{4,5},{5,6},{6,7},{7,4},{8,9},{9,10},{10,1... | collective-permute-start | bytes 3145736 | tf_op jit(solution)/shard_map/ppermute | solution.py:251
  86.7 149.2 %collective-permute-start.22 = (f32[2,1,128,1024]{3,2,1,0:T(8,128)}, f32[2,1,128,1024]{3,2,1,0:T(8,128)S(1)}, u32[]{:S(2)}, u32[]{:S(2)}) collective-permute-start(f32[2,1,128,1024]{3,2,1,0:T(8,128)} %get-tuple-element.61), channel_id=1, source_target_pairs={{0,3},{1,0},{2,1},{3,2},{4,7},{5,4},{6,5},{7,6},{8,11},{9,8},{10,9... | collective-permute-start | bytes 3145736 | tf_op jit(solution)/shard_map/ppermute | solution.py:251
  87.0 151.4 %collective-permute-start.21 = (f32[2,1,128,1024]{3,2,1,0:T(8,128)}, f32[2,1,128,1024]{3,2,1,0:T(8,128)S(1)}, u32[]{:S(2)}, u32[]{:S(2)}) collective-permute-start(f32[2,1,128,1024]{3,2,1,0:T(8,128)} %get-tuple-element.60), channel_id=1, source_target_pairs={{0,2},{1,3},{2,0},{3,1},{4,6},{5,7},{6,4},{7,5},{8,10},{9,11},{10,... | collective-permute-start | bytes 3145736 | tf_op jit(solution)/shard_map/ppermute | solution.py:251
  92.1 196.1 %collective-permute-start.20 = (f32[2,1,128,1024]{3,2,1,0:T(8,128)}, f32[2,1,128,1024]{3,2,1,0:T(8,128)S(1)}, u32[]{:S(2)}, u32[]{:S(2)}) collective-permute-start(f32[2,1,128,1024]{3,2,1,0:T(8,128)} %get-tuple-element.59), channel_id=1, source_target_pairs={{0,1},{1,2},{2,3},{3,0},{4,5},{5,6},{6,7},{7,4},{8,9},{9,10},{10,1... | collective-permute-start | bytes 3145736 | tf_op jit(solution)/shard_map/ppermute | solution.py:251
  171.8 123.3 %collective-permute-start.19 = (f32[2,1,128,1024]{3,2,1,0:T(8,128)}, f32[2,1,128,1024]{3,2,1,0:T(8,128)}, u32[]{:S(2)}, u32[]{:S(2)}) collective-permute-start(f32[2,1,128,1024]{3,2,1,0:T(8,128)} %get-tuple-element.58), channel_id=1, source_target_pairs={{0,3},{1,0},{2,1},{3,2},{4,7},{5,4},{6,5},{7,6},{8,11},{9,8},{10,9... | collective-permute-start | bytes 3145736 | tf_op jit(solution)/shard_map/ppermute | solution.py:251
  235.8 65.9 %collective-permute-start.18 = (f32[2,1,128,1024]{3,2,1,0:T(8,128)}, f32[2,1,128,1024]{3,2,1,0:T(8,128)}, u32[]{:S(2)}, u32[]{:S(2)}) collective-permute-start(f32[2,1,128,1024]{3,2,1,0:T(8,128)} %get-tuple-element.57), channel_id=1, source_target_pairs={{0,2},{1,3},{2,0},{3,1},{4,6},{5,7},{6,4},{7,5},{8,10},{9,11},{10,... | collective-permute-start | bytes 3145736 | tf_op jit(solution)/shard_map/ppermute | solution.py:251
  236.0 91.1 %collective-permute-start.17 = (f32[4,1,128,1024]{3,2,1,0:T(8,128)}, f32[4,1,128,1024]{3,2,1,0:T(8,128)}, u32[]{:S(2)}, u32[]{:S(2)}) collective-permute-start(f32[4,1,128,1024]{3,2,1,0:T(8,128)} %get-tuple-element.56), channel_id=1, source_target_pairs={{0,1},{1,2},{2,3},{3,0},{4,5},{5,6},{6,7},{7,4},{8,9},{9,10},{10,1... | collective-permute-start | bytes 6291464 | tf_op jit(solution)/shard_map/ppermute | solution.py:251
  238.3 485.8 %collective-permute-start.14 = (f32[8,1,128,1024]{3,2,1,0:T(8,128)}, f32[8,1,128,1024]{3,2,1,0:T(8,128)}, u32[]{:S(2)}, u32[]{:S(2)}) collective-permute-start(f32[8,1,128,1024]{3,2,1,0:T(8,128)} %get-tuple-element.53), channel_id=1, source_target_pairs={{0,1},{1,2},{2,3},{3,0},{4,5},{5,6},{6,7},{7,4},{8,9},{9,10},{10,1... | collective-permute-start | bytes 12582920 | tf_op jit(solution)/shard_map/ppermute | solution.py:251
  288.2 151.2 %collective-permute-start.16 = (f32[4,1,128,1024]{3,2,1,0:T(8,128)}, f32[4,1,128,1024]{3,2,1,0:T(8,128)}, u32[]{:S(2)}, u32[]{:S(2)}) collective-permute-start(f32[4,1,128,1024]{3,2,1,0:T(8,128)} %get-tuple-element.55), channel_id=1, source_target_pairs={{0,3},{1,0},{2,1},{3,2},{4,7},{5,4},{6,5},{7,6},{8,11},{9,8},{10,9... | collective-permute-start | bytes 6291464 | tf_op jit(solution)/shard_map/ppermute | solution.py:251
  295.1 453.4 %collective-permute-start.13 = (f32[8,1,128,1024]{3,2,1,0:T(8,128)}, f32[8,1,128,1024]{3,2,1,0:T(8,128)}, u32[]{:S(2)}, u32[]{:S(2)}) collective-permute-start(f32[8,1,128,1024]{3,2,1,0:T(8,128)} %get-tuple-element.52), channel_id=1, source_target_pairs={{0,3},{1,0},{2,1},{3,2},{4,7},{5,4},{6,5},{7,6},{8,11},{9,8},{10,9... | collective-permute-start | bytes 12582920 | tf_op jit(solution)/shard_map/ppermute | solution.py:251
  301.7 409.9 %collective-permute-start.15 = (f32[4,1,128,1024]{3,2,1,0:T(8,128)}, f32[4,1,128,1024]{3,2,1,0:T(8,128)}, u32[]{:S(2)}, u32[]{:S(2)}) collective-permute-start(f32[4,1,128,1024]{3,2,1,0:T(8,128)} %get-tuple-element.54), channel_id=1, source_target_pairs={{0,2},{1,3},{2,0},{3,1},{4,6},{5,7},{6,4},{7,5},{8,10},{9,11},{10,... | collective-permute-start | bytes 6291464 | tf_op jit(solution)/shard_map/ppermute | solution.py:251
  327.0 443.5 %collective-permute-start.12 = (f32[4,1,128,1024]{3,2,1,0:T(8,128)}, f32[4,1,128,1024]{3,2,1,0:T(8,128)}, u32[]{:S(2)}, u32[]{:S(2)}) collective-permute-start(f32[4,1,128,1024]{3,2,1,0:T(8,128)} %constant_dynamic-slice_fusion.7), channel_id=1, source_target_pairs={{0,2},{1,3},{2,0},{3,1},{4,6},{5,7},{6,4},{7,5},{8,10},{9,11},{10,... | collective-permute-start | bytes 6291464 | tf_op jit(solution)/shard_map/ppermute | solution.py:251
  439.4 356.4 %collective-permute-start.11 = (f32[2,1,128,1024]{3,2,1,0:T(8,128)}, f32[2,1,128,1024]{3,2,1,0:T(8,128)}, u32[]{:S(2)}, u32[]{:S(2)}) collective-permute-start(f32[2,1,128,1024]{3,2,1,0:T(8,128)} %constant_dynamic-slice_fusion.6), channel_id=1, source_target_pairs={{0,2},{1,3},{2,0},{3,1},{4,6},{5,7},{6,4},{7,5},{8,10},{9,11},{10,... | collective-permute-start | bytes 3145736 | tf_op jit(solution)/shard_map/ppermute | solution.py:251
  711.6 92.7 %collective-permute-start.10 = (f32[1,1,128,512]{3,2,1,0:T(8,128)}, f32[1,1,128,512]{3,2,1,0:T(8,128)}, u32[]{:S(2)}, u32[]{:S(2)}) collective-permute-start(f32[1,1,128,512]{3,2,1,0:T(8,128)} %get-tuple-element.49), channel_id=1, source_target_pairs={{0,2},{1,3},{2,0},{3,1},{4,6},{5,7},{6,4},{7,5},{8,10},{9,11},{10,... | collective-permute-start | bytes 786440 | tf_op jit(solution)/shard_map/ppermute | solution.py:251
  724.1 88.6 %collective-permute-start.9 = (f32[1,1,128,512]{3,2,1,0:T(8,128)}, f32[1,1,128,512]{3,2,1,0:T(8,128)}, u32[]{:S(2)}, u32[]{:S(2)}) collective-permute-start(f32[1,1,128,512]{3,2,1,0:T(8,128)} %get-tuple-element.48), channel_id=1, source_target_pairs={{0,2},{1,3},{2,0},{3,1},{4,6},{5,7},{6,4},{7,5},{8,10},{9,11},{10,... | collective-permute-start | bytes 786440 | tf_op jit(solution)/shard_map/ppermute | solution.py:251
  748.5 67.0 %collective-permute-start.8 = (f32[1,1,128,256]{3,2,1,0:T(8,128)}, f32[1,1,128,256]{3,2,1,0:T(8,128)}, u32[]{:S(2)}, u32[]{:S(2)}) collective-permute-start(f32[1,1,128,256]{3,2,1,0:T(8,128)} %get-tuple-element.47), channel_id=1, source_target_pairs={{0,2},{1,3},{2,0},{3,1},{4,6},{5,7},{6,4},{7,5},{8,10},{9,11},{10,... | collective-permute-start | bytes 393224 | tf_op jit(solution)/shard_map/ppermute | solution.py:251
  770.5 25.3 %copy-start.4 = (f32[1,1,128,256]{3,2,1,0:T(8,128)S(1)}, f32[1,1,128,256]{3,2,1,0:T(8,128)}, u32[]{:S(2)}) copy-start(f32[1,1,128,256]{3,2,1,0:T(8,128)} %get-tuple-element.45) | copy-start | bytes 393220
  770.5 47.8 %collective-permute-start.7 = (f32[1,1,128,256]{3,2,1,0:T(8,128)}, f32[1,1,128,256]{3,2,1,0:T(8,128)}, u32[]{:S(2)}, u32[]{:S(2)}) collective-permute-start(f32[1,1,128,256]{3,2,1,0:T(8,128)} %get-tuple-element.46), channel_id=1, source_target_pairs={{0,2},{1,3},{2,0},{3,1},{4,6},{5,7},{6,4},{7,5},{8,10},{9,11},{10,... | collective-permute-start | bytes 393224 | tf_op jit(solution)/shard_map/ppermute | solution.py:251
  785.4 18.9 %copy-start.3 = (f32[1,1,128,256]{3,2,1,0:T(8,128)S(1)}, f32[1,1,128,256]{3,2,1,0:T(8,128)}, u32[]{:S(2)}) copy-start(f32[1,1,128,256]{3,2,1,0:T(8,128)} %get-tuple-element.44) | copy-start | bytes 393220
  795.8 25.2 %collective-permute-start.6 = (f32[1,1,128,256]{3,2,1,0:T(8,128)S(1)}, f32[1,1,128,256]{3,2,1,0:T(8,128)S(1)}, u32[]{:S(2)}, u32[]{:S(2)}) collective-permute-start(f32[1,1,128,256]{3,2,1,0:T(8,128)S(1)} %copy-done.4), channel_id=1, source_target_pairs={{0,2},{1,3},{2,0},{3,1},{4,6},{5,7},{6,4},{7,5},{8,10},{9,11},{10,... | collective-permute-start | bytes 393224 | tf_op jit(solution)/shard_map/ppermute | solution.py:251
  804.3 19.6 %collective-permute-start = (f32[1,1,128,256]{3,2,1,0:T(8,128)S(1)}, f32[1,1,128,256]{3,2,1,0:T(8,128)S(1)}, u32[]{:S(2)}, u32[]{:S(2)}) collective-permute-start(f32[1,1,128,256]{3,2,1,0:T(8,128)S(1)} %copy-done.3), channel_id=1, source_target_pairs={{0,2},{1,3},{2,0},{3,1},{4,6},{5,7},{6,4},{7,5},{8,10},{9,11},{10,... | collective-permute-start | bytes 393224 | tf_op jit(solution)/shard_map/ppermute | solution.py:251
